TPU v7x, 32 devices: a whole 2x2x4 slice. The times are simulated.
32 devices in a mesh: seq: 8 (over z, y), rep: 4 (over x, core).
Axes of the slice: x: 2, y: 2, z: 4, core: 2. Of those that a mesh axis runs over, the one named last changes fastest.
Arguments:
- queries: bfloat16 [4, 2048, 512], P('rep', 'seq'), may hold values from -6 to 6
- key_vectors: bfloat16 [4, 2048, 128], P('rep', 'seq'), may hold values from -6 to 6
- values: bfloat16 [4, 2048, 128], P('rep', 'seq'), may hold values from -6 to 6
- forget_logit: bfloat16 [4, 4, 2048], P('rep', None, 'seq'), may hold values from 0 to 11
- out_grad: bfloat16 [4, 2048, 512], P('rep', 'seq'), may hold values from -6 to 6
- query_gain: float32 [128], replicated, may hold values from 0.1 to 1.9
- key_gain: float32 [128], replicated, may hold values from 0.1 to 1.9
- lengths: int32 [4, 4], P('rep'), may hold values from 1 to 24, 32 in all within a row
Outputs:
- attention: bfloat16 [4, 2048, 512], P('rep', 'seq')
- query_grad: bfloat16 [4, 2048, 512], P('rep', 'seq')
- key_grad: bfloat16 [4, 2048, 128], P('rep', 'seq')
- value_grad: bfloat16 [4, 2048, 128], P('rep', 'seq')
- forget_grad: float32 [4, 4, 2048], P('rep', None, 'seq')
- norm_gain_grad: float32 [2, 128], replicated
Inputs may be any that keep to these rules, and one draw needn't show every extreme that they name: `lengths`: each row lists the documents of one pack in order, in tiles of 64 tokens, and sums to 32.
All inputs are finite; a program needn't handle non-finite values.
Results may differ from a plain program's by a relative error of at most 0.02.
Values may be sent and summed in bfloat16 or wider, within the bound.
No kernel may reach another device: no remote copies, remote signals or barrier semaphores. Data moves between devices by JAX's collectives and lax.ppermute only.
A program may use at most 64 MiB of HBM per device.

v0:
```python
import functools

import jax
import jax.numpy as jnp
from jax import lax
from jax.experimental import pallas as pl
from jax.experimental.pallas import tpu as pltpu
from jax.sharding import PartitionSpec as P


TILE = 64
EPS = 1e-06
TAIL = 32
ONES = 16
CHUNK = 512
BIG = 1e30
F32 = jnp.float32
BF16 = jnp.bfloat16
VMEM = pl.BlockSpec(memory_space=pltpu.VMEM)
HBM = pl.BlockSpec(memory_space=pltpu.HBM)


def swap(value, axis, bit):
    count = lax.axis_size(axis)
    return lax.ppermute(value, axis, [(i, i ^ bit) for i in range(count)])


def struct(*shape, dtype=BF16):
    return jax.ShapeDtypeStruct(shape, dtype)


def kernel_call(kernel, operands, outs, scratch=(), limit=8 << 20, flops=1 << 20, far=0):
    in_specs = [HBM] * far + [VMEM] * (len(operands) - far)
    operands = [
        pltpu.with_memory_space_constraint(x, pltpu.HBM) if i < far else x
        for i, x in enumerate(operands)
    ]
    return pl.pallas_call(
        kernel,
        out_shape=outs,
        in_specs=in_specs,
        out_specs=jax.tree.map(lambda _: VMEM, outs),
        scratch_shapes=list(scratch),
        compiler_params=pltpu.CompilerParams(vmem_limit_bytes=limit),
        cost_estimate=pl.CostEstimate(flops=flops, bytes_accessed=1 << 20, transcendentals=0),
    )(*operands)


def dot_nn(a, b):
    return lax.dot_general(a, b, (((1,), (0,)), ((), ())), preferred_element_type=F32)


def dot_nt(a, b):
    return lax.dot_general(a, b, (((1,), (1,)), ((), ())), preferred_element_type=F32)


def iota(shape, axis):
    return lax.broadcasted_iota(jnp.int32, shape, axis)


def split3(x):
    hi = x.astype(BF16).astype(F32)
    rest = x - hi
    mid = rest.astype(BF16).astype(F32)
    return hi, mid, rest - mid


def rms(x):
    return lax.rsqrt(jnp.mean(x * x, axis=-1, keepdims=True) + EPS)


def flip(block):
    return block.astype(F32).T.astype(BF16)


def ones_where(count, test):
    shape = (count, count)
    return jnp.where(test(iota(shape, 0), iota(shape, 1)), 1.0, 0.0).astype(BF16)


def ones_rows(count):
    return jnp.where(iota((ONES, count), 0) == 0, 1.0, 0.0).astype(BF16)


def cols(h, rows):
    return slice(h * rows, (h + 1) * rows)


def chunks(wide):
    step = min(wide, CHUNK)
    return [slice(at, at + step) for at in range(0, wide, step)]


def lay_out(per_head):
    return jnp.concatenate([per_head[h : h + 1] for h in range(per_head.shape[0])], axis=1)


def log_sigmoid(x):
    small = jnp.exp(-jnp.abs(x))
    series = small * (1.0 - small * (0.5 - small * (1.0 / 3.0 - small * 0.25)))
    return jnp.minimum(x, 0.0) - jnp.where(small < 0.01, series, jnp.log(1.0 + small))


def bounds(len_ref, rows):
    me = lax.axis_index("seq")
    tiles = rows // TILE
    spans = []
    start = jnp.int32(0)
    begin = jnp.int32(0)
    for d in range(len_ref.shape[1]):
        end = start + len_ref[0, d]
        spans.append((start, end))
        begin = jnp.where(start <= me * tiles, start, begin)
        start = end
    return me, begin // tiles, spans


def first_block(low_ref):
    return lax.axis_index("seq"), low_ref[0, 0]


def is_active(me, low, k):
    b = me ^ k
    return (b <= me) & (b >= low)


def fetch(sources, targets, sem):
    copies = [pltpu.make_async_copy(*pair, sem.at[i]) for i, pair in enumerate(zip(sources, targets))]
    for copy in copies:
        copy.start()
    for copy in copies:
        copy.wait()


def near(operands):
    spaces = [pltpu.SMEM if x.dtype == jnp.int32 else pltpu.VMEM for x in operands]
    return [space(x.shape, x.dtype) for space, x in zip(spaces, operands)] + [
        pltpu.SemaphoreType.DMA((len(operands),))
    ]


def pack_kernel(*refs):
    own_ref, tail_ref, low_ref = refs[5:8]
    fetch(refs[:5], refs[8:13], refs[13])
    len_ref, k_ref, v_ref, logit_ref, gain_ref = refs[8:13]
    rows, dim = k_ref.shape
    heads = logit_ref.shape[0]
    me, low, spans = bounds(len_ref, rows)
    low_ref[...] = jnp.full(low_ref.shape, low, jnp.int32)
    key = k_ref[...].astype(F32)
    own_ref[:rows, :dim] = (key * rms(key) * gain_ref[...]).astype(BF16)
    own_ref[:rows, dim:] = v_ref[...]
    log_gate = log_sigmoid(logit_ref[...].astype(F32))
    zero = jnp.zeros((heads, rows), F32)
    parts = jnp.concatenate(list(split3(log_gate)) + [zero], axis=0).astype(BF16)

    def sums(test):
        result = dot_nn(parts, ones_where(rows, test))
        return result[:heads] + result[heads : 2 * heads] + result[2 * heads : 3 * heads]

    ahead = sums(lambda u, t: u > t)
    past = sums(lambda u, t: u <= t)
    whole = jnp.broadcast_to(past[:, rows - 1 :], (heads, rows))
    room = TAIL - 6 * heads
    row = iota((room, rows), 0)
    tile = iota((room, rows), 1) // TILE + me * (rows // TILE)
    middle = jnp.where(row < 3, 1.0, 0.0)
    for d, (start, end) in enumerate(spans):
        inside = jnp.where((tile >= start) & (tile < end), 1.0, 0.0)
        middle = jnp.where(row == 3 + d, inside, middle)
    rest = [middle] + list(split3(whole))
    tail = jnp.concatenate(list(split3(ahead)) + rest, axis=0)
    own_ref[rows:, :] = tail.astype(BF16)
    tail_ref[...] = jnp.concatenate(list(split3(-past)) + rest, axis=0).astype(BF16)


def key_columns(kaug, raw, tail):
    rows = kaug.shape[0]
    dim = raw.shape[1] // 2
    kaug[:, :dim] = raw[:rows, :dim]
    filled = jnp.concatenate([tail.astype(F32), jnp.zeros((dim - TAIL, rows), F32)], axis=0)
    kaug[:, dim:] = filled.T.astype(BF16)


def forward_block(kaug, qt, raw, tail, kt, store, mixed, causal):
    rows = kaug.shape[0]
    dim = raw.shape[1] // 2
    key_columns(kaug, raw, tail)
    both = flip(raw[:rows, :])
    kt[:dim, :] = both[:dim]
    kt[dim:, :] = ones_rows(rows)
    value_t = jnp.concatenate([both[dim:], ones_rows(rows)], axis=0)
    for part in chunks(qt.shape[1]):
        scores = dot_nn(kaug[...], qt[:, part])
        if causal:
            place = iota(scores.shape, 1)
            scores = jnp.where(iota(scores.shape, 0) <= place - place // rows * rows, scores, -BIG)
        store[:, part] = jnp.exp(scores).astype(BF16)
    for part in chunks(qt.shape[1]):
        mixed(part, dot_nn(value_t, store[:, part]))


def own_kernel(*refs):
    own_ref, tail_ref, qt, gt, acc, w_ref, kt, kaug = refs[3:11]
    fetch(refs[:3], refs[11:14], refs[14])
    q_ref, g_ref, gain_ref = refs[11:14]
    rows = q_ref.shape[0]
    dim = gain_ref.shape[1]
    heads = q_ref.shape[1] // dim
    scale = dim ** (-0.5)
    tail = tail_ref[...].astype(F32)
    past = -(tail[:heads] + tail[heads : 2 * heads] + tail[2 * heads : 3 * heads])
    parts = split3(past)
    row = iota((TAIL, rows), 0)
    doc_first = 3 * heads + 3
    docs = (row >= doc_first) & (row < TAIL - 3 * heads)
    fixed = jnp.where(docs, (tail - 1.0) * BIG, 0.0)
    for h in range(heads):
        x = q_ref[:, cols(h, dim)].astype(F32)
        normed = x * rms(x) * (gain_ref[...] * scale)
        qt[:dim, cols(h, rows)] = flip(normed.astype(BF16))
        gt[:, cols(h, rows)] = flip(g_ref[:, cols(h, dim)])
        extra = jnp.where(row < 3 * heads, jnp.where(row - row // heads * heads == h, 1.0, 0.0), fixed)
        for s in range(3):
            extra = jnp.where(row == 3 * heads + s, parts[s][h : h + 1], extra)
        qt[dim : dim + TAIL, cols(h, rows)] = extra.astype(BF16)
        qt[dim + TAIL :, cols(h, rows)] = jnp.zeros((dim - TAIL, rows), BF16)

    def mixed(part, value):
        acc[:, part] = value

    forward_block(kaug, qt, own_ref, tail_ref[...], kt, w_ref, mixed, True)


def early_kernel(n, low_ref, qt, *refs):
    half = n // 2
    raw_refs = refs[:half]
    w_ref, o_ref, kt_ref, kaug = refs[half:]
    rows = kaug.shape[0]
    me, low = first_block(low_ref)
    for s in range(half):
        raw = raw_refs[s]

        def mixed(part, value):
            o_ref[s, :, part] = value

        @pl.when(is_active(me, low, 2 * s if s else 1))
        def _():
            forward_block(
                kaug, qt, raw, raw[rows:, :], kt_ref.at[s], w_ref.at[s], mixed, False
            )


def backward_block(rows, raw, weights, factor, inner, kt, qt, gt, ds, plow, acc, kg, piece, gcol):
    dim = raw.shape[1] // 2
    for part in chunks(qt.shape[1]):
        grad = dot_nn(raw[:rows, dim:], gt[:, part])
        prob = weights[:, part].astype(F32) * factor[:, part]
        plow[:, part] = prob.astype(BF16)
        ds[:, part] = (prob * (grad - inner[:, part])).astype(BF16)
    for part in chunks(qt.shape[1]):
        acc[:, part] += dot_nn(kt[...], ds[:, part])
    key_part = dot_nt(qt[: dim + ONES, :], ds[...])
    piece[:dim, :] = key_part[:dim].astype(BF16)
    gcol[...] = -key_part[dim : dim + 8]
    kg[...] += key_part[:dim] * kt[:dim, :].astype(F32)
    piece[dim:, :] = dot_nt(gt[...], plow[...]).astype(BF16)


def idle_block(piece, gcol):
    piece[...] = jnp.zeros(piece.shape, BF16)
    gcol[...] = jnp.zeros(gcol.shape, F32)


def middle_kernel(n, heads, low_ref, qt, gt, acc0, w1_ref, o1, kt1, *refs):
    half = n // 2
    raw_refs = refs[:n]
    out_ref, acc, between_ref, log_ref, inner_ref, gcol, kg = refs[n : n + 7]
    piece_refs = refs[n + 7 : n + 7 + half]
    w, kts, kaug, ds, plow = refs[n + 7 + half :]
    rows = qt.shape[1] // heads
    dim = gt.shape[0]
    me, low = first_block(low_ref)

    wholes = []
    for k in range(n):
        tail = raw_refs[k][rows:, :].astype(F32)[TAIL - 3 * heads :]
        wholes.append(tail[:heads] + tail[heads : 2 * heads] + tail[2 * heads :])
    for k in range(n):
        total = jnp.zeros((heads, rows), F32)
        for other in range(1, n):
            if other != k:
                b = me ^ other
                total = total + jnp.where((b > (me ^ k)) & (b < me), wholes[other], 0.0)
        between_ref[k] = lay_out(total)

    acc[...] = acc0[...]
    for s in range(1, half):
        k = 2 * s + 1

        @pl.when(is_active(me, low, k))
        def _():
            root = jnp.exp(0.5 * between_ref[k])

            def mixed(part, value):
                acc[:, part] += value * root[:, part] * root[:, part]

            raw = raw_refs[k]
            forward_block(kaug, qt, raw, raw[rows:, :], kts.at[s], w.at[s], mixed, False)

    for s in range(half):
        k = 2 * s if s else 1

        @pl.when(is_active(me, low, k))
        def _():
            root = jnp.exp(0.5 * between_ref[k])
            for part in chunks(root.shape[1]):
                acc[:, part] += o1[s, :, part] * root[:, part] * root[:, part]

    eye = ones_where(rows, lambda i, j: i == j)
    for h in range(heads):
        part = cols(h, rows)
        total = acc[dim : dim + 1, part]
        mixed_t = (acc[:dim, part] * (1.0 / total)).astype(BF16)
        out_ref[:, cols(h, dim)] = dot_nt(eye, mixed_t).astype(BF16)
        log_ref[:, part] = jnp.log(total)
        product = gt[:, part].astype(F32) * mixed_t.astype(F32)
        inner_ref[:, part] = jnp.sum(product, axis=0, keepdims=True)
    acc[...] = jnp.zeros(acc.shape, F32)
    kg[...] = jnp.zeros(kg.shape, F32)
    for s in range(half - 1, -1, -1):
        k = 2 * s + 1

        @pl.when(is_active(me, low, k))
        def _():
            factor = jnp.exp(between_ref[k] - log_ref[...])
            weights, kt = (w.at[s], kts.at[s]) if s else (w1_ref.at[0], kt1.at[0])
            backward_block(
                rows, raw_refs[k], weights, factor, inner_ref, kt, qt, gt, ds, plow,
                acc, kg, piece_refs[s], gcol.at[s],
            )

        @pl.when(~is_active(me, low, k))
        def _():
            idle_block(piece_refs[s], gcol.at[s])


def late_block(s, me, low, rows, raw, source, between_ref, log_ref, inner_ref, kt, state, outs):
    qt, gt, ds, plow, acc, kg = state
    piece, gcol = outs

    @pl.when(is_active(me, low, 2 * s))
    def _():
        factor = jnp.exp(between_ref[2 * s] - log_ref[...])
        backward_block(
            rows, raw, source, factor, inner_ref, kt, qt, gt, ds, plow, acc, kg, piece, gcol
        )

    if s:

        @pl.when(~is_active(me, low, 2 * s))
        def _():
            idle_block(piece, gcol)


def late_a_kernel(rows, slots, low_ref, qt, gt, acc0, between, log_ref, inner, kg0, w1, kt1, *refs):
    count = len(slots)
    raw_refs = refs[:count]
    acc, kg, gcol = refs[count : count + 3]
    piece_refs = refs[count + 3 : 2 * count + 3]
    ds, plow = refs[2 * count + 3 :]
    me, low = first_block(low_ref)
    acc[...] = acc0[...]
    kg[...] = kg0[...]
    for i, s in enumerate(slots):
        late_block(
            s, me, low, rows, raw_refs[i], w1.at[s], between, log_ref, inner, kt1.at[s],
            (qt, gt, ds, plow, acc, kg), (piece_refs[i], gcol.at[i]),
        )


def late_b_kernel(n, slots, top, low_ref, q_ref, qgain_ref, kgain_ref, *refs):
    half = n // 2
    count = len(slots)
    qt, gt, acc0, between, log_ref, inner, kg0, w0, kt0, w1, kt1, g_odd, g_top = refs[:13]
    raw_refs = refs[13 : 13 + count]
    qgrad_ref = refs[13 + count]
    keep_ref, give_ref = refs[14 + count : 16 + count]
    piece_refs = refs[16 + count : 16 + 2 * count]
    acc, kg, ds, plow, gall = refs[16 + 2 * count :]
    rows, full = q_ref.shape
    dim = qgain_ref.shape[1]
    heads = full // dim
    scale = dim ** (-0.5)
    me, low = first_block(low_ref)
    acc[...] = acc0[...]
    kg[...] = kg0[...]
    for s in range(half):
        gall[2 * s + 1] = g_odd[s]
    for i, s in enumerate(top):
        gall[2 * s] = g_top[i]
    for i, s in enumerate(slots):
        weights, kt = (w1.at[s], kt1.at[s]) if s else (w0, kt0)
        late_block(
            s, me, low, rows, raw_refs[i], weights, between, log_ref, inner, kt,
            (qt, gt, ds, plow, acc, kg), (piece_refs[i], gall.at[2 * s]),
        )

    query_gain = jnp.zeros((1, dim), F32)
    row_sums = []
    for h in range(heads):
        x = q_ref[:, cols(h, dim)].astype(F32)
        rstd = rms(x)
        hat = x * rstd
        back = acc[:dim, cols(h, rows)].T.astype(BF16).astype(F32)
        row_sums.append(acc[dim : dim + 1, cols(h, rows)])
        query_gain = query_gain + jnp.sum(back * hat, axis=0, keepdims=True)
        back = back * (qgain_ref[...] * scale)
        mean = jnp.mean(back * hat, axis=-1, keepdims=True)
        qgrad_ref[:, cols(h, dim)] = (rstd * (back - hat * mean)).astype(BF16)
    gall[0] += jnp.concatenate(row_sums + row_sums, axis=0)[:8]
    key_gain = jnp.sum(kg[...].T, axis=0, keepdims=True) / kgain_ref[...]
    gain_row = jnp.concatenate([query_gain * scale, key_gain], axis=1)
    is_gain = iota((8, rows), 0) == heads
    later = ones_where(rows, lambda u, t: u >= t)
    stacked = jnp.concatenate([gall[k] for k in range(n)], axis=0)
    suffix = sum(dot_nn(part.astype(BF16), later) for part in split3(stacked))
    locals_ = [suffix[8 * k : 8 * k + 8] for k in range(n)]
    wholes = [jnp.broadcast_to(local[:, :1], (8, rows)) for local in locals_]
    results = []
    for k in range(n):
        total = locals_[k]
        for other in range(n):
            if other != k:
                total = total + jnp.where((me ^ other) > (me ^ k), wholes[other], 0.0)
        total = jnp.where(is_active(me, low, k), total, 0.0)
        results.append(jnp.where(is_gain, gain_row, total))
    for s in range(half):
        keep_ref[8 * s : 8 * s + 8, :] = results[2 * s]
        give_ref[8 * s : 8 * s + 8, :] = results[2 * s + 1]


def add_kernel(a_ref, b_ref, o_ref):
    o_ref[...] = (a_ref[...].astype(F32) + b_ref[...].astype(F32)).astype(BF16)


def settle_kernel(heads, keep_ref, got_ref, total_ref, gain_ref):
    total_ref[...] = keep_ref[...] + got_ref[...]
    gain_ref[...] = total_ref[heads : heads + 1, :]


def pair_kernel(a_ref, b_ref, o_ref):
    o_ref[...] = a_ref[...] + b_ref[...]


def spread_kernel(heads, total_ref, a_ref, b_ref, *outs):
    gain = a_ref[...] + b_ref[...]
    for s, out in enumerate(outs):
        rows = total_ref[8 * s : 8 * s + 8, :]
        out[...] = jnp.where(iota(rows.shape, 0) == heads, gain, rows)


def finish_kernel(half, k_ref, logit_ref, gain_ref, *refs):
    piece_refs = refs[half:-4]
    kgrad_ref, vgrad_ref, fgrad_ref, gains_ref = refs[-4:]
    dim = k_ref.shape[1]
    heads = logit_ref.shape[0]
    small = refs[0][...]
    for ref in refs[1:half]:
        small = small + ref[...]
    row = small[heads : heads + 1]
    gains_ref[...] = jnp.concatenate([row[:, :dim], row[:, dim:]], axis=0)
    total = piece_refs[0][...].astype(F32)
    for ref in piece_refs[1:]:
        total = total + ref[...].astype(F32)
    vgrad_ref[...] = total[dim:].T.astype(BF16)
    x = k_ref[...].astype(F32)
    rstd = rms(x)
    hat = x * rstd
    back = total[:dim].T * gain_ref[...]
    mean = jnp.mean(back * hat, axis=-1, keepdims=True)
    kgrad_ref[...] = (rstd * (back - hat * mean)).astype(BF16)
    logit = logit_ref[...].astype(F32)
    fgrad_ref[...] = small[:heads] * (1.0 / (1.0 + jnp.exp(logit)))


def whole_step(queries, key_vectors, values, forget_logit, out_grad, query_gain, key_gain, lengths):
    n = lax.axis_size("seq")
    half = n // 2
    rows, full = queries.shape[1:]
    dim = query_gain.shape[0]
    heads = full // dim
    wide = heads * rows
    width = 2 * dim
    tall = dim + ONES
    query, grad, key, logit = queries[0], out_grad[0], key_vectors[0], forget_logit[0]
    qgain, kgain = query_gain[None], key_gain[None]
    matmul = 2 * rows * wide * width
    head_row = struct(heads, rows, dtype=F32)
    line = struct(1, wide, dtype=F32)
    state = struct(tall, wide, dtype=F32)
    key_sum = struct(dim, rows, dtype=F32)
    piece = struct(rows, width)
    wide_scratch = pltpu.VMEM((rows, wide), BF16)

    inputs = [lengths, key, values[0], logit, kgain]
    own, own_tail, low = kernel_call(
        pack_kernel, inputs, (
            struct(rows + TAIL, width), struct(TAIL, rows), struct(8, 128, dtype=jnp.int32),
        ),
        near(inputs), far=5,
    )
    blocks = {0: own}
    for k in range(n - 2, 0, -2):
        blocks[k] = swap(own, "seq", k)
    blocks[1] = swap(own, "seq", 1)
    for k in range(n - 2, 0, -2):
        blocks[k + 1] = swap(blocks[k], "seq", 1)

    qt, gt, acc, w0, kt0 = kernel_call(
        own_kernel, [query, grad, qgain, own, own_tail],
        (struct(width, wide), struct(dim, wide), state, struct(rows, wide), struct(tall, rows)),
        [pltpu.VMEM((rows, width), BF16)] + near([query, grad, qgain]),
        flops=2 * matmul,
        far=3,
    )
    early = [1] + [2 * s for s in range(1, half)]
    w1, o1, kt1 = kernel_call(
        functools.partial(early_kernel, n),
        [low, qt] + [blocks[k] for k in early],
        (
            struct(half, rows, wide),
            struct(half, tall, wide, dtype=F32),
            struct(half, tall, rows),
        ),
        [pltpu.VMEM((rows, width), BF16)],
        flops=2 * half * matmul,
    )
    results = kernel_call(
        functools.partial(middle_kernel, n, heads),
        [low, qt, gt, acc, w1, o1, kt1] + [blocks[k] for k in range(n)],
        (
            struct(rows, full), state, struct(n, 1, wide, dtype=F32), line, line,
            struct(half, 8, rows, dtype=F32), key_sum,
        )
        + (piece,) * half,
        [
            pltpu.VMEM((half, rows, wide), BF16),
            pltpu.VMEM((half, tall, rows), BF16),
            pltpu.VMEM((rows, width), BF16),
            wide_scratch,
            wide_scratch,
        ],
        limit=(8 << 20) + n * (1 << 19),
        flops=6 * half * matmul,
    )
    attention, acc, between, log_total, inner, gate_odd, key_acc = results[:7]
    odd = results[7:]
    across = [swap(odd[s], "seq", 1) for s in range(half)]

    top = list(range(half - 1, half // 2 - 1, -1))
    bottom = list(range(half // 2 - 1, -1, -1))
    results = kernel_call(
        functools.partial(late_a_kernel, rows, top),
        [low, qt, gt, acc, between, log_total, inner, key_acc, w1, kt1]
        + [blocks[2 * s] for s in top],
        (state, key_sum, struct(len(top), 8, rows, dtype=F32)) + (piece,) * len(top),
        [wide_scratch, wide_scratch],
        flops=4 * len(top) * matmul,
    )
    acc, key_acc, gate_top = results[:3]
    even = dict(zip(top, results[3:]))
    results = kernel_call(
        functools.partial(late_b_kernel, n, bottom, top),
        [low, query, qgain, kgain, qt, gt, acc, between, log_total, inner, key_acc]
        + [w0, kt0, w1, kt1, gate_odd, gate_top]
        + [blocks[2 * s] for s in bottom],
        (struct(rows, full),)
        + (struct(8 * half, rows, dtype=F32),) * 2
        + (piece,) * len(bottom),
        [
            pltpu.VMEM((tall, wide), F32),
            pltpu.VMEM((dim, rows), F32),
            wide_scratch,
            wide_scratch,
            pltpu.VMEM((n, 8, rows), F32),
        ],
        flops=4 * len(bottom) * matmul,
    )
    query_grad, keep, give = results[:3]
    even.update(zip(bottom, results[3:]))

    arrived = [even[0], across[0]]
    for s in range(half - 1, 0, -1):
        both = kernel_call(add_kernel, [even[s], across[s]], piece)
        arrived.append(swap(both, "seq", 2 * s))

    gain_line = struct(1, width, dtype=F32)
    eight = struct(8, rows, dtype=F32)
    total, gain = kernel_call(
        functools.partial(settle_kernel, heads), [keep, swap(give, "seq", 1)],
        (struct(8 * half, rows, dtype=F32), gain_line),
    )
    bit = 1
    while 2 * bit < lax.axis_size("rep"):
        gain = kernel_call(pair_kernel, [gain, swap(gain, "rep", bit)], gain_line)
        bit *= 2
    smalls = kernel_call(
        functools.partial(spread_kernel, heads),
        [total, gain, swap(gain, "rep", bit)], (eight,) * half,
    )
    smalls = [smalls[0]] + [swap(smalls[s], "seq", 2 * s) for s in range(1, half)]
    key_grad, value_grad, forget_grad, gains = kernel_call(
        functools.partial(finish_kernel, half), [key, logit, kgain] + smalls + arrived,
        (struct(rows, dim), struct(rows, dim), head_row, struct(2, dim, dtype=F32)),
    )
    return (
        attention[None],
        query_grad[None],
        key_grad[None],
        value_grad[None],
        forget_grad[None],
        gains,
    )


def solution(mesh):
    return jax.shard_map(
        whole_step,
        mesh=mesh,
        in_specs=(
            P("rep", "seq", None),
            P("rep", "seq", None),
            P("rep", "seq", None),
            P("rep", None, "seq"),
            P("rep", "seq", None),
            P(),
            P(),
            P("rep", None),
        ),
        out_specs=(
            P("rep", "seq", None),
            P("rep", "seq", None),
            P("rep", "seq", None),
            P("rep", "seq", None),
            P("rep", None, "seq"),
            P(),
        ),
        check_vma=False,
    )
```

profile of v0, /device:TPU:0, one launch (start us, length us, event | category | flops | bytes accessed | tf_op | source)
XLA Modules:
  0.0 70.5 jit_solution(17238636930213122110)
XLA Ops:
  0.6 1.2 %shard_map.127 = (bf16[288,256]{1,0:T(8,128)(2,1)S(1)}, bf16[32,256]{1,0:T(8,128)(2,1)S(1)}, s32[8,128]{1,0:T(8,128)S(1)}) custom-call(s32[1,4]{1,0:T(1,128)} %refs_0_.1, bf16[256,128]{1,0:T(8,128)(2,1)} %bitcast.14, bf16[256,128]{1,0:T(8,128)(2,1)} %bitcast.23, bf16[4,256]{1,0:T(4,128)(2,1)} %bitcast.16, f32[1,128]{1,0:T(1,128)} %bitcast.18), custom_call_target="tpu_custom_call" | custom-call | flops 1048576 | bytes 1048576 | tf_op jit(solution)/shard_map/pallas_call | solution.py:38
  1.8 5.1 %collective-permute-start.3 = (bf16[288,256]{1,0:T(8,128)(2,1)S(1)}, bf16[288,256]{1,0:T(8,128)(2,1)S(1)}, u32[]{:S(2)}, u32[]{:S(2)}) collective-permute-start(bf16[288,256]{1,0:T(8,128)(2,1)S(1)} %get-tuple-element.49.refs_3_.refs_0_.refs_14_), channel_id=1, source_target_pairs={{0,24},{4,28},{8,16},{12,20},{16,8},{20,12},{24,0},{28,4},{1,25},{... | collective-permute-start | bytes 442376 | tf_op jit(solution)/shard_map/ppermute | solution.py:25
  7.0 0.0 collective-permute-start.2
  7.0 0.6 collective-permute-start.1
  7.6 1.7 %collective-permute-start = (bf16[288,256]{1,0:T(8,128)(2,1)S(1)}, bf16[288,256]{1,0:T(8,128)(2,1)S(1)}, u32[]{:S(2)}, u32[]{:S(2)}) collective-permute-start(bf16[288,256]{1,0:T(8,128)(2,1)S(1)} %get-tuple-element.49.refs_3_.refs_0_.refs_14_), channel_id=1, source_target_pairs={{0,4},{4,0},{8,12},{12,8},{16,20},{20,16},{24,28},{28,24},{1,5},{5... | collective-permute-start | bytes 442376 | tf_op jit(solution)/shard_map/ppermute | solution.py:25
  9.3 2.5 %collective-permute-done.3.refs_3_.refs_6_.refs_0_ = bf16[288,256]{1,0:T(8,128)(2,1)S(1)} collective-permute-done((bf16[288,256]{1,0:T(8,128)(2,1)S(1)}, bf16[288,256]{1,0:T(8,128)(2,1)S(1)}, u32[]{:S(2)}, u32[]{:S(2)}) %collective-permute-start.3) | collective-permute-done | bytes 147488 | tf_op jit(solution)/shard_map/ppermute | solution.py:25
  11.8 1.7 %collective-permute-start.6 = (bf16[288,256]{1,0:T(8,128)(2,1)S(1)}, bf16[288,256]{1,0:T(8,128)(2,1)S(1)}, u32[]{:S(2)}, u32[]{:S(2)}) collective-permute-start(bf16[288,256]{1,0:T(8,128)(2,1)S(1)} %collective-permute-done.3.refs_3_.refs_6_.refs_0_), channel_id=1, source_target_pairs={{0,4},{4,0},{8,12},{12,8},{16,20},{20,16},{24,28},{28,24},{1,5},{5... | collective-permute-start | bytes 442376 | tf_op jit(solution)/shard_map/ppermute | solution.py:25
  13.5 6.0 %collective-permute-done.2.refs_2_.refs_4_.refs_1_ = bf16[288,256]{1,0:T(8,128)(2,1)S(1)} collective-permute-done((bf16[288,256]{1,0:T(8,128)(2,1)S(1)}, bf16[288,256]{1,0:T(8,128)(2,1)S(1)}, u32[]{:S(2)}, u32[]{:S(2)}) %collective-permute-start.2) | collective-permute-done | bytes 147488 | tf_op jit(solution)/shard_map/ppermute | solution.py:25
  19.4 1.5 %collective-permute-start.5 = (bf16[288,256]{1,0:T(8,128)(2,1)S(1)}, bf16[288,256]{1,0:T(8,128)(2,1)S(1)}, u32[]{:S(2)}, u32[]{:S(2)}) collective-permute-start(bf16[288,256]{1,0:T(8,128)(2,1)S(1)} %collective-permute-done.2.refs_2_.refs_4_.refs_1_), channel_id=1, source_target_pairs={{0,4},{4,0},{8,12},{12,8},{16,20},{20,16},{24,28},{28,24},{1,5},{5... | collective-permute-start | bytes 442376 | tf_op jit(solution)/shard_map/ppermute | solution.py:25
  21.0 0.0 collective-permute-done.1.refs_1_.refs_2_.refs_13_
  21.0 0.5 collective-permute-start.4
  21.5 2.0 %shard_map.128 = (bf16[256,1024]{1,0:T(8,128)(2,1)S(1)}, bf16[128,1024]{1,0:T(8,128)(2,1)S(1)}, f32[144,1024]{1,0:T(8,128)S(1)}, bf16[256,1024]{1,0:T(8,128)(2,1)S(1)}, bf16[144,256]{1,0:T(8,128)(2,1)S(1)}) custom-call(bf16[256,512]{1,0:T(8,128)(2,1)} %bitcast.12, bf16[256,512]{1,0:T(8,128)(2,1)} %bitcast.24, f32[1,128]{1,0:T(1,128)} %bitcast.21, ...), custom_call_target="tpu_custom_call" | custom-call | flops 268435456 | bytes 1048576 | tf_op jit(solution)/shard_map/pallas_call | solution.py:38
  23.5 0.0 collective-permute-done.refs_0_.refs_1_
  23.5 0.1 shard_map.129
  23.6 0.0 collective-permute-done.6.refs_7_
  23.6 2.4 %collective-permute-done.5.refs_5_ = bf16[288,256]{1,0:T(8,128)(2,1)S(1)} collective-permute-done((bf16[288,256]{1,0:T(8,128)(2,1)S(1)}, bf16[288,256]{1,0:T(8,128)(2,1)S(1)}, u32[]{:S(2)}, u32[]{:S(2)}) %collective-permute-start.5) | collective-permute-done | bytes 147488 | tf_op jit(solution)/shard_map/ppermute | solution.py:25
  25.9 1.6 %collective-permute-done.4.refs_3_ = bf16[288,256]{1,0:T(8,128)(2,1)S(1)} collective-permute-done((bf16[288,256]{1,0:T(8,128)(2,1)S(1)}, bf16[288,256]{1,0:T(8,128)(2,1)S(1)}, u32[]{:S(2)}, u32[]{:S(2)}) %collective-permute-start.4) | collective-permute-done | bytes 147488 | tf_op jit(solution)/shard_map/ppermute | solution.py:25
  27.5 1.3 %shard_map.130 = (bf16[256,512]{1,0:T(8,128)(2,1)}, f32[144,1024]{1,0:T(8,128)S(1)}, f32[8,1,1024]{2,1,0:T(1,128)S(1)}, f32[1,1024]{1,0:T(1,128)S(1)}, f32[1,102...) custom-call(s32[8,128]{1,0:T(8,128)S(1)} %get-tuple-element.48.low_r, ...), custom_call_target="tpu_custom_call" | custom-call | flops 3221225472 | bytes 1048576 | tf_op jit(solution)/shard_map/pallas_call | solution.py:38
  28.8 0.0 copy-start
  28.8 0.0 copy-start.3
  28.8 0.0 copy-start.4
  28.8 2.4 %collective-permute-start.13 = (bf16[256,256]{1,0:T(8,128)(2,1)S(1)}, bf16[256,256]{1,0:T(8,128)(2,1)S(1)}, u32[]{:S(2)}, u32[]{:S(2)}) collective-permute-start(bf16[256,256]{1,0:T(8,128)(2,1)S(1)} %get-tuple-element.79), channel_id=1, source_target_pairs={{0,4},{4,0},{8,12},{12,8},{16,20},{20,16},{24,28},{28,24},{1,5},{5... | collective-permute-start | bytes 393224 | tf_op jit(solution)/shard_map/ppermute | solution.py:25
  31.2 0.1 collective-permute-start.14
  31.3 2.0 %collective-permute-start.16 = (bf16[256,256]{1,0:T(8,128)(2,1)S(1)}, bf16[256,256]{1,0:T(8,128)(2,1)S(1)}, u32[]{:S(2)}, u32[]{:S(2)}) collective-permute-start(bf16[256,256]{1,0:T(8,128)(2,1)S(1)} %get-tuple-element.83), channel_id=1, source_target_pairs={{0,4},{4,0},{8,12},{12,8},{16,20},{20,16},{24,28},{28,24},{1,5},{5... | collective-permute-start | bytes 393224 | tf_op jit(solution)/shard_map/ppermute | solution.py:25
  33.3 0.1 collective-permute-start.18
  33.3 0.1 shard_map.131
  33.4 0.0 copy-done
  33.4 0.0 copy-done.3
  33.4 0.0 copy-done.4
  33.5 0.0 copy-start.1
  33.5 0.0 copy-start.2
  33.5 2.5 %shard_map.132 = (bf16[256,512]{1,0:T(8,128)(2,1)}, f32[32,256]{1,0:T(8,128)S(1)}, f32[32,256]{1,0:T(8,128)S(1)}, bf16[256,256]{1,0:T(8,128)(2,1)S(1)}, bf16[256,256]{1,0:T(8,128)(2,1)S(1)}) custom-call(s32[8,128]{1,0:T(8,128)S(1)} %get-tuple-element.48.low_ref, bf16[256,512]{1,0:T(8,128)(2,1)S(1)} %bitcast.13, f32[1,128]{1,0:T(1,128)S(1)} %bitcast.22, ...), custom_call_target="tpu_custom_call" | custom-call | flops 1073741824 | bytes 1048576 | tf_op jit(solution)/shard_map/pallas_call | solution.py:38
  36.0 5.7 %collective-permute-done.18.b_ref = bf16[256,256]{1,0:T(8,128)(2,1)S(1)} collective-permute-done((bf16[256,256]{1,0:T(8,128)(2,1)S(1)}, bf16[256,256]{1,0:T(8,128)(2,1)S(1)}, u32[]{:S(2)}, u32[]{:S(2)}) %collective-permute-start.18) | collective-permute-done | bytes 131104 | tf_op jit(solution)/shard_map/ppermute | solution.py:25
  41.7 2.2 %collective-permute-start.19 = (bf16[256,256]{1,0:T(8,128)(2,1)S(1)}, bf16[256,256]{1,0:T(8,128)(2,1)S(1)}, u32[]{:S(2)}, u32[]{:S(2)}) collective-permute-start(bf16[256,256]{1,0:T(8,128)(2,1)S(1)} %shard_map.138), channel_id=1, source_target_pairs={{0,8},{4,12},{8,0},{12,4},{16,24},{20,28},{24,16},{28,20},{1,9},{5... | collective-permute-start | bytes 393224 | tf_op jit(solution)/shard_map/ppermute | solution.py:25
  43.9 0.0 collective-permute-done.14.b_ref
  43.9 1.9 %collective-permute-start.15 = (bf16[256,256]{1,0:T(8,128)(2,1)S(1)}, bf16[256,256]{1,0:T(8,128)(2,1)S(1)}, u32[]{:S(2)}, u32[]{:S(2)}) collective-permute-start(bf16[256,256]{1,0:T(8,128)(2,1)S(1)} %shard_map.136), channel_id=1, source_target_pairs={{0,24},{4,28},{8,16},{12,20},{16,8},{20,12},{24,0},{28,4},{1,25},{... | collective-permute-start | bytes 393224 | tf_op jit(solution)/shard_map/ppermute | solution.py:25
  45.8 0.0 collective-permute-done.16.b_ref
  45.8 0.1 collective-permute-start.17
  45.9 1.7 %collective-permute-start.7 = (f32[32,256]{1,0:T(8,128)S(1)}, f32[32,256]{1,0:T(8,128)S(1)}, u32[]{:S(2)}, u32[]{:S(2)}) collective-permute-start(f32[32,256]{1,0:T(8,128)S(1)} %get-tuple-element.71), channel_id=1, source_target_pairs={{0,4},{4,0},{8,12},{12,8},{16,20},{20,16},{24,28},{28,24},{1,5},{5... | collective-permute-start | bytes 98312 | tf_op jit(solution)/shard_map/ppermute | solution.py:25
  47.7 2.2 %collective-permute-done.7.got_ref = f32[32,256]{1,0:T(8,128)S(1)} collective-permute-done((f32[32,256]{1,0:T(8,128)S(1)}, f32[32,256]{1,0:T(8,128)S(1)}, u32[]{:S(2)}, u32[]{:S(2)}) %collective-permute-start.7) | collective-permute-done | bytes 32800 | tf_op jit(solution)/shard_map/ppermute | solution.py:25
  49.9 0.1 collective-permute-start.8
  50.0 1.1 %collective-permute-done.8.b_ref = f32[1,256]{1,0:T(1,128)S(1)} collective-permute-done((f32[1,256]{1,0:T(1,128)S(1)}, f32[1,256]{1,0:T(1,128)S(1)}, u32[]{:S(2)}, u32[]{:S(2)}) %collective-permute-start.8) | collective-permute-done | bytes 1056 | tf_op jit(solution)/shard_map/ppermute | solution.py:25
  51.1 3.1 %collective-permute-start.9 = (f32[1,256]{1,0:T(1,128)S(1)}, f32[1,256]{1,0:T(1,128)S(1)}, u32[]{:S(2)}, u32[]{:S(2)}) collective-permute-start(f32[1,256]{1,0:T(1,128)S(1)} %shard_map.134.a_ref), channel_id=1, source_target_pairs={{0,2},{1,3},{2,0},{3,1},{4,6},{5,7},{6,4},{7,5},{8,10},{9,11},{10,... | collective-permute-start | bytes 3080 | tf_op jit(solution)/shard_map/ppermute | solution.py:25
  54.3 1.6 %collective-permute-done.9.b_ref = f32[1,256]{1,0:T(1,128)S(1)} collective-permute-done((f32[1,256]{1,0:T(1,128)S(1)}, f32[1,256]{1,0:T(1,128)S(1)}, u32[]{:S(2)}, u32[]{:S(2)}) %collective-permute-start.9) | collective-permute-done | bytes 1056 | tf_op jit(solution)/shard_map/ppermute | solution.py:25
  55.8 1.4 %collective-permute-start.10 = (f32[8,256]{1,0:T(8,128)S(1)}, f32[8,256]{1,0:T(8,128)S(1)}, u32[]{:S(2)}, u32[]{:S(2)}) collective-permute-start(f32[8,256]{1,0:T(8,128)S(1)} %get-tuple-element.75), channel_id=1, source_target_pairs={{0,8},{4,12},{8,0},{12,4},{16,24},{20,28},{24,16},{28,20},{1,9},{5... | collective-permute-start | bytes 24584 | tf_op jit(solution)/shard_map/ppermute | solution.py:25
  57.2 2.3 %collective-permute-done.10.refs_1_ = f32[8,256]{1,0:T(8,128)S(1)} collective-permute-done((f32[8,256]{1,0:T(8,128)S(1)}, f32[8,256]{1,0:T(8,128)S(1)}, u32[]{:S(2)}, u32[]{:S(2)}) %collective-permute-start.10) | collective-permute-done | bytes 8224 | tf_op jit(solution)/shard_map/ppermute | solution.py:25
  59.5 2.4 %collective-permute-start.11 = (f32[8,256]{1,0:T(8,128)S(1)}, f32[8,256]{1,0:T(8,128)S(1)}, u32[]{:S(2)}, u32[]{:S(2)}) collective-permute-start(f32[8,256]{1,0:T(8,128)S(1)} %get-tuple-element.76), channel_id=1, source_target_pairs={{0,16},{4,20},{8,24},{12,28},{16,0},{20,4},{24,8},{28,12},{1,17},{... | collective-permute-start | bytes 24584 | tf_op jit(solution)/shard_map/ppermute | solution.py:25
  61.8 2.2 %collective-permute-done.11.refs_2_ = f32[8,256]{1,0:T(8,128)S(1)} collective-permute-done((f32[8,256]{1,0:T(8,128)S(1)}, f32[8,256]{1,0:T(8,128)S(1)}, u32[]{:S(2)}, u32[]{:S(2)}) %collective-permute-start.11) | collective-permute-done | bytes 8224 | tf_op jit(solution)/shard_map/ppermute | solution.py:25
  64.0 2.9 %collective-permute-start.12 = (f32[8,256]{1,0:T(8,128)S(1)}, f32[8,256]{1,0:T(8,128)S(1)}, u32[]{:S(2)}, u32[]{:S(2)}) collective-permute-start(f32[8,256]{1,0:T(8,128)S(1)} %get-tuple-element.77), channel_id=1, source_target_pairs={{0,24},{4,28},{8,16},{12,20},{16,8},{20,12},{24,0},{28,4},{1,25},{... | collective-permute-start | bytes 24584 | tf_op jit(solution)/shard_map/ppermute | solution.py:25
  67.0 2.5 %collective-permute-done.12.refs_3_ = f32[8,256]{1,0:T(8,128)S(1)} collective-permute-done((f32[8,256]{1,0:T(8,128)S(1)}, f32[8,256]{1,0:T(8,128)S(1)}, u32[]{:S(2)}, u32[]{:S(2)}) %collective-permute-start.12) | collective-permute-done | bytes 8224 | tf_op jit(solution)/shard_map/ppermute | solution.py:25
  69.5 0.0 collective-permute-done.13.refs_5_
  69.5 0.0 collective-permute-done.19.refs_8_
  69.5 0.0 collective-permute-done.15.refs_6_
  69.5 0.0 collective-permute-done.17.refs_7_
  69.5 0.0 copy-done.1
  69.5 0.0 copy-done.2
  69.5 0.9 %shard_map.139 = (bf16[256,128]{1,0:T(8,128)(2,1)}, bf16[256,128]{1,0:T(8,128)(2,1)}, f32[4,256]{1,0:T(4,128)}, f32[2,128]{1,0:T(2,128)}) custom-call(bf16[256,128]{1,0:T(8,128)(2,1)S(1)} %bitcast.15, bf16[4,256]{1,0:T(4,128)(2,1)S(1)} %bitcast.17, f32[1,128]{1,0:T(1,128)S(1)} %bitcast.20, f32[8,256]{1,0:T(8,128)S(1)} %get-tuple-element.74.refs_0_, ...), custom_call_target="tpu_custom_call" | custom-call | flops 1048576 | bytes 1048576 | tf_op jit(solution)/shard_map/pallas_call | solution.py:38
  (6 shorter events, 0.1 us)
Async XLA Ops:
  1.8 9.9 %collective-permute-start.3 = (bf16[288,256]{1,0:T(8,128)(2,1)S(1)}, bf16[288,256]{1,0:T(8,128)(2,1)S(1)}, u32[]{:S(2)}, u32[]{:S(2)}) collective-permute-start(bf16[288,256]{1,0:T(8,128)(2,1)S(1)} %get-tuple-element.49.refs_3_.refs_0_.refs_14_), channel_id=1, source_target_pairs={{0,24},{4,28},{8,16},{12,20},{16,8},{20,12},{24,0},{28,4},{1,25},{... | collective-permute-start | bytes 442376 | tf_op jit(solution)/shard_map/ppermute | solution.py:25
  7.0 12.5 %collective-permute-start.2 = (bf16[288,256]{1,0:T(8,128)(2,1)S(1)}, bf16[288,256]{1,0:T(8,128)(2,1)S(1)}, u32[]{:S(2)}, u32[]{:S(2)}) collective-permute-start(bf16[288,256]{1,0:T(8,128)(2,1)S(1)} %get-tuple-element.49.refs_3_.refs_0_.refs_14_), channel_id=1, source_target_pairs={{0,16},{4,20},{8,24},{12,28},{16,0},{20,4},{24,8},{28,12},{1,17},{... | collective-permute-start | bytes 442376 | tf_op jit(solution)/shard_map/ppermute | solution.py:25
  7.0 14.0 %collective-permute-start.1 = (bf16[288,256]{1,0:T(8,128)(2,1)S(1)}, bf16[288,256]{1,0:T(8,128)(2,1)S(1)}, u32[]{:S(2)}, u32[]{:S(2)}) collective-permute-start(bf16[288,256]{1,0:T(8,128)(2,1)S(1)} %get-tuple-element.49.refs_3_.refs_0_.refs_14_), channel_id=1, source_target_pairs={{0,8},{4,12},{8,0},{12,4},{16,24},{20,28},{24,16},{28,20},{1,9},{5... | collective-permute-start | bytes 442376 | tf_op jit(solution)/shard_map/ppermute | solution.py:25
  7.6 15.9 %collective-permute-start = (bf16[288,256]{1,0:T(8,128)(2,1)S(1)}, bf16[288,256]{1,0:T(8,128)(2,1)S(1)}, u32[]{:S(2)}, u32[]{:S(2)}) collective-permute-start(bf16[288,256]{1,0:T(8,128)(2,1)S(1)} %get-tuple-element.49.refs_3_.refs_0_.refs_14_), channel_id=1, source_target_pairs={{0,4},{4,0},{8,12},{12,8},{16,20},{20,16},{24,28},{28,24},{1,5},{5... | collective-permute-start | bytes 442376 | tf_op jit(solution)/shard_map/ppermute | solution.py:25
  11.8 11.8 %collective-permute-start.6 = (bf16[288,256]{1,0:T(8,128)(2,1)S(1)}, bf16[288,256]{1,0:T(8,128)(2,1)S(1)}, u32[]{:S(2)}, u32[]{:S(2)}) collective-permute-start(bf16[288,256]{1,0:T(8,128)(2,1)S(1)} %collective-permute-done.3.refs_3_.refs_6_.refs_0_), channel_id=1, source_target_pairs={{0,4},{4,0},{8,12},{12,8},{16,20},{20,16},{24,28},{28,24},{1,5},{5... | collective-permute-start | bytes 442376 | tf_op jit(solution)/shard_map/ppermute | solution.py:25
  19.4 6.5 %collective-permute-start.5 = (bf16[288,256]{1,0:T(8,128)(2,1)S(1)}, bf16[288,256]{1,0:T(8,128)(2,1)S(1)}, u32[]{:S(2)}, u32[]{:S(2)}) collective-permute-start(bf16[288,256]{1,0:T(8,128)(2,1)S(1)} %collective-permute-done.2.refs_2_.refs_4_.refs_1_), channel_id=1, source_target_pairs={{0,4},{4,0},{8,12},{12,8},{16,20},{20,16},{24,28},{28,24},{1,5},{5... | collective-permute-start | bytes 442376 | tf_op jit(solution)/shard_map/ppermute | solution.py:25
  21.0 6.6 %collective-permute-start.4 = (bf16[288,256]{1,0:T(8,128)(2,1)S(1)}, bf16[288,256]{1,0:T(8,128)(2,1)S(1)}, u32[]{:S(2)}, u32[]{:S(2)}) collective-permute-start(bf16[288,256]{1,0:T(8,128)(2,1)S(1)} %collective-permute-done.1.refs_1_.refs_2_.refs_13_), channel_id=1, source_target_pairs={{0,4},{4,0},{8,12},{12,8},{16,20},{20,16},{24,28},{28,24},{1,5},{5... | collective-permute-start | bytes 442376 | tf_op jit(solution)/shard_map/ppermute | solution.py:25
  28.8 4.6 %copy-start = (bf16[1,256,512]{2,1,0:T(8,128)(2,1)S(1)}, bf16[1,256,512]{2,1,0:T(8,128)(2,1)}, u32[]{:S(2)}) copy-start(bf16[1,256,512]{2,1,0:T(8,128)(2,1)} %param.8) | copy-start | bytes 786436
  28.8 4.6 %copy-start.3 = (f32[128]{0:T(128)S(1)}, f32[128]{0:T(128)}, u32[]{:S(2)}) copy-start(f32[128]{0:T(128)} %param.14) | copy-start | bytes 1540
  28.8 4.6 %copy-start.4 = (f32[128]{0:T(128)S(1)}, f32[128]{0:T(128)}, u32[]{:S(2)}) copy-start(f32[128]{0:T(128)} %param.13) | copy-start | bytes 1540
  28.8 40.7 %collective-permute-start.13 = (bf16[256,256]{1,0:T(8,128)(2,1)S(1)}, bf16[256,256]{1,0:T(8,128)(2,1)S(1)}, u32[]{:S(2)}, u32[]{:S(2)}) collective-permute-start(bf16[256,256]{1,0:T(8,128)(2,1)S(1)} %get-tuple-element.79), channel_id=1, source_target_pairs={{0,4},{4,0},{8,12},{12,8},{16,20},{20,16},{24,28},{28,24},{1,5},{5... | collective-permute-start | bytes 393224 | tf_op jit(solution)/shard_map/ppermute | solution.py:25
  31.2 12.7 %collective-permute-start.14 = (bf16[256,256]{1,0:T(8,128)(2,1)S(1)}, bf16[256,256]{1,0:T(8,128)(2,1)S(1)}, u32[]{:S(2)}, u32[]{:S(2)}) collective-permute-start(bf16[256,256]{1,0:T(8,128)(2,1)S(1)} %get-tuple-element.81), channel_id=1, source_target_pairs={{0,4},{4,0},{8,12},{12,8},{16,20},{20,16},{24,28},{28,24},{1,5},{5... | collective-permute-start | bytes 393224 | tf_op jit(solution)/shard_map/ppermute | solution.py:25
  31.3 14.5 %collective-permute-start.16 = (bf16[256,256]{1,0:T(8,128)(2,1)S(1)}, bf16[256,256]{1,0:T(8,128)(2,1)S(1)}, u32[]{:S(2)}, u32[]{:S(2)}) collective-permute-start(bf16[256,256]{1,0:T(8,128)(2,1)S(1)} %get-tuple-element.83), channel_id=1, source_target_pairs={{0,4},{4,0},{8,12},{12,8},{16,20},{20,16},{24,28},{28,24},{1,5},{5... | collective-permute-start | bytes 393224 | tf_op jit(solution)/shard_map/ppermute | solution.py:25
  33.3 8.4 %collective-permute-start.18 = (bf16[256,256]{1,0:T(8,128)(2,1)S(1)}, bf16[256,256]{1,0:T(8,128)(2,1)S(1)}, u32[]{:S(2)}, u32[]{:S(2)}) collective-permute-start(bf16[256,256]{1,0:T(8,128)(2,1)S(1)} %get-tuple-element.85), channel_id=1, source_target_pairs={{0,4},{4,0},{8,12},{12,8},{16,20},{20,16},{24,28},{28,24},{1,5},{5... | collective-permute-start | bytes 393224 | tf_op jit(solution)/shard_map/ppermute | solution.py:25
  33.5 36.1 %copy-start.1 = (bf16[1,256,128]{2,1,0:T(8,128)(2,1)S(1)}, bf16[1,256,128]{2,1,0:T(8,128)(2,1)}, u32[]{:S(2)}) copy-start(bf16[1,256,128]{2,1,0:T(8,128)(2,1)} %param.9) | copy-start | bytes 196612
  33.5 36.1 %copy-start.2 = (bf16[1,4,256]{2,1,0:T(4,128)(2,1)S(1)}, bf16[1,4,256]{2,1,0:T(4,128)(2,1)}, u32[]{:S(2)}) copy-start(bf16[1,4,256]{2,1,0:T(4,128)(2,1)} %param.11) | copy-start | bytes 6148
  41.7 27.8 %collective-permute-start.19 = (bf16[256,256]{1,0:T(8,128)(2,1)S(1)}, bf16[256,256]{1,0:T(8,128)(2,1)S(1)}, u32[]{:S(2)}, u32[]{:S(2)}) collective-permute-start(bf16[256,256]{1,0:T(8,128)(2,1)S(1)} %shard_map.138), channel_id=1, source_target_pairs={{0,8},{4,12},{8,0},{12,4},{16,24},{20,28},{24,16},{28,20},{1,9},{5... | collective-permute-start | bytes 393224 | tf_op jit(solution)/shard_map/ppermute | solution.py:25
  43.9 25.6 %collective-permute-start.15 = (bf16[256,256]{1,0:T(8,128)(2,1)S(1)}, bf16[256,256]{1,0:T(8,128)(2,1)S(1)}, u32[]{:S(2)}, u32[]{:S(2)}) collective-permute-start(bf16[256,256]{1,0:T(8,128)(2,1)S(1)} %shard_map.136), channel_id=1, source_target_pairs={{0,24},{4,28},{8,16},{12,20},{16,8},{20,12},{24,0},{28,4},{1,25},{... | collective-permute-start | bytes 393224 | tf_op jit(solution)/shard_map/ppermute | solution.py:25
  45.8 23.7 %collective-permute-start.17 = (bf16[256,256]{1,0:T(8,128)(2,1)S(1)}, bf16[256,256]{1,0:T(8,128)(2,1)S(1)}, u32[]{:S(2)}, u32[]{:S(2)}) collective-permute-start(bf16[256,256]{1,0:T(8,128)(2,1)S(1)} %shard_map.137), channel_id=1, source_target_pairs={{0,16},{4,20},{8,24},{12,28},{16,0},{20,4},{24,8},{28,12},{1,17},{... | collective-permute-start | bytes 393224 | tf_op jit(solution)/shard_map/ppermute | solution.py:25
  45.9 4.0 %collective-permute-start.7 = (f32[32,256]{1,0:T(8,128)S(1)}, f32[32,256]{1,0:T(8,128)S(1)}, u32[]{:S(2)}, u32[]{:S(2)}) collective-permute-start(f32[32,256]{1,0:T(8,128)S(1)} %get-tuple-element.71), channel_id=1, source_target_pairs={{0,4},{4,0},{8,12},{12,8},{16,20},{20,16},{24,28},{28,24},{1,5},{5... | collective-permute-start | bytes 98312 | tf_op jit(solution)/shard_map/ppermute | solution.py:25
  49.9 1.2 %collective-permute-start.8 = (f32[1,256]{1,0:T(1,128)S(1)}, f32[1,256]{1,0:T(1,128)S(1)}, u32[]{:S(2)}, u32[]{:S(2)}) collective-permute-start(f32[1,256]{1,0:T(1,128)S(1)} %get-tuple-element.73.a_ref), channel_id=1, source_target_pairs={{0,1},{1,0},{2,3},{3,2},{4,5},{5,4},{6,7},{7,6},{8,9},{9,8},{10,11... | collective-permute-start | bytes 3080 | tf_op jit(solution)/shard_map/ppermute | solution.py:25
  51.1 4.7 %collective-permute-start.9 = (f32[1,256]{1,0:T(1,128)S(1)}, f32[1,256]{1,0:T(1,128)S(1)}, u32[]{:S(2)}, u32[]{:S(2)}) collective-permute-start(f32[1,256]{1,0:T(1,128)S(1)} %shard_map.134.a_ref), channel_id=1, source_target_pairs={{0,2},{1,3},{2,0},{3,1},{4,6},{5,7},{6,4},{7,5},{8,10},{9,11},{10,... | collective-permute-start | bytes 3080 | tf_op jit(solution)/shard_map/ppermute | solution.py:25
  55.8 3.7 %collective-permute-start.10 = (f32[8,256]{1,0:T(8,128)S(1)}, f32[8,256]{1,0:T(8,128)S(1)}, u32[]{:S(2)}, u32[]{:S(2)}) collective-permute-start(f32[8,256]{1,0:T(8,128)S(1)} %get-tuple-element.75), channel_id=1, source_target_pairs={{0,8},{4,12},{8,0},{12,4},{16,24},{20,28},{24,16},{28,20},{1,9},{5... | collective-permute-start | bytes 24584 | tf_op jit(solution)/shard_map/ppermute | solution.py:25
  59.5 4.5 %collective-permute-start.11 = (f32[8,256]{1,0:T(8,128)S(1)}, f32[8,256]{1,0:T(8,128)S(1)}, u32[]{:S(2)}, u32[]{:S(2)}) collective-permute-start(f32[8,256]{1,0:T(8,128)S(1)} %get-tuple-element.76), channel_id=1, source_target_pairs={{0,16},{4,20},{8,24},{12,28},{16,0},{20,4},{24,8},{28,12},{1,17},{... | collective-permute-start | bytes 24584 | tf_op jit(solution)/shard_map/ppermute | solution.py:25
  64.0 5.4 %collective-permute-start.12 = (f32[8,256]{1,0:T(8,128)S(1)}, f32[8,256]{1,0:T(8,128)S(1)}, u32[]{:S(2)}, u32[]{:S(2)}) collective-permute-start(f32[8,256]{1,0:T(8,128)S(1)} %get-tuple-element.77), channel_id=1, source_target_pairs={{0,24},{4,28},{8,16},{12,20},{16,8},{20,12},{24,0},{28,4},{1,25},{... | collective-permute-start | bytes 24584 | tf_op jit(solution)/shard_map/ppermute | solution.py:25
where the time goes:
time: 70.7 us; the launch traced here: 70.5 us
  starting transfers between devices  31.4 us (44%)
  waiting for transfers between devices  30.1 us (43%)
  Pallas kernels  8.12 us (11%)
  between operations  0.79 us (1%)
    ppermute x20, starting transfers between devices, swap(): return lax.ppermute(value, axis, [(i, i ^ bit) for i in range(count)])  31.4 us
    ppermute x20, waiting for transfers between devices, swap(): return lax.ppermute(value, axis, [(i, i ^ bit) for i in range(count)])  30.1 us
    pallas_call x13, Pallas kernels, kernel_call(): pl.pallas_call(kernel, out_shape=outs, in_specs=in_specs, out_specs=jax.t...  8.12 us
  transfers between devices with their start and end apart: 20, of which 11 were waited for; matrix products, arithmetic and copies ran while one was open for 0% of the time, Pallas kernels for 7%

commit v1 on v0

--- a/solution.py
+++ b/solution.py
@@ -23,6 +23,11 @@
 def swap(value, axis, bit):
     count = lax.axis_size(axis)
     return lax.ppermute(value, axis, [(i, i ^ bit) for i in range(count)])
+
+
+def swap_both(value, bit):
+    count = lax.axis_size("seq") * lax.axis_size("rep")
+    return lax.ppermute(value, ("seq", "rep"), [(i, i ^ bit) for i in range(count)])
 
 
 def struct(*shape, dtype=BF16):
@@ -363,64 +368,39 @@
             idle_block(piece, gcol)
 
 
-def late_a_kernel(rows, slots, low_ref, qt, gt, acc0, between, log_ref, inner, kg0, w1, kt1, *refs):
-    count = len(slots)
-    raw_refs = refs[:count]
-    acc, kg, gcol = refs[count : count + 3]
-    piece_refs = refs[count + 3 : 2 * count + 3]
-    ds, plow = refs[2 * count + 3 :]
-    me, low = first_block(low_ref)
-    acc[...] = acc0[...]
-    kg[...] = kg0[...]
-    for i, s in enumerate(slots):
-        late_block(
-            s, me, low, rows, raw_refs[i], w1.at[s], between, log_ref, inner, kt1.at[s],
-            (qt, gt, ds, plow, acc, kg), (piece_refs[i], gcol.at[i]),
-        )
-
-
-def late_b_kernel(n, slots, top, low_ref, q_ref, qgain_ref, kgain_ref, *refs):
+def late_kernel(n, low_ref, kgain_ref, qgain_ref, *refs):
     half = n // 2
-    count = len(slots)
-    qt, gt, acc0, between, log_ref, inner, kg0, w0, kt0, w1, kt1, g_odd, g_top = refs[:13]
-    raw_refs = refs[13 : 13 + count]
-    qgrad_ref = refs[13 + count]
-    keep_ref, give_ref = refs[14 + count : 16 + count]
-    piece_refs = refs[16 + count : 16 + 2 * count]
-    acc, kg, ds, plow, gall = refs[16 + 2 * count :]
-    rows, full = q_ref.shape
+    qt, gt, acc0, between, log_ref, inner, kg0, w0, kt0, w1, kt1, g_odd = refs[:12]
+    raw_refs = refs[12 : 12 + half]
+    acc, keep_ref, give_ref, gain_ref = refs[12 + half : 16 + half]
+    piece_refs = refs[16 + half : 16 + 2 * half]
+    kg, ds, plow, gall = refs[16 + 2 * half :]
+    rows = ds.shape[0]
     dim = qgain_ref.shape[1]
-    heads = full // dim
-    scale = dim ** (-0.5)
+    heads = qt.shape[1] // rows
     me, low = first_block(low_ref)
     acc[...] = acc0[...]
     kg[...] = kg0[...]
     for s in range(half):
         gall[2 * s + 1] = g_odd[s]
-    for i, s in enumerate(top):
-        gall[2 * s] = g_top[i]
-    for i, s in enumerate(slots):
+    for s in range(half - 1, -1, -1):
         weights, kt = (w1.at[s], kt1.at[s]) if s else (w0, kt0)
         late_block(
-            s, me, low, rows, raw_refs[i], weights, between, log_ref, inner, kt,
-            (qt, gt, ds, plow, acc, kg), (piece_refs[i], gall.at[2 * s]),
+            s, me, low, rows, raw_refs[s], weights, between, log_ref, inner, kt,
+            (qt, gt, ds, plow, acc, kg), (piece_refs[s], gall.at[2 * s]),
         )
 
-    query_gain = jnp.zeros((1, dim), F32)
+    qg = jnp.zeros((dim, rows), F32)
     row_sums = []
     for h in range(heads):
-        x = q_ref[:, cols(h, dim)].astype(F32)
-        rstd = rms(x)
-        hat = x * rstd
-        back = acc[:dim, cols(h, rows)].T.astype(BF16).astype(F32)
-        row_sums.append(acc[dim : dim + 1, cols(h, rows)])
-        query_gain = query_gain + jnp.sum(back * hat, axis=0, keepdims=True)
-        back = back * (qgain_ref[...] * scale)
-        mean = jnp.mean(back * hat, axis=-1, keepdims=True)
-        qgrad_ref[:, cols(h, dim)] = (rstd * (back - hat * mean)).astype(BF16)
+        part = cols(h, rows)
+        qg = qg + acc[:dim, part] * qt[:dim, part].astype(F32)
+        row_sums.append(acc[dim : dim + 1, part])
     gall[0] += jnp.concatenate(row_sums + row_sums, axis=0)[:8]
+    query_gain = jnp.sum(qg.T, axis=0, keepdims=True) / qgain_ref[...]
     key_gain = jnp.sum(kg[...].T, axis=0, keepdims=True) / kgain_ref[...]
-    gain_row = jnp.concatenate([query_gain * scale, key_gain], axis=1)
+    gain_row = jnp.concatenate([query_gain, key_gain], axis=1)
+    gain_ref[...] = gain_row
     is_gain = iota((8, rows), 0) == heads
     later = ones_where(rows, lambda u, t: u >= t)
     stacked = jnp.concatenate([gall[k] for k in range(n)], axis=0)
@@ -440,36 +420,42 @@
         give_ref[8 * s : 8 * s + 8, :] = results[2 * s + 1]
 
 
+def query_kernel(q_ref, qgain_ref, acc, qgrad_ref):
+    rows = q_ref.shape[0]
+    dim = qgain_ref.shape[1]
+    scale = dim ** (-0.5)
+    for h in range(q_ref.shape[1] // dim):
+        x = q_ref[:, cols(h, dim)].astype(F32)
+        rstd = rms(x)
+        hat = x * rstd
+        back = acc[:dim, cols(h, rows)].T.astype(BF16).astype(F32) * (qgain_ref[...] * scale)
+        mean = jnp.mean(back * hat, axis=-1, keepdims=True)
+        qgrad_ref[:, cols(h, dim)] = (rstd * (back - hat * mean)).astype(BF16)
+
+
 def add_kernel(a_ref, b_ref, o_ref):
     o_ref[...] = (a_ref[...].astype(F32) + b_ref[...].astype(F32)).astype(BF16)
 
 
-def settle_kernel(heads, keep_ref, got_ref, total_ref, gain_ref):
+def settle_kernel(heads, keep_ref, got_ref, a_ref, b_ref, total_ref, gain_ref):
     total_ref[...] = keep_ref[...] + got_ref[...]
-    gain_ref[...] = total_ref[heads : heads + 1, :]
+    gain_ref[...] = total_ref[heads : heads + 1, :] + a_ref[...] + b_ref[...]
 
 
 def pair_kernel(a_ref, b_ref, o_ref):
     o_ref[...] = a_ref[...] + b_ref[...]
 
 
-def spread_kernel(heads, total_ref, a_ref, b_ref, *outs):
-    gain = a_ref[...] + b_ref[...]
+def spread_kernel(heads, total_ref, gain_ref, *outs):
     for s, out in enumerate(outs):
         rows = total_ref[8 * s : 8 * s + 8, :]
-        out[...] = jnp.where(iota(rows.shape, 0) == heads, gain, rows)
-
-
-def finish_kernel(half, k_ref, logit_ref, gain_ref, *refs):
-    piece_refs = refs[half:-4]
-    kgrad_ref, vgrad_ref, fgrad_ref, gains_ref = refs[-4:]
+        out[...] = jnp.where(iota(rows.shape, 0) == heads, gain_ref[...], rows)
+
+
+def finish_kernel(k_ref, gain_ref, *refs):
+    piece_refs = refs[:-2]
+    kgrad_ref, vgrad_ref = refs[-2:]
     dim = k_ref.shape[1]
-    heads = logit_ref.shape[0]
-    small = refs[0][...]
-    for ref in refs[1:half]:
-        small = small + ref[...]
-    row = small[heads : heads + 1]
-    gains_ref[...] = jnp.concatenate([row[:, :dim], row[:, dim:]], axis=0)
     total = piece_refs[0][...].astype(F32)
     for ref in piece_refs[1:]:
         total = total + ref[...].astype(F32)
@@ -480,8 +466,20 @@
     back = total[:dim].T * gain_ref[...]
     mean = jnp.mean(back * hat, axis=-1, keepdims=True)
     kgrad_ref[...] = (rstd * (back - hat * mean)).astype(BF16)
+
+
+def forget_kernel(logit_ref, *refs):
+    small_refs = refs[:-2]
+    fgrad_ref, gains_ref = refs[-2:]
+    heads = logit_ref.shape[0]
+    small = small_refs[0][...]
+    for ref in small_refs[1:]:
+        small = small + ref[...]
     logit = logit_ref[...].astype(F32)
     fgrad_ref[...] = small[:heads] * (1.0 / (1.0 + jnp.exp(logit)))
+    row = small[heads : heads + 1]
+    dim = row.shape[1] // 2
+    gains_ref[...] = jnp.concatenate([row[:, :dim], row[:, dim:]], axis=0)
 
 
 def whole_step(queries, key_vectors, values, forget_logit, out_grad, query_gain, key_gain, lengths):
@@ -511,10 +509,11 @@
         near(inputs), far=5,
     )
     blocks = {0: own}
-    for k in range(n - 2, 0, -2):
+    gather_order = [2] + list(range(n - 2, 2, -2))
+    for k in gather_order:
         blocks[k] = swap(own, "seq", k)
     blocks[1] = swap(own, "seq", 1)
-    for k in range(n - 2, 0, -2):
+    for k in gather_order:
         blocks[k + 1] = swap(blocks[k], "seq", 1)
 
     qt, gt, acc, w0, kt0 = kernel_call(
@@ -556,63 +555,52 @@
     )
     attention, acc, between, log_total, inner, gate_odd, key_acc = results[:7]
     odd = results[7:]
-    across = [swap(odd[s], "seq", 1) for s in range(half)]
-
-    top = list(range(half - 1, half // 2 - 1, -1))
-    bottom = list(range(half // 2 - 1, -1, -1))
+    order = list(range(half - 1, 0, -1))
+    across = {s: swap(odd[s], "seq", 1) for s in order + [0]}
+
     results = kernel_call(
-        functools.partial(late_a_kernel, rows, top),
-        [low, qt, gt, acc, between, log_total, inner, key_acc, w1, kt1]
-        + [blocks[2 * s] for s in top],
-        (state, key_sum, struct(len(top), 8, rows, dtype=F32)) + (piece,) * len(top),
-        [wide_scratch, wide_scratch],
-        flops=4 * len(top) * matmul,
-    )
-    acc, key_acc, gate_top = results[:3]
-    even = dict(zip(top, results[3:]))
-    results = kernel_call(
-        functools.partial(late_b_kernel, n, bottom, top),
-        [low, query, qgain, kgain, qt, gt, acc, between, log_total, inner, key_acc]
-        + [w0, kt0, w1, kt1, gate_odd, gate_top]
-        + [blocks[2 * s] for s in bottom],
-        (struct(rows, full),)
-        + (struct(8 * half, rows, dtype=F32),) * 2
-        + (piece,) * len(bottom),
-        [
-            pltpu.VMEM((tall, wide), F32),
-            pltpu.VMEM((dim, rows), F32),
-            wide_scratch,
-            wide_scratch,
-            pltpu.VMEM((n, 8, rows), F32),
-        ],
-        flops=4 * len(bottom) * matmul,
-    )
-    query_grad, keep, give = results[:3]
-    even.update(zip(bottom, results[3:]))
-
+        functools.partial(late_kernel, n),
+        [low, kgain, qgain, qt, gt, acc, between, log_total, inner, key_acc]
+        + [w0, kt0, w1, kt1, gate_odd]
+        + [blocks[2 * s] for s in range(half)],
+        (
+            state, struct(8 * half, rows, dtype=F32), struct(8 * half, rows, dtype=F32),
+            struct(1, width, dtype=F32),
+        )
+        + (piece,) * half,
+        [pltpu.VMEM((dim, rows), F32), wide_scratch, wide_scratch, pltpu.VMEM((n, 8, rows), F32)],
+        flops=4 * half * matmul,
+    )
+    acc, keep, give, gain = results[:4]
+    even = results[4:]
+
+    gain_line = struct(1, width, dtype=F32)
+    eight = struct(8, rows, dtype=F32)
+    got = swap(give, "seq", 1)
+    near_gain = swap(gain, "rep", 1)
+    far_gain = swap_both(gain, lax.axis_size("rep") + 1)
+    query_grad = kernel_call(query_kernel, [query, qgain, acc], struct(rows, full), flops=matmul)
     arrived = [even[0], across[0]]
-    for s in range(half - 1, 0, -1):
+    for s in order:
         both = kernel_call(add_kernel, [even[s], across[s]], piece)
         arrived.append(swap(both, "seq", 2 * s))
 
-    gain_line = struct(1, width, dtype=F32)
-    eight = struct(8, rows, dtype=F32)
     total, gain = kernel_call(
-        functools.partial(settle_kernel, heads), [keep, swap(give, "seq", 1)],
+        functools.partial(settle_kernel, heads), [keep, got, near_gain, far_gain],
         (struct(8 * half, rows, dtype=F32), gain_line),
     )
-    bit = 1
-    while 2 * bit < lax.axis_size("rep"):
+    bit = 2
+    while bit < lax.axis_size("rep"):
         gain = kernel_call(pair_kernel, [gain, swap(gain, "rep", bit)], gain_line)
         bit *= 2
-    smalls = kernel_call(
-        functools.partial(spread_kernel, heads),
-        [total, gain, swap(gain, "rep", bit)], (eight,) * half,
-    )
+    smalls = kernel_call(functools.partial(spread_kernel, heads), [total, gain], (eight,) * half)
     smalls = [smalls[0]] + [swap(smalls[s], "seq", 2 * s) for s in range(1, half)]
-    key_grad, value_grad, forget_grad, gains = kernel_call(
-        functools.partial(finish_kernel, half), [key, logit, kgain] + smalls + arrived,
-        (struct(rows, dim), struct(rows, dim), head_row, struct(2, dim, dtype=F32)),
+    key_grad, value_grad = kernel_call(
+        finish_kernel, [key, kgain] + arrived, (struct(rows, dim), struct(rows, dim)),
+        flops=matmul,
+    )
+    forget_grad, gains = kernel_call(
+        forget_kernel, [logit] + smalls, (head_row, struct(2, dim, dtype=F32))
     )
     return (
         attention[None],

time: 70.7 us -> 72.9 us (1.031)
  waiting for transfers between devices: 30.1 us -> 32.7 us
  starting transfers between devices: 31.4 us -> 30.2 us
  Pallas kernels: 8.12 us -> 8.96 us
    ppermute x0 -> x1, waiting for transfers between devices: none -> 3 us  [swap_both(): lax.ppermute(value, ('seq', 'rep'), [(i, i ^ bit) for i in range(count)])]
    ppermute x20, starting transfers between devices: 31.4 us -> 30.2 us  [swap(): return lax.ppermute(value, axis, [(i, i ^ bit) for i in range(count)])]
    pallas_call x13 -> x14, Pallas kernels: 8.12 us -> 8.96 us  [kernel_call(): pl.pallas_call(kernel, out_shape=outs, in_specs=in_specs, out_specs=jax.t...]
  transfers between devices with their start and end apart: 20 -> 21, of which waited for: 11 -> 12; matrix products, arithmetic and copies ran while one was open for 0% -> 0% of each run, Pallas kernels for 7% -> 8%
where the time goes in v1:
time: 72.9 us; the launch traced here: 72.7 us
  waiting for transfers between devices  32.7 us (45%)
  starting transfers between devices  30.2 us (41%)
  Pallas kernels  8.96 us (12%)
  between operations  0.76 us (1%)
    ppermute x20, starting transfers between devices, swap(): return lax.ppermute(value, axis, [(i, i ^ bit) for i in range(count)])  30.2 us
    ppermute x20, waiting for transfers between devices, swap(): return lax.ppermute(value, axis, [(i, i ^ bit) for i in range(count)])  29.7 us
    pallas_call x14, Pallas kernels, kernel_call(): pl.pallas_call(kernel, out_shape=outs, in_specs=in_specs, out_specs=jax.t...  8.96 us
    ppermute x1, waiting for transfers between devices, swap_both(): lax.ppermute(value, ('seq', 'rep'), [(i, i ^ bit) for i in range(count)])  3 us
  transfers between devices with their start and end apart: 21, of which 12 were waited for; matrix products, arithmetic and copies ran while one was open for 0% of the time, Pallas kernels for 8%

profile of v1, /device:TPU:0, one launch (start us, length us, event | category | flops | bytes accessed | tf_op | source)
XLA Modules:
  0.0 72.7 jit_solution(1992253577010385226)
XLA Ops:
  0.6 1.2 %shard_map.127 = (bf16[288,256]{1,0:T(8,128)(2,1)S(1)}, bf16[32,256]{1,0:T(8,128)(2,1)S(1)}, s32[8,128]{1,0:T(8,128)S(1)}) custom-call(s32[1,4]{1,0:T(1,128)} %refs_0_.1, bf16[256,128]{1,0:T(8,128)(2,1)} %bitcast.12, bf16[256,128]{1,0:T(8,128)(2,1)} %bitcast.25, bf16[4,256]{1,0:T(4,128)(2,1)} %bitcast.16, f32[1,128]{1,0:T(1,128)} %bitcast.18), custom_call_target="tpu_custom_call" | custom-call | flops 1048576 | bytes 1048576 | tf_op jit(solution)/shard_map/pallas_call | solution.py:43
  1.8 5.1 %collective-permute-start.3 = (bf16[288,256]{1,0:T(8,128)(2,1)S(1)}, bf16[288,256]{1,0:T(8,128)(2,1)S(1)}, u32[]{:S(2)}, u32[]{:S(2)}) collective-permute-start(bf16[288,256]{1,0:T(8,128)(2,1)S(1)} %get-tuple-element.47.refs_3_.refs_0_.refs_12_), channel_id=1, source_target_pairs={{0,24},{4,28},{8,16},{12,20},{16,8},{20,12},{24,0},{28,4},{1,25},{... | collective-permute-start | bytes 442376 | tf_op jit(solution)/shard_map/ppermute | solution.py:25
  7.0 0.0 collective-permute-start.2
  7.0 0.6 collective-permute-start.1
  7.6 1.7 %collective-permute-start = (bf16[288,256]{1,0:T(8,128)(2,1)S(1)}, bf16[288,256]{1,0:T(8,128)(2,1)S(1)}, u32[]{:S(2)}, u32[]{:S(2)}) collective-permute-start(bf16[288,256]{1,0:T(8,128)(2,1)S(1)} %get-tuple-element.47.refs_3_.refs_0_.refs_12_), channel_id=1, source_target_pairs={{0,4},{4,0},{8,12},{12,8},{16,20},{20,16},{24,28},{28,24},{1,5},{5... | collective-permute-start | bytes 442376 | tf_op jit(solution)/shard_map/ppermute | solution.py:25
  9.3 2.5 %collective-permute-done.3.refs_3_.refs_6_.refs_15_ = bf16[288,256]{1,0:T(8,128)(2,1)S(1)} collective-permute-done((bf16[288,256]{1,0:T(8,128)(2,1)S(1)}, bf16[288,256]{1,0:T(8,128)(2,1)S(1)}, u32[]{:S(2)}, u32[]{:S(2)}) %collective-permute-start.3) | collective-permute-done | bytes 147488 | tf_op jit(solution)/shard_map/ppermute | solution.py:25
  11.8 1.7 %collective-permute-start.6 = (bf16[288,256]{1,0:T(8,128)(2,1)S(1)}, bf16[288,256]{1,0:T(8,128)(2,1)S(1)}, u32[]{:S(2)}, u32[]{:S(2)}) collective-permute-start(bf16[288,256]{1,0:T(8,128)(2,1)S(1)} %collective-permute-done.3.refs_3_.refs_6_.refs_15_), channel_id=1, source_target_pairs={{0,4},{4,0},{8,12},{12,8},{16,20},{20,16},{24,28},{28,24},{1,5},{5... | collective-permute-start | bytes 442376 | tf_op jit(solution)/shard_map/ppermute | solution.py:25
  13.5 6.0 %collective-permute-done.2.refs_2_.refs_4_.refs_14_ = bf16[288,256]{1,0:T(8,128)(2,1)S(1)} collective-permute-done((bf16[288,256]{1,0:T(8,128)(2,1)S(1)}, bf16[288,256]{1,0:T(8,128)(2,1)S(1)}, u32[]{:S(2)}, u32[]{:S(2)}) %collective-permute-start.2) | collective-permute-done | bytes 147488 | tf_op jit(solution)/shard_map/ppermute | solution.py:25
  19.4 1.5 %collective-permute-start.5 = (bf16[288,256]{1,0:T(8,128)(2,1)S(1)}, bf16[288,256]{1,0:T(8,128)(2,1)S(1)}, u32[]{:S(2)}, u32[]{:S(2)}) collective-permute-start(bf16[288,256]{1,0:T(8,128)(2,1)S(1)} %collective-permute-done.2.refs_2_.refs_4_.refs_14_), channel_id=1, source_target_pairs={{0,4},{4,0},{8,12},{12,8},{16,20},{20,16},{24,28},{28,24},{1,5},{5... | collective-permute-start | bytes 442376 | tf_op jit(solution)/shard_map/ppermute | solution.py:25
  21.0 0.0 collective-permute-done.1.refs_1_.refs_2_.refs_13_
  21.0 0.5 collective-permute-start.4
  21.5 2.0 %shard_map.128 = (bf16[256,1024]{1,0:T(8,128)(2,1)S(1)}, bf16[128,1024]{1,0:T(8,128)(2,1)S(1)}, f32[144,1024]{1,0:T(8,128)S(1)}, bf16[256,1024]{1,0:T(8,128)(2,1)S(1)}, bf16[144,256]{1,0:T(8,128)(2,1)S(1)}) custom-call(bf16[256,512]{1,0:T(8,128)(2,1)} %bitcast.14, bf16[256,512]{1,0:T(8,128)(2,1)} %bitcast.26, f32[1,128]{1,0:T(1,128)} %bitcast.21, ...), custom_call_target="tpu_custom_call" | custom-call | flops 268435456 | bytes 1048576 | tf_op jit(solution)/shard_map/pallas_call | solution.py:43
  23.5 0.0 collective-permute-done.refs_0_.refs_1_
  23.5 0.1 shard_map.129
  23.6 0.0 collective-permute-done.6.refs_7_
  23.6 2.4 %collective-permute-done.5.refs_5_ = bf16[288,256]{1,0:T(8,128)(2,1)S(1)} collective-permute-done((bf16[288,256]{1,0:T(8,128)(2,1)S(1)}, bf16[288,256]{1,0:T(8,128)(2,1)S(1)}, u32[]{:S(2)}, u32[]{:S(2)}) %collective-permute-start.5) | collective-permute-done | bytes 147488 | tf_op jit(solution)/shard_map/ppermute | solution.py:25
  25.9 1.6 %collective-permute-done.4.refs_3_ = bf16[288,256]{1,0:T(8,128)(2,1)S(1)} collective-permute-done((bf16[288,256]{1,0:T(8,128)(2,1)S(1)}, bf16[288,256]{1,0:T(8,128)(2,1)S(1)}, u32[]{:S(2)}, u32[]{:S(2)}) %collective-permute-start.4) | collective-permute-done | bytes 147488 | tf_op jit(solution)/shard_map/ppermute | solution.py:25
  27.5 0.0 copy-start.3
  27.5 0.0 copy-start.4
  27.5 1.3 %shard_map.130 = (bf16[256,512]{1,0:T(8,128)(2,1)}, f32[144,1024]{1,0:T(8,128)S(1)}, f32[8,1,1024]{2,1,0:T(1,128)S(1)}, f32[1,1024]{1,0:T(1,128)S(1)}, f32[1,102...) custom-call(s32[8,128]{1,0:T(8,128)S(1)} %get-tuple-element.46.low_r, ...), custom_call_target="tpu_custom_call" | custom-call | flops 3221225472 | bytes 1048576 | tf_op jit(solution)/shard_map/pallas_call | solution.py:43
  28.8 2.4 %collective-permute-start.7 = (bf16[256,256]{1,0:T(8,128)(2,1)S(1)}, bf16[256,256]{1,0:T(8,128)(2,1)S(1)}, u32[]{:S(2)}, u32[]{:S(2)}) collective-permute-start(bf16[256,256]{1,0:T(8,128)(2,1)S(1)} %get-tuple-element.66), channel_id=1, source_target_pairs={{0,4},{4,0},{8,12},{12,8},{16,20},{20,16},{24,28},{28,24},{1,5},{5... | collective-permute-start | bytes 393224 | tf_op jit(solution)/shard_map/ppermute | solution.py:25
  31.2 0.0 collective-permute-start.8
  31.3 2.0 %collective-permute-start.10 = (bf16[256,256]{1,0:T(8,128)(2,1)S(1)}, bf16[256,256]{1,0:T(8,128)(2,1)S(1)}, u32[]{:S(2)}, u32[]{:S(2)}) collective-permute-start(bf16[256,256]{1,0:T(8,128)(2,1)S(1)} %get-tuple-element.70), channel_id=1, source_target_pairs={{0,4},{4,0},{8,12},{12,8},{16,20},{20,16},{24,28},{28,24},{1,5},{5... | collective-permute-start | bytes 393224 | tf_op jit(solution)/shard_map/ppermute | solution.py:25
  33.3 0.0 collective-permute-start.12
  33.3 0.0 copy-done.3
  33.3 0.0 copy-done.4
  33.3 0.0 copy-start.1
  33.3 1.3 %shard_map.131 = (f32[144,1024]{1,0:T(8,128)S(1)}, f32[32,256]{1,0:T(8,128)S(1)}, f32[32,256]{1,0:T(8,128)S(1)}, f32[1,256]{1,0:T(1,128)S(1)}, bf16[256,256]{1,0...) custom-call(s32[8,128]{1,0:T(8,128)S(1)} %get-tuple-element.46.low_ref,, ...), custom_call_target="tpu_custom_call" | custom-call | flops 2147483648 | bytes 1048576 | tf_op jit(solution)/shard_map/pallas_call | solution.py:43
  34.6 0.0 copy-start.2
  34.6 0.0 copy-start
  34.6 3.8 %collective-permute-done.8.b_ref = bf16[256,256]{1,0:T(8,128)(2,1)S(1)} collective-permute-done((bf16[256,256]{1,0:T(8,128)(2,1)S(1)}, bf16[256,256]{1,0:T(8,128)(2,1)S(1)}, u32[]{:S(2)}, u32[]{:S(2)}) %collective-permute-start.8) | collective-permute-done | bytes 131104 | tf_op jit(solution)/shard_map/ppermute | solution.py:25
  38.4 5.2 %collective-permute-start.9 = (bf16[256,256]{1,0:T(8,128)(2,1)S(1)}, bf16[256,256]{1,0:T(8,128)(2,1)S(1)}, u32[]{:S(2)}, u32[]{:S(2)}) collective-permute-start(bf16[256,256]{1,0:T(8,128)(2,1)S(1)} %shard_map.133), channel_id=1, source_target_pairs={{0,24},{4,28},{8,16},{12,20},{16,8},{20,12},{24,0},{28,4},{1,25},{... | collective-permute-start | bytes 393224 | tf_op jit(solution)/shard_map/ppermute | solution.py:25
  43.6 0.0 collective-permute-done.10.b_ref
  43.7 0.1 collective-permute-start.11
  43.7 0.0 collective-permute-done.12.b_ref
  43.8 0.6 collective-permute-start.13
  44.4 0.0 collective-permute-start.16
  44.4 3.0 %collective-permute-done.16.b_ref = f32[1,256]{1,0:T(1,128)S(1)} collective-permute-done((f32[1,256]{1,0:T(1,128)S(1)}, f32[1,256]{1,0:T(1,128)S(1)}, u32[]{:S(2)}, u32[]{:S(2)}) %collective-permute-start.16) | collective-permute-done | bytes 1056 | tf_op jit(solution)/shard_map/ppermute | solution.py:30
  47.4 0.0 collective-permute-start.15
  47.4 1.2 %collective-permute-done.15.a_ref = f32[1,256]{1,0:T(1,128)S(1)} collective-permute-done((f32[1,256]{1,0:T(1,128)S(1)}, f32[1,256]{1,0:T(1,128)S(1)}, u32[]{:S(2)}, u32[]{:S(2)}) %collective-permute-start.15) | collective-permute-done | bytes 1056 | tf_op jit(solution)/shard_map/ppermute | solution.py:25
  48.6 1.2 %collective-permute-start.14 = (f32[32,256]{1,0:T(8,128)S(1)}, f32[32,256]{1,0:T(8,128)S(1)}, u32[]{:S(2)}, u32[]{:S(2)}) collective-permute-start(f32[32,256]{1,0:T(8,128)S(1)} %get-tuple-element.76), channel_id=1, source_target_pairs={{0,4},{4,0},{8,12},{12,8},{16,20},{20,16},{24,28},{28,24},{1,5},{5... | collective-permute-start | bytes 98312 | tf_op jit(solution)/shard_map/ppermute | solution.py:25
  49.8 2.7 %collective-permute-done.14.got_ref = f32[32,256]{1,0:T(8,128)S(1)} collective-permute-done((f32[32,256]{1,0:T(8,128)S(1)}, f32[32,256]{1,0:T(8,128)S(1)}, u32[]{:S(2)}, u32[]{:S(2)}) %collective-permute-start.14) | collective-permute-done | bytes 32800 | tf_op jit(solution)/shard_map/ppermute | solution.py:25
  52.5 3.3 %collective-permute-start.17 = (f32[1,256]{1,0:T(1,128)S(1)}, f32[1,256]{1,0:T(1,128)S(1)}, u32[]{:S(2)}, u32[]{:S(2)}) collective-permute-start(f32[1,256]{1,0:T(1,128)S(1)} %get-tuple-element.79.a_ref), channel_id=1, source_target_pairs={{0,2},{1,3},{2,0},{3,1},{4,6},{5,7},{6,4},{7,5},{8,10},{9,11},{10,... | collective-permute-start | bytes 3080 | tf_op jit(solution)/shard_map/ppermute | solution.py:25
  55.8 1.6 %collective-permute-done.17.b_ref = f32[1,256]{1,0:T(1,128)S(1)} collective-permute-done((f32[1,256]{1,0:T(1,128)S(1)}, f32[1,256]{1,0:T(1,128)S(1)}, u32[]{:S(2)}, u32[]{:S(2)}) %collective-permute-start.17) | collective-permute-done | bytes 1056 | tf_op jit(solution)/shard_map/ppermute | solution.py:25
  57.4 0.3 collective-permute-start.18
  57.7 3.4 %collective-permute-done.18.refs_1_ = f32[8,256]{1,0:T(8,128)S(1)} collective-permute-done((f32[8,256]{1,0:T(8,128)S(1)}, f32[8,256]{1,0:T(8,128)S(1)}, u32[]{:S(2)}, u32[]{:S(2)}) %collective-permute-start.18) | collective-permute-done | bytes 8224 | tf_op jit(solution)/shard_map/ppermute | solution.py:25
  61.1 1.3 %collective-permute-start.19 = (f32[8,256]{1,0:T(8,128)S(1)}, f32[8,256]{1,0:T(8,128)S(1)}, u32[]{:S(2)}, u32[]{:S(2)}) collective-permute-start(f32[8,256]{1,0:T(8,128)S(1)} %get-tuple-element.82), channel_id=1, source_target_pairs={{0,16},{4,20},{8,24},{12,28},{16,0},{20,4},{24,8},{28,12},{1,17},{... | collective-permute-start | bytes 24584 | tf_op jit(solution)/shard_map/ppermute | solution.py:25
  62.4 3.2 %collective-permute-done.19.refs_2_ = f32[8,256]{1,0:T(8,128)S(1)} collective-permute-done((f32[8,256]{1,0:T(8,128)S(1)}, f32[8,256]{1,0:T(8,128)S(1)}, u32[]{:S(2)}, u32[]{:S(2)}) %collective-permute-start.19) | collective-permute-done | bytes 8224 | tf_op jit(solution)/shard_map/ppermute | solution.py:25
  65.6 2.6 %collective-permute-start.20 = (f32[8,256]{1,0:T(8,128)S(1)}, f32[8,256]{1,0:T(8,128)S(1)}, u32[]{:S(2)}, u32[]{:S(2)}) collective-permute-start(f32[8,256]{1,0:T(8,128)S(1)} %get-tuple-element.83), channel_id=1, source_target_pairs={{0,24},{4,28},{8,16},{12,20},{16,8},{20,12},{24,0},{28,4},{1,25},{... | collective-permute-start | bytes 24584 | tf_op jit(solution)/shard_map/ppermute | solution.py:25
  68.2 0.0 copy-done.1
  68.2 1.5 %shard_map.132 = bf16[256,512]{1,0:T(8,128)(2,1)} custom-call(bf16[256,512]{1,0:T(8,128)(2,1)S(1)} %bitcast.15, f32[1,128]{1,0:T(1,128)S(1)} %bitcast.23, f32[144,1024]{1,0:T(8,128)S(1)} %get-tuple-element.64.acc), custom_call_target="tpu_custom_call" | custom-call | flops 134217728 | bytes 1048576 | tf_op jit(solution)/shard_map/pallas_call | solution.py:43
  69.7 1.4 %collective-permute-done.20.refs_3_ = f32[8,256]{1,0:T(8,128)S(1)} collective-permute-done((f32[8,256]{1,0:T(8,128)S(1)}, f32[8,256]{1,0:T(8,128)S(1)}, u32[]{:S(2)}, u32[]{:S(2)}) %collective-permute-start.20) | collective-permute-done | bytes 8224 | tf_op jit(solution)/shard_map/ppermute | solution.py:25
  71.1 0.0 copy-done.2
  71.1 0.6 shard_map.140
  71.7 0.0 collective-permute-done.7.refs_1_
  71.7 0.0 collective-permute-done.9.refs_2_
  71.7 0.0 collective-permute-done.11.refs_3_
  71.7 0.0 collective-permute-done.13.refs_4_
  71.7 0.0 copy-done
  71.7 0.9 %shard_map.136 = (bf16[256,128]{1,0:T(8,128)(2,1)}, bf16[256,128]{1,0:T(8,128)(2,1)}) custom-call(bf16[256,128]{1,0:T(8,128)(2,1)S(1)} %bitcast.13, f32[1,128]{1,0:T(1,128)S(1)} %bitcast.20, bf16[256,256]{1,0:T(8,128)(2,1)S(1)} %get-tuple-element.65.refs_0_, bf16[256,256]{1,0:T(8,128)(2,1)S(1)} %collective-permute-done.7.refs_1_, ...), custom_call_target="tpu_custom_call" | custom-call | flops 134217728 | bytes 1048576 | tf_op jit(solution)/shard_map/pallas_call | solution.py:43
  (6 shorter events, 0.1 us)
Async XLA Ops:
  1.8 9.9 %collective-permute-start.3 = (bf16[288,256]{1,0:T(8,128)(2,1)S(1)}, bf16[288,256]{1,0:T(8,128)(2,1)S(1)}, u32[]{:S(2)}, u32[]{:S(2)}) collective-permute-start(bf16[288,256]{1,0:T(8,128)(2,1)S(1)} %get-tuple-element.47.refs_3_.refs_0_.refs_12_), channel_id=1, source_target_pairs={{0,24},{4,28},{8,16},{12,20},{16,8},{20,12},{24,0},{28,4},{1,25},{... | collective-permute-start | bytes 442376 | tf_op jit(solution)/shard_map/ppermute | solution.py:25
  7.0 12.5 %collective-permute-start.2 = (bf16[288,256]{1,0:T(8,128)(2,1)S(1)}, bf16[288,256]{1,0:T(8,128)(2,1)S(1)}, u32[]{:S(2)}, u32[]{:S(2)}) collective-permute-start(bf16[288,256]{1,0:T(8,128)(2,1)S(1)} %get-tuple-element.47.refs_3_.refs_0_.refs_12_), channel_id=1, source_target_pairs={{0,16},{4,20},{8,24},{12,28},{16,0},{20,4},{24,8},{28,12},{1,17},{... | collective-permute-start | bytes 442376 | tf_op jit(solution)/shard_map/ppermute | solution.py:25
  7.0 14.0 %collective-permute-start.1 = (bf16[288,256]{1,0:T(8,128)(2,1)S(1)}, bf16[288,256]{1,0:T(8,128)(2,1)S(1)}, u32[]{:S(2)}, u32[]{:S(2)}) collective-permute-start(bf16[288,256]{1,0:T(8,128)(2,1)S(1)} %get-tuple-element.47.refs_3_.refs_0_.refs_12_), channel_id=1, source_target_pairs={{0,8},{4,12},{8,0},{12,4},{16,24},{20,28},{24,16},{28,20},{1,9},{5... | collective-permute-start | bytes 442376 | tf_op jit(solution)/shard_map/ppermute | solution.py:25
  7.6 15.9 %collective-permute-start = (bf16[288,256]{1,0:T(8,128)(2,1)S(1)}, bf16[288,256]{1,0:T(8,128)(2,1)S(1)}, u32[]{:S(2)}, u32[]{:S(2)}) collective-permute-start(bf16[288,256]{1,0:T(8,128)(2,1)S(1)} %get-tuple-element.47.refs_3_.refs_0_.refs_12_), channel_id=1, source_target_pairs={{0,4},{4,0},{8,12},{12,8},{16,20},{20,16},{24,28},{28,24},{1,5},{5... | collective-permute-start | bytes 442376 | tf_op jit(solution)/shard_map/ppermute | solution.py:25
  11.8 11.8 %collective-permute-start.6 = (bf16[288,256]{1,0:T(8,128)(2,1)S(1)}, bf16[288,256]{1,0:T(8,128)(2,1)S(1)}, u32[]{:S(2)}, u32[]{:S(2)}) collective-permute-start(bf16[288,256]{1,0:T(8,128)(2,1)S(1)} %collective-permute-done.3.refs_3_.refs_6_.refs_15_), channel_id=1, source_target_pairs={{0,4},{4,0},{8,12},{12,8},{16,20},{20,16},{24,28},{28,24},{1,5},{5... | collective-permute-start | bytes 442376 | tf_op jit(solution)/shard_map/ppermute | solution.py:25
  19.4 6.5 %collective-permute-start.5 = (bf16[288,256]{1,0:T(8,128)(2,1)S(1)}, bf16[288,256]{1,0:T(8,128)(2,1)S(1)}, u32[]{:S(2)}, u32[]{:S(2)}) collective-permute-start(bf16[288,256]{1,0:T(8,128)(2,1)S(1)} %collective-permute-done.2.refs_2_.refs_4_.refs_14_), channel_id=1, source_target_pairs={{0,4},{4,0},{8,12},{12,8},{16,20},{20,16},{24,28},{28,24},{1,5},{5... | collective-permute-start | bytes 442376 | tf_op jit(solution)/shard_map/ppermute | solution.py:25
  21.0 6.6 %collective-permute-start.4 = (bf16[288,256]{1,0:T(8,128)(2,1)S(1)}, bf16[288,256]{1,0:T(8,128)(2,1)S(1)}, u32[]{:S(2)}, u32[]{:S(2)}) collective-permute-start(bf16[288,256]{1,0:T(8,128)(2,1)S(1)} %collective-permute-done.1.refs_1_.refs_2_.refs_13_), channel_id=1, source_target_pairs={{0,4},{4,0},{8,12},{12,8},{16,20},{20,16},{24,28},{28,24},{1,5},{5... | collective-permute-start | bytes 442376 | tf_op jit(solution)/shard_map/ppermute | solution.py:25
  27.5 5.8 %copy-start.3 = (f32[128]{0:T(128)S(1)}, f32[128]{0:T(128)}, u32[]{:S(2)}) copy-start(f32[128]{0:T(128)} %param.14) | copy-start | bytes 1540
  27.5 5.8 %copy-start.4 = (f32[128]{0:T(128)S(1)}, f32[128]{0:T(128)}, u32[]{:S(2)}) copy-start(f32[128]{0:T(128)} %param.13) | copy-start | bytes 1540
  28.8 42.9 %collective-permute-start.7 = (bf16[256,256]{1,0:T(8,128)(2,1)S(1)}, bf16[256,256]{1,0:T(8,128)(2,1)S(1)}, u32[]{:S(2)}, u32[]{:S(2)}) collective-permute-start(bf16[256,256]{1,0:T(8,128)(2,1)S(1)} %get-tuple-element.66), channel_id=1, source_target_pairs={{0,4},{4,0},{8,12},{12,8},{16,20},{20,16},{24,28},{28,24},{1,5},{5... | collective-permute-start | bytes 393224 | tf_op jit(solution)/shard_map/ppermute | solution.py:25
  31.2 7.2 %collective-permute-start.8 = (bf16[256,256]{1,0:T(8,128)(2,1)S(1)}, bf16[256,256]{1,0:T(8,128)(2,1)S(1)}, u32[]{:S(2)}, u32[]{:S(2)}) collective-permute-start(bf16[256,256]{1,0:T(8,128)(2,1)S(1)} %get-tuple-element.68), channel_id=1, source_target_pairs={{0,4},{4,0},{8,12},{12,8},{16,20},{20,16},{24,28},{28,24},{1,5},{5... | collective-permute-start | bytes 393224 | tf_op jit(solution)/shard_map/ppermute | solution.py:25
  31.3 12.4 %collective-permute-start.10 = (bf16[256,256]{1,0:T(8,128)(2,1)S(1)}, bf16[256,256]{1,0:T(8,128)(2,1)S(1)}, u32[]{:S(2)}, u32[]{:S(2)}) collective-permute-start(bf16[256,256]{1,0:T(8,128)(2,1)S(1)} %get-tuple-element.70), channel_id=1, source_target_pairs={{0,4},{4,0},{8,12},{12,8},{16,20},{20,16},{24,28},{28,24},{1,5},{5... | collective-permute-start | bytes 393224 | tf_op jit(solution)/shard_map/ppermute | solution.py:25
  33.3 10.5 %collective-permute-start.12 = (bf16[256,256]{1,0:T(8,128)(2,1)S(1)}, bf16[256,256]{1,0:T(8,128)(2,1)S(1)}, u32[]{:S(2)}, u32[]{:S(2)}) collective-permute-start(bf16[256,256]{1,0:T(8,128)(2,1)S(1)} %get-tuple-element.72), channel_id=1, source_target_pairs={{0,4},{4,0},{8,12},{12,8},{16,20},{20,16},{24,28},{28,24},{1,5},{5... | collective-permute-start | bytes 393224 | tf_op jit(solution)/shard_map/ppermute | solution.py:25
  33.3 34.9 %copy-start.1 = (bf16[1,256,512]{2,1,0:T(8,128)(2,1)S(1)}, bf16[1,256,512]{2,1,0:T(8,128)(2,1)}, u32[]{:S(2)}) copy-start(bf16[1,256,512]{2,1,0:T(8,128)(2,1)} %param.8) | copy-start | bytes 786436
  34.6 36.5 %copy-start.2 = (bf16[1,4,256]{2,1,0:T(4,128)(2,1)S(1)}, bf16[1,4,256]{2,1,0:T(4,128)(2,1)}, u32[]{:S(2)}) copy-start(bf16[1,4,256]{2,1,0:T(4,128)(2,1)} %param.11) | copy-start | bytes 6148
  34.6 37.1 %copy-start = (bf16[1,256,128]{2,1,0:T(8,128)(2,1)S(1)}, bf16[1,256,128]{2,1,0:T(8,128)(2,1)}, u32[]{:S(2)}) copy-start(bf16[1,256,128]{2,1,0:T(8,128)(2,1)} %param.9) | copy-start | bytes 196612
  38.4 33.3 %collective-permute-start.9 = (bf16[256,256]{1,0:T(8,128)(2,1)S(1)}, bf16[256,256]{1,0:T(8,128)(2,1)S(1)}, u32[]{:S(2)}, u32[]{:S(2)}) collective-permute-start(bf16[256,256]{1,0:T(8,128)(2,1)S(1)} %shard_map.133), channel_id=1, source_target_pairs={{0,24},{4,28},{8,16},{12,20},{16,8},{20,12},{24,0},{28,4},{1,25},{... | collective-permute-start | bytes 393224 | tf_op jit(solution)/shard_map/ppermute | solution.py:25
  43.7 28.0 %collective-permute-start.11 = (bf16[256,256]{1,0:T(8,128)(2,1)S(1)}, bf16[256,256]{1,0:T(8,128)(2,1)S(1)}, u32[]{:S(2)}, u32[]{:S(2)}) collective-permute-start(bf16[256,256]{1,0:T(8,128)(2,1)S(1)} %shard_map.134), channel_id=1, source_target_pairs={{0,16},{4,20},{8,24},{12,28},{16,0},{20,4},{24,8},{28,12},{1,17},{... | collective-permute-start | bytes 393224 | tf_op jit(solution)/shard_map/ppermute | solution.py:25
  43.8 27.9 %collective-permute-start.13 = (bf16[256,256]{1,0:T(8,128)(2,1)S(1)}, bf16[256,256]{1,0:T(8,128)(2,1)S(1)}, u32[]{:S(2)}, u32[]{:S(2)}) collective-permute-start(bf16[256,256]{1,0:T(8,128)(2,1)S(1)} %shard_map.135), channel_id=1, source_target_pairs={{0,8},{4,12},{8,0},{12,4},{16,24},{20,28},{24,16},{28,20},{1,9},{5... | collective-permute-start | bytes 393224 | tf_op jit(solution)/shard_map/ppermute | solution.py:25
  44.4 3.0 %collective-permute-start.16 = (f32[1,256]{1,0:T(1,128)S(1)}, f32[1,256]{1,0:T(1,128)S(1)}, u32[]{:S(2)}, u32[]{:S(2)}) collective-permute-start(f32[1,256]{1,0:T(1,128)S(1)} %get-tuple-element.77), channel_id=1, source_target_pairs={{0,5},{1,4},{2,7},{3,6},{4,1},{5,0},{6,3},{7,2},{8,13},{9,12},{10,... | collective-permute-start | bytes 3080 | tf_op jit(solution)/shard_map/ppermute | solution.py:30
  47.4 1.2 %collective-permute-start.15 = (f32[1,256]{1,0:T(1,128)S(1)}, f32[1,256]{1,0:T(1,128)S(1)}, u32[]{:S(2)}, u32[]{:S(2)}) collective-permute-start(f32[1,256]{1,0:T(1,128)S(1)} %get-tuple-element.77), channel_id=1, source_target_pairs={{0,1},{1,0},{2,3},{3,2},{4,5},{5,4},{6,7},{7,6},{8,9},{9,8},{10,11... | collective-permute-start | bytes 3080 | tf_op jit(solution)/shard_map/ppermute | solution.py:25
  48.6 3.9 %collective-permute-start.14 = (f32[32,256]{1,0:T(8,128)S(1)}, f32[32,256]{1,0:T(8,128)S(1)}, u32[]{:S(2)}, u32[]{:S(2)}) collective-permute-start(f32[32,256]{1,0:T(8,128)S(1)} %get-tuple-element.76), channel_id=1, source_target_pairs={{0,4},{4,0},{8,12},{12,8},{16,20},{20,16},{24,28},{28,24},{1,5},{5... | collective-permute-start | bytes 98312 | tf_op jit(solution)/shard_map/ppermute | solution.py:25
  52.5 4.8 %collective-permute-start.17 = (f32[1,256]{1,0:T(1,128)S(1)}, f32[1,256]{1,0:T(1,128)S(1)}, u32[]{:S(2)}, u32[]{:S(2)}) collective-permute-start(f32[1,256]{1,0:T(1,128)S(1)} %get-tuple-element.79.a_ref), channel_id=1, source_target_pairs={{0,2},{1,3},{2,0},{3,1},{4,6},{5,7},{6,4},{7,5},{8,10},{9,11},{10,... | collective-permute-start | bytes 3080 | tf_op jit(solution)/shard_map/ppermute | solution.py:25
  57.4 3.7 %collective-permute-start.18 = (f32[8,256]{1,0:T(8,128)S(1)}, f32[8,256]{1,0:T(8,128)S(1)}, u32[]{:S(2)}, u32[]{:S(2)}) collective-permute-start(f32[8,256]{1,0:T(8,128)S(1)} %get-tuple-element.81), channel_id=1, source_target_pairs={{0,8},{4,12},{8,0},{12,4},{16,24},{20,28},{24,16},{28,20},{1,9},{5... | collective-permute-start | bytes 24584 | tf_op jit(solution)/shard_map/ppermute | solution.py:25
  61.1 4.5 %collective-permute-start.19 = (f32[8,256]{1,0:T(8,128)S(1)}, f32[8,256]{1,0:T(8,128)S(1)}, u32[]{:S(2)}, u32[]{:S(2)}) collective-permute-start(f32[8,256]{1,0:T(8,128)S(1)} %get-tuple-element.82), channel_id=1, source_target_pairs={{0,16},{4,20},{8,24},{12,28},{16,0},{20,4},{24,8},{28,12},{1,17},{... | collective-permute-start | bytes 24584 | tf_op jit(solution)/shard_map/ppermute | solution.py:25
  65.6 5.4 %collective-permute-start.20 = (f32[8,256]{1,0:T(8,128)S(1)}, f32[8,256]{1,0:T(8,128)S(1)}, u32[]{:S(2)}, u32[]{:S(2)}) collective-permute-start(f32[8,256]{1,0:T(8,128)S(1)} %get-tuple-element.83), channel_id=1, source_target_pairs={{0,24},{4,28},{8,16},{12,20},{16,8},{20,12},{24,0},{28,4},{1,25},{... | collective-permute-start | bytes 24584 | tf_op jit(solution)/shard_map/ppermute | solution.py:25

commit v2 on v1

v2 whole, which is shorter than its diff:
```python
import functools

import jax
import jax.numpy as jnp
from jax import lax
from jax.experimental import pallas as pl
from jax.experimental.pallas import tpu as pltpu
from jax.sharding import PartitionSpec as P


TILE = 64
EPS = 1e-06
TAIL = 16
ONES = 16
CHUNK = 512
BIG = 1e30
F32 = jnp.float32
BF16 = jnp.bfloat16
VMEM = pl.BlockSpec(memory_space=pltpu.VMEM)
HBM = pl.BlockSpec(memory_space=pltpu.HBM)


def swap(value, axis, bit):
    count = lax.axis_size(axis)
    return lax.ppermute(value, axis, [(i, i ^ bit) for i in range(count)])


def struct(*shape, dtype=BF16):
    return jax.ShapeDtypeStruct(shape, dtype)


def kernel_call(kernel, operands, outs, scratch=(), limit=8 << 20, flops=1 << 20, far=0):
    in_specs = [HBM] * far + [VMEM] * (len(operands) - far)
    operands = [
        pltpu.with_memory_space_constraint(x, pltpu.HBM) if i < far else x
        for i, x in enumerate(operands)
    ]
    return pl.pallas_call(
        kernel,
        out_shape=outs,
        in_specs=in_specs,
        out_specs=jax.tree.map(lambda _: VMEM, outs),
        scratch_shapes=list(scratch),
        compiler_params=pltpu.CompilerParams(vmem_limit_bytes=limit),
        cost_estimate=pl.CostEstimate(flops=flops, bytes_accessed=1 << 20, transcendentals=0),
    )(*operands)


def dot_nn(a, b):
    return lax.dot_general(a, b, (((1,), (0,)), ((), ())), preferred_element_type=F32)


def dot_nt(a, b):
    return lax.dot_general(a, b, (((1,), (1,)), ((), ())), preferred_element_type=F32)


def iota(shape, axis):
    return lax.broadcasted_iota(jnp.int32, shape, axis)


def split3(x):
    hi = x.astype(BF16).astype(F32)
    rest = x - hi
    mid = rest.astype(BF16).astype(F32)
    return hi, mid, rest - mid


def rms(x):
    return lax.rsqrt(jnp.mean(x * x, axis=-1, keepdims=True) + EPS)


def flip(block):
    return block.astype(F32).T.astype(BF16)


def ones_where(count, test):
    shape = (count, count)
    return jnp.where(test(iota(shape, 0), iota(shape, 1)), 1.0, 0.0).astype(BF16)


def ones_rows(count):
    return jnp.where(iota((ONES, count), 0) == 0, 1.0, 0.0).astype(BF16)


def cols(h, rows):
    return slice(h * rows, (h + 1) * rows)


def chunks(wide):
    step = min(wide, CHUNK)
    return [slice(at, at + step) for at in range(0, wide, step)]


def lay_out(per_head):
    return jnp.concatenate([per_head[h : h + 1] for h in range(per_head.shape[0])], axis=1)


def log_sigmoid(x):
    small = jnp.exp(-jnp.abs(x))
    series = small * (1.0 - small * (0.5 - small * (1.0 / 3.0 - small * 0.25)))
    return jnp.minimum(x, 0.0) - jnp.where(small < 0.01, series, jnp.log(1.0 + small))


def bounds(len_ref, rows):
    me = lax.axis_index("seq")
    tiles = rows // TILE
    spans = []
    start = jnp.int32(0)
    begin = jnp.int32(0)
    for d in range(len_ref.shape[1]):
        end = start + len_ref[0, d]
        spans.append((start, end))
        begin = jnp.where(start <= me * tiles, start, begin)
        start = end
    return me, begin // tiles, spans


def first_block(low_ref):
    return lax.axis_index("seq"), low_ref[0, 0]


def is_active(me, low, k):
    b = me ^ k
    return (b <= me) & (b >= low)


def fetch(sources, targets, sem):
    copies = [pltpu.make_async_copy(*pair, sem.at[i]) for i, pair in enumerate(zip(sources, targets))]
    for copy in copies:
        copy.start()
    for copy in copies:
        copy.wait()


def near(operands):
    spaces = [pltpu.SMEM if x.dtype == jnp.int32 else pltpu.VMEM for x in operands]
    return [space(x.shape, x.dtype) for space, x in zip(spaces, operands)] + [
        pltpu.SemaphoreType.DMA((len(operands),))
    ]


def pack_kernel(*refs):
    own_ref, share_ref, tail_ref, low_ref = refs[5:9]
    fetch(refs[:5], refs[9:14], refs[14])
    len_ref, k_ref, v_ref, logit_ref, gain_ref = refs[9:14]
    rows, dim = k_ref.shape
    heads = logit_ref.shape[0]
    _, low, _ = bounds(len_ref, rows)
    low_ref[...] = jnp.full(low_ref.shape, low, jnp.int32)
    key = k_ref[...].astype(F32)
    own_ref[:rows, :dim] = (key * rms(key) * gain_ref[...]).astype(BF16)
    own_ref[:rows, dim:] = v_ref[...]
    log_gate = log_sigmoid(logit_ref[...].astype(F32))
    zero = jnp.zeros((TAIL - 3 * heads, rows), F32)
    parts = jnp.concatenate(list(split3(log_gate)) + [zero], axis=0).astype(BF16)

    def sums(test):
        result = dot_nn(parts, ones_where(rows, test))
        total = result[:heads] + result[heads : 2 * heads] + result[2 * heads : 3 * heads]
        return total

    onward = jnp.concatenate(list(split3(sums(lambda u, t: u >= t))) + [zero], axis=0)
    own_ref[rows:, :] = onward.astype(BF16)
    share_ref[...] = onward.astype(BF16)
    past = -sums(lambda u, t: u <= t)
    tail_ref[...] = jnp.concatenate(list(split3(past)) + [zero], axis=0).astype(BF16)


def key_columns(kaug, raw, tail, extra):
    rows = kaug.shape[0]
    dim = raw.shape[1] // 2
    kaug[:, :dim] = raw[:rows, :dim]
    zero = jnp.zeros((dim - 2 * TAIL, rows), F32)
    filled = jnp.concatenate([tail, extra.astype(F32), zero], axis=0)
    kaug[:, dim:] = filled.T.astype(BF16)


def strictly_after(tail):
    rows = tail.shape[1]
    moved = pltpu.roll(tail.astype(F32), rows - 1, 1)
    return jnp.where(iota(moved.shape, 1) == rows - 1, 0.0, moved)


def forward_block(kaug, qt, raw, tail, extra, kt, store, mixed, causal):
    rows = kaug.shape[0]
    dim = raw.shape[1] // 2
    key_columns(kaug, raw, tail, extra)
    both = flip(raw[:rows, :])
    kt[:dim, :] = both[:dim]
    kt[dim:, :] = ones_rows(rows)
    value_t = jnp.concatenate([both[dim:], ones_rows(rows)], axis=0)
    for part in chunks(qt.shape[1]):
        scores = dot_nn(kaug[...], qt[:, part])
        if causal:
            place = iota(scores.shape, 1)
            scores = jnp.where(iota(scores.shape, 0) <= place - place // rows * rows, scores, -BIG)
        store[:, part] = jnp.exp(scores).astype(BF16)
    for part in chunks(qt.shape[1]):
        mixed(part, dot_nn(value_t, store[:, part]))


def own_kernel(n, *refs):
    own_ref, tail_ref, qt, gt, acc, w_ref, kt, extra_ref, kaug = refs[4:13]
    fetch(refs[:4], refs[13:17], refs[17])
    len_ref, q_ref, g_ref, gain_ref = refs[13:17]
    rows = q_ref.shape[0]
    dim = gain_ref.shape[1]
    heads = q_ref.shape[1] // dim
    scale = dim ** (-0.5)
    me, _, spans = bounds(len_ref, rows)
    row = iota((TAIL, rows), 0)
    for k in range(n):
        tile = iota((TAIL, rows), 1) // TILE + (me ^ k) * (rows // TILE)
        extra = jnp.where(row < 3, 1.0, 0.0)
        for d, (start, end) in enumerate(spans):
            inside = jnp.where((tile >= start) & (tile < end), 1.0, 0.0)
            extra = jnp.where(row == 3 + d, inside, extra)
        extra_ref[k] = extra.astype(BF16)
    tail = tail_ref[...].astype(F32)
    past = -(tail[:heads] + tail[heads : 2 * heads] + tail[2 * heads : 3 * heads])
    parts = split3(past)
    docs = (row >= 3) & (row < 3 + len(spans))
    other = jnp.where(docs, (extra_ref[0].astype(F32) - 1.0) * BIG, 0.0)
    for h in range(heads):
        x = q_ref[:, cols(h, dim)].astype(F32)
        normed = x * rms(x) * (gain_ref[...] * scale)
        qt[:dim, cols(h, rows)] = flip(normed.astype(BF16))
        gt[:, cols(h, rows)] = flip(g_ref[:, cols(h, dim)])
        mine = (row < 3 * heads) & (row - row // heads * heads == h)
        qt[dim : dim + TAIL, cols(h, rows)] = jnp.where(mine, 1.0, 0.0).astype(BF16)
        gate = other
        for s in range(3):
            gate = jnp.where(row == s, parts[s][h : h + 1], gate)
        qt[dim + TAIL : dim + 2 * TAIL, cols(h, rows)] = gate.astype(BF16)
        qt[dim + 2 * TAIL :, cols(h, rows)] = jnp.zeros((dim - 2 * TAIL, rows), BF16)

    def mixed(part, value):
        acc[:, part] = value

    forward_block(kaug, qt, own_ref, tail, extra_ref[0], kt, w_ref, mixed, True)


def early_kernel(ks, low_ref, qt, extra_ref, *refs):
    raw_refs = refs[: len(ks)]
    w_ref, o_ref, kt_ref, kaug = refs[len(ks) :]
    rows = kaug.shape[0]
    me, low = first_block(low_ref)
    for i, k in enumerate(ks):
        raw = raw_refs[i]

        def mixed(part, value):
            o_ref[i, :, part] = value

        @pl.when(is_active(me, low, k))
        def _():
            tail = strictly_after(raw[rows:, :])
            forward_block(
                kaug, qt, raw, tail, extra_ref[k], kt_ref.at[i], w_ref.at[i], mixed, False
            )


def second_kernel(n, heads, before, ks, last, low_ref, qt, extra_ref, acc0, o_ref, share_ref, *refs):
    raw_refs = dict(zip([k for k in range(1, n) if k != last], refs[: n - 2]))
    w_ref, acc, kt_ref, between_ref, kaug = refs[n - 2 :]
    rows = kaug.shape[0]
    me, low = first_block(low_ref)
    wholes = {}
    for k in range(1, n):
        tail = share_ref[...] if k == last else raw_refs[k][rows:, :]
        tail = tail.astype(F32)
        total = tail[:heads] + tail[heads : 2 * heads] + tail[2 * heads : 3 * heads]
        wholes[k] = jnp.broadcast_to(total[:, :1], (heads, rows))
    for k in range(n):
        total = jnp.zeros((heads, rows), F32)
        for other in range(1, n):
            if other != k:
                b = me ^ other
                total = total + jnp.where((b > (me ^ k)) & (b < me), wholes[other], 0.0)
        between_ref[k] = lay_out(total)

    acc[...] = acc0[...]
    for i, k in enumerate(before):

        @pl.when(is_active(me, low, k))
        def _():
            root = jnp.exp(0.5 * between_ref[k])
            for part in chunks(root.shape[1]):
                acc[:, part] += o_ref[i, :, part] * root[:, part] * root[:, part]

    for i, k in enumerate(ks):

        @pl.when(is_active(me, low, k))
        def _():
            root = jnp.exp(0.5 * between_ref[k])

            def mixed(part, value):
                acc[:, part] += value * root[:, part] * root[:, part]

            raw = raw_refs[k]
            tail = strictly_after(raw[rows:, :])
            forward_block(
                kaug, qt, raw, tail, extra_ref[k], kt_ref.at[i], w_ref.at[i], mixed, False
            )


def backward_block(rows, raw, weights, factor, inner, kt, qt, gt, ds, plow, acc, kg, piece, gcol):
    dim = raw.shape[1] // 2
    for part in chunks(qt.shape[1]):
        grad = dot_nn(raw[:rows, dim:], gt[:, part])
        prob = weights[:, part].astype(F32) * factor[:, part]
        plow[:, part] = prob.astype(BF16)
        ds[:, part] = (prob * (grad - inner[:, part])).astype(BF16)
    for part in chunks(qt.shape[1]):
        acc[:, part] += dot_nn(kt[...], ds[:, part])
    key_part = dot_nt(qt[: dim + ONES, :], ds[...])
    piece[:dim, :] = key_part[:dim].astype(BF16)
    gcol[...] = -key_part[dim : dim + 8]
    kg[...] += key_part[:dim] * kt[:dim, :].astype(F32)
    piece[dim:, :] = dot_nt(gt[...], plow[...]).astype(BF16)


def idle_block(piece, gcol):
    piece[...] = jnp.zeros(piece.shape, BF16)
    gcol[...] = jnp.zeros(gcol.shape, F32)


def backward_set(ks, me, low, rows, raws, sources, between, log_ref, inner, state, pieces, gcols):
    qt, gt, ds, plow, acc, kg = state
    for i, k in enumerate(ks):
        weights, kt = sources[k]

        @pl.when(is_active(me, low, k))
        def _():
            factor = jnp.exp(between[k] - log_ref[...])
            backward_block(
                rows, raws[k], weights, factor, inner, kt, qt, gt, ds, plow, acc, kg,
                pieces[i], gcols[i],
            )

        if k:

            @pl.when(~is_active(me, low, k))
            def _():
                idle_block(pieces[i], gcols[i])


def source_map(ks_a, ks_b, last, arrays):
    wa, ka, wb, kb, wl, kl = arrays
    found = {k: (wa.at[i], ka.at[i]) for i, k in enumerate(ks_a)}
    found.update({k: (wb.at[i], kb.at[i]) for i, k in enumerate(ks_b)})
    found[last] = (wl, kl)
    return found


def middle_kernel(ks_a, ks_b, last, ks, heads, *refs):
    low_ref, qt, gt, extra_ref, acc0, between = refs[:6]
    stores = refs[6:10]
    raws = dict(zip([last] + ks, refs[10 : 11 + len(ks)]))
    refs = refs[11 + len(ks) :]
    mixed_ref, acc, log_ref, inner, kg, w_last, kt_last = refs[:7]
    gcols = [refs[7].at[i] for i in range(len(ks))]
    rows = qt.shape[1] // heads
    pieces = [refs[8].at[cols(i, rows)] for i in range(len(ks))]
    kaug, ds, plow = refs[9:]
    dim = gt.shape[0]
    me, low = first_block(low_ref)
    acc[...] = acc0[...]

    @pl.when(is_active(me, low, last))
    def _():
        root = jnp.exp(0.5 * between[last])

        def mixed(part, value):
            acc[:, part] += value * root[:, part] * root[:, part]

        raw = raws[last]
        tail = strictly_after(raw[rows:, :])
        forward_block(kaug, qt, raw, tail, extra_ref[last], kt_last, w_last, mixed, False)

    for part in chunks(qt.shape[1]):
        total = acc[dim : dim + 1, part]
        mixed_t = (acc[:dim, part] * (1.0 / total)).astype(BF16)
        mixed_ref[:, part] = mixed_t
        log_ref[:, part] = jnp.log(total)
        product = gt[:, part].astype(F32) * mixed_t.astype(F32)
        inner[:, part] = jnp.sum(product, axis=0, keepdims=True)
    acc[...] = jnp.zeros(acc.shape, F32)
    kg[...] = jnp.zeros(kg.shape, F32)
    sources = source_map(ks_a, ks_b, last, stores + (w_last, kt_last))
    state = (qt, gt, ds, plow, acc, kg)
    backward_set(ks, me, low, rows, raws, sources, between, log_ref, inner, state, pieces, gcols)


def middle_two_kernel(ks_a, ks_b, last, ks, heads, *refs):
    low_ref, qt, gt, acc0, between, log_ref, inner, kg0 = refs[:8]
    sources = source_map(ks_a, ks_b, last, refs[8:14])
    raws = dict(zip(ks, refs[14 : 14 + len(ks)]))
    refs = refs[14 + len(ks) :]
    acc, kg = refs[:2]
    gcols = [refs[2].at[i] for i in range(len(ks))]
    rows = qt.shape[1] // heads
    pieces = [refs[3].at[cols(i, rows)] for i in range(len(ks))]
    ds, plow = refs[4:]
    me, low = first_block(low_ref)
    acc[...] = acc0[...]
    kg[...] = kg0[...]
    state = (qt, gt, ds, plow, acc, kg)
    backward_set(ks, me, low, rows, raws, sources, between, log_ref, inner, state, pieces, gcols)


def late_kernel(n, ks_a, ks_b, odds, low_ref, kgain_ref, qgain_ref, *refs):
    half = n // 2
    qt, gt, acc0, between, log_ref, inner, kg0 = refs[:7]
    sources = source_map(ks_a, ks_b, 0, refs[7:13])
    g_odds = refs[13 : 13 + len(odds)]
    refs = refs[13 + len(odds) :]
    raws = {2 * s: refs[s] for s in range(half)}
    acc, keep_ref, give_ref = refs[half : half + 3]
    piece_refs = refs[half + 3 : 2 * half + 3]
    kg, ds, plow, gall = refs[2 * half + 3 :]
    rows = ds.shape[0]
    dim = qgain_ref.shape[1]
    heads = qt.shape[1] // rows
    me, low = first_block(low_ref)
    acc[...] = acc0[...]
    kg[...] = kg0[...]
    for ks, g_odd in zip(odds, g_odds):
        for i, k in enumerate(ks):
            gall[k] = g_odd[i]
    ks = [2 * s for s in range(half - 1, -1, -1)]
    pieces = [piece_refs[k // 2] for k in ks]
    gcols = [gall.at[k] for k in ks]
    state = (qt, gt, ds, plow, acc, kg)
    backward_set(ks, me, low, rows, raws, sources, between, log_ref, inner, state, pieces, gcols)

    qg = jnp.zeros((dim, rows), F32)
    row_sums = []
    for h in range(heads):
        part = cols(h, rows)
        qg = qg + acc[:dim, part] * qt[:dim, part].astype(F32)
        row_sums.append(acc[dim : dim + 1, part])
    gall[0] += jnp.concatenate(row_sums + row_sums, axis=0)[:8]
    query_gain = jnp.sum(qg.T, axis=0, keepdims=True) / qgain_ref[...]
    key_gain = jnp.sum(kg[...].T, axis=0, keepdims=True) / kgain_ref[...]
    gain_row = jnp.concatenate([query_gain, key_gain], axis=1)
    is_gain = iota((8, rows), 0) == heads
    later = ones_where(rows, lambda u, t: u >= t)
    stacked = jnp.concatenate([gall[k] for k in range(n)], axis=0)
    suffix = sum(dot_nn(part.astype(BF16), later) for part in split3(stacked))
    locals_ = [suffix[8 * k : 8 * k + 8] for k in range(n)]
    wholes = [jnp.broadcast_to(local[:, :1], (8, rows)) for local in locals_]
    results = []
    for k in range(n):
        total = locals_[k]
        for other in range(n):
            if other != k:
                total = total + jnp.where((me ^ other) > (me ^ k), wholes[other], 0.0)
        total = jnp.where(is_active(me, low, k), total, 0.0)
        results.append(jnp.where(is_gain, gain_row, total))
    for s in range(half):
        keep_ref[8 * s : 8 * s + 8, :] = results[2 * s]
        give_ref[8 * s : 8 * s + 8, :] = results[2 * s + 1]


def query_kernel(q_ref, qgain_ref, acc, mixed_ref, qgrad_ref, out_ref):
    rows = q_ref.shape[0]
    dim = qgain_ref.shape[1]
    scale = dim ** (-0.5)
    eye = ones_where(rows, lambda i, j: i == j)
    for h in range(q_ref.shape[1] // dim):
        out_ref[:, cols(h, dim)] = dot_nt(eye, mixed_ref[:, cols(h, rows)]).astype(BF16)
        x = q_ref[:, cols(h, dim)].astype(F32)
        rstd = rms(x)
        hat = x * rstd
        back = acc[:dim, cols(h, rows)].T.astype(BF16).astype(F32) * (qgain_ref[...] * scale)
        mean = jnp.mean(back * hat, axis=-1, keepdims=True)
        qgrad_ref[:, cols(h, dim)] = (rstd * (back - hat * mean)).astype(BF16)


def add_kernel(at, a_ref, b_ref, o_ref):
    other = b_ref[cols(at, a_ref.shape[0]), :]
    o_ref[...] = (a_ref[...].astype(F32) + other.astype(F32)).astype(BF16)


def settle_kernel(heads, keep_ref, got_ref, total_ref, gain_ref):
    total_ref[...] = keep_ref[...] + got_ref[...]
    gain_ref[...] = total_ref[heads : heads + 1, :]


def pair_kernel(a_ref, b_ref, o_ref):
    o_ref[...] = a_ref[...] + b_ref[...]


def spread_kernel(heads, total_ref, a_ref, b_ref, *outs):
    gain = a_ref[...] + b_ref[...]
    for s, out in enumerate(outs):
        rows = total_ref[8 * s : 8 * s + 8, :]
        out[...] = jnp.where(iota(rows.shape, 0) == heads, gain, rows)


def finish_kernel(at, k_ref, gain_ref, *refs):
    piece_refs = refs[:-2]
    kgrad_ref, vgrad_ref = refs[-2:]
    dim = k_ref.shape[1]
    rows = k_ref.shape[0]
    total = piece_refs[0][...].astype(F32) + piece_refs[1][at * rows :, :].astype(F32)
    for ref in piece_refs[2:]:
        total = total + ref[...].astype(F32)
    vgrad_ref[...] = total[dim:].T.astype(BF16)
    x = k_ref[...].astype(F32)
    rstd = rms(x)
    hat = x * rstd
    back = total[:dim].T * gain_ref[...]
    mean = jnp.mean(back * hat, axis=-1, keepdims=True)
    kgrad_ref[...] = (rstd * (back - hat * mean)).astype(BF16)


def forget_kernel(logit_ref, *refs):
    small_refs = refs[:-2]
    fgrad_ref, gains_ref = refs[-2:]
    heads = logit_ref.shape[0]
    small = small_refs[0][...]
    for ref in small_refs[1:]:
        small = small + ref[...]
    logit = logit_ref[...].astype(F32)
    fgrad_ref[...] = small[:heads] * (1.0 / (1.0 + jnp.exp(logit)))
    row = small[heads : heads + 1]
    dim = row.shape[1] // 2
    gains_ref[...] = jnp.concatenate([row[:, :dim], row[:, dim:]], axis=0)


def whole_step(queries, key_vectors, values, forget_logit, out_grad, query_gain, key_gain, lengths):
    n = lax.axis_size("seq")
    half = n // 2
    rows, full = queries.shape[1:]
    dim = query_gain.shape[0]
    heads = full // dim
    wide = heads * rows
    width = 2 * dim
    tall = dim + ONES
    query, grad, key, logit = queries[0], out_grad[0], key_vectors[0], forget_logit[0]
    qgain, kgain = query_gain[None], key_gain[None]
    matmul = 2 * rows * wide * width
    head_row = struct(heads, rows, dtype=F32)
    line = struct(1, wide, dtype=F32)
    state = struct(tall, wide, dtype=F32)
    key_sum = struct(dim, rows, dtype=F32)
    piece = struct(rows, width)
    wide_scratch = pltpu.VMEM((rows, wide), BF16)

    inputs = [lengths, key, values[0], logit, kgain]
    own, share, own_tail, low = kernel_call(
        pack_kernel, inputs,
        (
            struct(rows + TAIL, width), struct(TAIL, rows), struct(TAIL, rows),
            struct(8, 128, dtype=jnp.int32),
        ),
        near(inputs), far=5,
    )
    gather_order = [2] + list(range(n - 2, 2, -2))
    last = gather_order[-1] + 1
    blocks = {0: own}
    for k in gather_order:
        blocks[k] = swap(own, "seq", k)
    blocks[1] = swap(own, "seq", 1)
    share = swap(share, "seq", last)
    for k in gather_order:
        blocks[k + 1] = swap(blocks[k], "seq", 1)

    inputs = [lengths, query, grad, qgain]
    kaug_scratch = pltpu.VMEM((rows, width), BF16)
    qt, gt, acc, w0, kt0, extra = kernel_call(
        functools.partial(own_kernel, n), inputs + [own, own_tail],
        (
            struct(width, wide), struct(dim, wide), state, struct(rows, wide), struct(tall, rows),
            struct(n, TAIL, rows),
        ),
        [kaug_scratch] + near(inputs),
        flops=2 * matmul, far=4,
    )

    def stores(count):
        return struct(count, rows, wide), struct(count, tall, rows)

    ks_a = [1] + gather_order[:-1]
    ks_b = [gather_order[-1]] + [k + 1 for k in gather_order[:-1]]
    w_a, o_a, kt_a = kernel_call(
        functools.partial(early_kernel, ks_a),
        [low, qt, extra] + [blocks[k] for k in ks_a],
        (stores(half)[0], struct(half, tall, wide, dtype=F32), stores(half)[1]),
        [kaug_scratch],
        flops=2 * half * matmul,
    )
    w_b, acc, kt_b, between = kernel_call(
        functools.partial(second_kernel, n, heads, ks_a, ks_b, last),
        [low, qt, extra, acc, o_a, share] + [blocks[k] for k in range(1, n) if k != last],
        (stores(half - 1)[0], state, stores(half - 1)[1], struct(n, 1, wide, dtype=F32)),
        [kaug_scratch],
        flops=2 * half * matmul,
    )
    down = list(range(n - 1, 0, -2))
    odds = [down[: half // 2], down[half // 2 :]]
    kept = [w_a, kt_a, w_b, kt_b]
    results = kernel_call(
        functools.partial(middle_kernel, ks_a, ks_b, last, odds[0], heads),
        [low, qt, gt, extra, acc, between] + kept + [blocks[k] for k in [last] + odds[0]],
        (
            struct(dim, wide), state, line, line, key_sum, struct(rows, wide), struct(tall, rows),
            struct(len(odds[0]), 8, rows, dtype=F32), struct(len(odds[0]) * rows, width),
        ),
        [kaug_scratch, wide_scratch, wide_scratch],
        flops=4 * half * matmul,
    )
    mixed_t, acc, log_total, inner, key_acc, w_last, kt_last, gate_one, stack = results
    stacks = [swap(stack, "seq", 1)]
    results = kernel_call(
        functools.partial(middle_two_kernel, ks_a, ks_b, last, odds[1], heads),
        [low, qt, gt, acc, between, log_total, inner, key_acc] + kept + [w_last, kt_last]
        + [blocks[k] for k in odds[1]],
        (
            state, key_sum, struct(len(odds[1]), 8, rows, dtype=F32),
            struct(len(odds[1]) * rows, width),
        ),
        [wide_scratch, wide_scratch],
        flops=2 * half * matmul,
    )
    acc, key_acc, gate_two, stack = results
    stacks.append(swap(stack, "seq", 1))
    place = {k: (g, i) for g, ks in enumerate(odds) for i, k in enumerate(ks)}

    small = struct(8 * half, rows, dtype=F32)
    results = kernel_call(
        functools.partial(late_kernel, n, ks_a, ks_b, odds),
        [low, kgain, qgain, qt, gt, acc, between, log_total, inner, key_acc]
        + kept + [w0, kt0, gate_one, gate_two]
        + [blocks[2 * s] for s in range(half)],
        (state, small, small) + (piece,) * half,
        [pltpu.VMEM((dim, rows), F32), wide_scratch, wide_scratch, pltpu.VMEM((n, 8, rows), F32)],
        flops=4 * half * matmul,
    )
    acc, keep, give = results[:3]
    even = results[3:]

    got = swap(give, "seq", 1)
    query_grad, attention = kernel_call(
        query_kernel, [query, qgain, acc, mixed_t],
        (struct(rows, full), struct(rows, full)), flops=matmul,
    )
    arrived = [even[0], stacks[1]]
    for s in range(half - 1, 0, -1):
        group, at = place[2 * s + 1]
        both = kernel_call(functools.partial(add_kernel, at), [even[s], stacks[group]], piece)
        arrived.append(swap(both, "seq", 2 * s))
    eight = struct(8, rows, dtype=F32)
    gain_line = struct(1, width, dtype=F32)
    total, gain = kernel_call(
        functools.partial(settle_kernel, heads), [keep, got], (small, gain_line)
    )
    bit = 1
    while 2 * bit < lax.axis_size("rep"):
        gain = kernel_call(pair_kernel, [gain, swap(gain, "rep", bit)], gain_line)
        bit *= 2
    smalls = kernel_call(
        functools.partial(spread_kernel, heads),
        [total, gain, swap(gain, "rep", bit)], (eight,) * half,
    )
    smalls = [smalls[0]] + [swap(smalls[s], "seq", 2 * s) for s in range(1, half)]
    forget_grad, gains = kernel_call(
        forget_kernel, [logit] + smalls, (head_row, struct(2, dim, dtype=F32))
    )
    key_grad, value_grad = kernel_call(
        functools.partial(finish_kernel, place[1][1]), [key, kgain] + arrived, (struct(rows, dim), struct(rows, dim)),
        flops=matmul,
    )
    return (
        attention[None],
        query_grad[None],
        key_grad[None],
        value_grad[None],
        forget_grad[None],
        gains,
    )


def solution(mesh):
    return jax.shard_map(
        whole_step,
        mesh=mesh,
        in_specs=(
            P("rep", "seq", None),
            P("rep", "seq", None),
            P("rep", "seq", None),
            P("rep", None, "seq"),
            P("rep", "seq", None),
            P(),
            P(),
            P("rep", None),
        ),
        out_specs=(
            P("rep", "seq", None),
            P("rep", "seq", None),
            P("rep", "seq", None),
            P("rep", "seq", None),
            P("rep", None, "seq"),
            P(),
        ),
        check_vma=False,
    )
```

time: 72.9 us -> 63.5 us (0.87)
  waiting for transfers between devices: 32.7 us -> 22.4 us
  starting transfers between devices: 30.2 us -> 32 us
  Pallas kernels: 8.96 us -> 8.14 us
    ppermute x20 -> x19, waiting for transfers between devices: 29.7 us -> 22.4 us  [swap(): return lax.ppermute(value, axis, [(i, i ^ bit) for i in range(count)])]
    ppermute x1 -> x0, waiting for transfers between devices: 3 us -> none  [swap_both(): lax.ppermute(value, ('seq', 'rep'), [(i, i ^ bit) for i in range(count)])]
    ppermute x20 -> x19, starting transfers between devices: 30.2 us -> 32 us  [swap(): return lax.ppermute(value, axis, [(i, i ^ bit) for i in range(count)])]
    pallas_call x14 -> x16, Pallas kernels: 8.96 us -> 8.14 us  [kernel_call(): pl.pallas_call(kernel, out_shape=outs, in_specs=in_specs, out_specs=jax.t...]
  transfers between devices with their start and end apart: 21 -> 19, of which waited for: 12 -> 8; matrix products, arithmetic and copies ran while one was open for 0% -> 0% of each run, Pallas kernels for 8% -> 9%
where the time goes in v2:
time: 63.5 us; the launch traced here: 63.3 us
  starting transfers between devices  32 us (50%)
  waiting for transfers between devices  22.4 us (35%)
  Pallas kernels  8.14 us (13%)
  between operations  0.81 us (1%)
    ppermute x19, starting transfers between devices, swap(): return lax.ppermute(value, axis, [(i, i ^ bit) for i in range(count)])  32 us
    ppermute x19, waiting for transfers between devices, swap(): return lax.ppermute(value, axis, [(i, i ^ bit) for i in range(count)])  22.4 us
    pallas_call x16, Pallas kernels, kernel_call(): pl.pallas_call(kernel, out_shape=outs, in_specs=in_specs, out_specs=jax.t...  8.14 us
  transfers between devices with their start and end apart: 19, of which 8 were waited for; matrix products, arithmetic and copies ran while one was open for 0% of the time, Pallas kernels for 9%

profile of v2, /device:TPU:0, one launch (start us, length us, event | category | flops | bytes accessed | tf_op | source)
XLA Modules:
  0.0 63.3 jit_solution(2394439956963899338)
XLA Ops:
  0.6 1.1 %shard_map.127 = (bf16[272,256]{1,0:T(8,128)(2,1)S(1)}, bf16[16,256]{1,0:T(8,128)(2,1)S(1)}, bf16[16,256]{1,0:T(8,128)(2,1)S(1)}, s32[8,128]{1,0:T(8,128)S(1)}) custom-call(s32[1,4]{1,0:T(1,128)} %refs_0_.3, bf16[256,128]{1,0:T(8,128)(2,1)} %bitcast.12, bf16[256,128]{1,0:T(8,128)(2,1)} %bitcast.24, bf16[4,256]{1,0:T(4,128)(2,1)} %bitcast.16, f32[1,128]{1,0:T(1,128)} %bitcast.18), custom_call_target="tpu_custom_call" | custom-call | flops 1048576 | bytes 1048576 | tf_op jit(solution)/shard_map/pallas_call | solution.py:38
  1.7 3.1 %collective-permute-start.1 = (bf16[272,256]{1,0:T(8,128)(2,1)S(1)}, bf16[272,256]{1,0:T(8,128)(2,1)S(1)}, u32[]{:S(2)}, u32[]{:S(2)}) collective-permute-start(bf16[272,256]{1,0:T(8,128)(2,1)S(1)} %get-tuple-element.56.refs_4_.refs_15_), channel_id=1, source_target_pairs={{0,8},{4,12},{8,0},{12,4},{16,24},{20,28},{24,16},{28,20},{1,9},{5... | collective-permute-start | bytes 417800 | tf_op jit(solution)/shard_map/ppermute | solution.py:25
  4.9 2.5 %collective-permute-start.2 = (bf16[272,256]{1,0:T(8,128)(2,1)S(1)}, bf16[272,256]{1,0:T(8,128)(2,1)S(1)}, u32[]{:S(2)}, u32[]{:S(2)}) collective-permute-start(bf16[272,256]{1,0:T(8,128)(2,1)S(1)} %get-tuple-element.56.refs_4_.refs_15_), channel_id=1, source_target_pairs={{0,24},{4,28},{8,16},{12,20},{16,8},{20,12},{24,0},{28,4},{1,25},{... | collective-permute-start | bytes 417800 | tf_op jit(solution)/shard_map/ppermute | solution.py:25
  7.3 0.1 collective-permute-start.5
  7.5 1.5 %collective-permute-start = (bf16[272,256]{1,0:T(8,128)(2,1)S(1)}, bf16[272,256]{1,0:T(8,128)(2,1)S(1)}, u32[]{:S(2)}, u32[]{:S(2)}) collective-permute-start(bf16[272,256]{1,0:T(8,128)(2,1)S(1)} %get-tuple-element.56.refs_4_.refs_15_), channel_id=1, source_target_pairs={{0,4},{4,0},{8,12},{12,8},{16,20},{20,16},{24,28},{28,24},{1,5},{5... | collective-permute-start | bytes 417800 | tf_op jit(solution)/shard_map/ppermute | solution.py:25
  9.0 0.0 collective-permute-done.1.refs_1_.refs_16_
  9.0 1.2 %collective-permute-start.4 = (bf16[272,256]{1,0:T(8,128)(2,1)S(1)}, bf16[272,256]{1,0:T(8,128)(2,1)S(1)}, u32[]{:S(2)}, u32[]{:S(2)}) collective-permute-start(bf16[272,256]{1,0:T(8,128)(2,1)S(1)} %collective-permute-done.1.refs_1_.refs_16_), channel_id=1, source_target_pairs={{0,4},{4,0},{8,12},{12,8},{16,20},{20,16},{24,28},{28,24},{1,5},{5... | collective-permute-start | bytes 417800 | tf_op jit(solution)/shard_map/ppermute | solution.py:25
  10.2 4.7 %collective-permute-done.2.refs_2_.refs_4_.refs_18_ = bf16[272,256]{1,0:T(8,128)(2,1)S(1)} collective-permute-done((bf16[272,256]{1,0:T(8,128)(2,1)S(1)}, bf16[272,256]{1,0:T(8,128)(2,1)S(1)}, u32[]{:S(2)}, u32[]{:S(2)}) %collective-permute-start.2) | collective-permute-done | bytes 139296 | tf_op jit(solution)/shard_map/ppermute | solution.py:25
  14.9 1.5 %collective-permute-start.6 = (bf16[272,256]{1,0:T(8,128)(2,1)S(1)}, bf16[272,256]{1,0:T(8,128)(2,1)S(1)}, u32[]{:S(2)}, u32[]{:S(2)}) collective-permute-start(bf16[272,256]{1,0:T(8,128)(2,1)S(1)} %collective-permute-done.2.refs_2_.refs_4_.refs_18_), channel_id=1, source_target_pairs={{0,4},{4,0},{8,12},{12,8},{16,20},{20,16},{24,28},{28,24},{1,5},{5... | collective-permute-start | bytes 417800 | tf_op jit(solution)/shard_map/ppermute | solution.py:25
  16.5 4.7 %collective-permute-start.3 = (bf16[16,256]{1,0:T(8,128)(2,1)S(1)}, bf16[16,256]{1,0:T(8,128)(2,1)S(1)}, u32[]{:S(2)}, u32[]{:S(2)}) collective-permute-start(bf16[16,256]{1,0:T(8,128)(2,1)S(1)} %get-tuple-element.63), channel_id=1, source_target_pairs={{0,20},{4,16},{8,28},{12,24},{16,4},{20,0},{24,12},{28,8},{1,21},{... | collective-permute-start | bytes 24584 | tf_op jit(solution)/shard_map/ppermute | solution.py:25
  21.1 2.0 %shard_map.128 = (bf16[256,1024]{1,0:T(8,128)(2,1)S(1)}, bf16[128,1024]{1,0:T(8,128)(2,1)S(1)}, f32[144,1024]{1,0:T(8,128)S(1)}, bf16[256,1024]{1,0:T(8,128)(2,1...) custom-call(s32[1,4]{1,0:T(1,128)} %refs_0_.3, bf16[256,512]{1,0:T(8,128)(2,1)} %bitcast.14, ...), custom_call_target="tpu_custom_call" | custom-call | flops 268435456 | bytes 1048576 | tf_op jit(solution)/shard_map/pallas_call | solution.py:38
  23.1 0.0 collective-permute-done.5.refs_3_.refs_17_
  23.1 1.6 %collective-permute-start.7 = (bf16[272,256]{1,0:T(8,128)(2,1)S(1)}, bf16[272,256]{1,0:T(8,128)(2,1)S(1)}, u32[]{:S(2)}, u32[]{:S(2)}) collective-permute-start(bf16[272,256]{1,0:T(8,128)(2,1)S(1)} %collective-permute-done.5.refs_3_.refs_17_), channel_id=1, source_target_pairs={{0,4},{4,0},{8,12},{12,8},{16,20},{20,16},{24,28},{28,24},{1,5},{5... | collective-permute-start | bytes 417800 | tf_op jit(solution)/shard_map/ppermute | solution.py:25
  24.7 0.0 collective-permute-done.refs_0_.refs_15_
  24.7 0.1 shard_map.129
  24.8 0.0 collective-permute-done.3.share_ref
  24.8 0.0 collective-permute-done.4.refs_2_.refs_14_
  24.8 0.0 collective-permute-done.6.refs_5_.refs_11_
  24.8 0.2 shard_map.130
  25.0 3.4 %collective-permute-done.7.refs_10_.refs_12_ = bf16[272,256]{1,0:T(8,128)(2,1)S(1)} collective-permute-done((bf16[272,256]{1,0:T(8,128)(2,1)S(1)}, bf16[272,256]{1,0:T(8,128)(2,1)S(1)}, u32[]{:S(2)}, u32[]{:S(2)}) %collective-permute-start.7) | collective-permute-done | bytes 139296 | tf_op jit(solution)/shard_map/ppermute | solution.py:25
  28.4 0.2 shard_map.131
  28.7 0.0 copy-start.3
  28.7 0.0 copy-start.4
  28.7 0.1 shard_map.132
  28.8 2.3 %collective-permute-start.8 = (bf16[512,256]{1,0:T(8,128)(2,1)S(1)}, bf16[512,256]{1,0:T(8,128)(2,1)S(1)}, u32[]{:S(2)}, u32[]{:S(2)}) collective-permute-start(bf16[512,256]{1,0:T(8,128)(2,1)S(1)} %get-tuple-element.87), channel_id=1, source_target_pairs={{0,4},{4,0},{8,12},{12,8},{16,20},{20,16},{24,28},{28,24},{1,5},{5... | collective-permute-start | bytes 786440 | tf_op jit(solution)/shard_map/ppermute | solution.py:25
  31.1 0.1 collective-permute-start.9
  31.1 0.0 copy-done.3
  31.1 0.0 copy-done.4
  31.1 0.0 copy-start.1
  31.1 1.3 %shard_map.133 = (f32[144,1024]{1,0:T(8,128)S(1)}, f32[32,256]{1,0:T(8,128)S(1)}, f32[32,256]{1,0:T(8,128)S(1)}, bf16[256,256]{1,0:T(8,128)(2,1)S(1)}, bf16[256,...) custom-call(s32[8,128]{1,0:T(8,128)S(1)} %get-tuple-element.55.low_ref.refs_0_, ...), custom_call_target="tpu_custom_call" | custom-call | flops 2147483648 | bytes 1048576 | tf_op jit(solution)/shard_map/pallas_call | solution.py:38
  32.4 0.0 copy-start.2
  32.4 0.0 copy-start
  32.4 4.2 %collective-permute-done.8.b_ref.refs_1_ = bf16[512,256]{1,0:T(8,128)(2,1)S(1)} collective-permute-done((bf16[512,256]{1,0:T(8,128)(2,1)S(1)}, bf16[512,256]{1,0:T(8,128)(2,1)S(1)}, u32[]{:S(2)}, u32[]{:S(2)}) %collective-permute-start.8) | collective-permute-done | bytes 262176 | tf_op jit(solution)/shard_map/ppermute | solution.py:25
  36.7 0.1 collective-permute-start.12
  36.8 2.7 %collective-permute-done.9.b_ref = bf16[512,256]{1,0:T(8,128)(2,1)S(1)} collective-permute-done((bf16[512,256]{1,0:T(8,128)(2,1)S(1)}, bf16[512,256]{1,0:T(8,128)(2,1)S(1)}, u32[]{:S(2)}, u32[]{:S(2)}) %collective-permute-start.9) | collective-permute-done | bytes 262176 | tf_op jit(solution)/shard_map/ppermute | solution.py:25
  39.5 3.5 %collective-permute-start.11 = (bf16[256,256]{1,0:T(8,128)(2,1)S(1)}, bf16[256,256]{1,0:T(8,128)(2,1)S(1)}, u32[]{:S(2)}, u32[]{:S(2)}) collective-permute-start(bf16[256,256]{1,0:T(8,128)(2,1)S(1)} %shard_map.136), channel_id=1, source_target_pairs={{0,16},{4,20},{8,24},{12,28},{16,0},{20,4},{24,8},{28,12},{1,17},{... | collective-permute-start | bytes 393224 | tf_op jit(solution)/shard_map/ppermute | solution.py:25
  43.1 0.1 collective-permute-start.10
  43.2 1.2 %collective-permute-start.13 = (f32[32,256]{1,0:T(8,128)S(1)}, f32[32,256]{1,0:T(8,128)S(1)}, u32[]{:S(2)}, u32[]{:S(2)}) collective-permute-start(f32[32,256]{1,0:T(8,128)S(1)} %get-tuple-element.95), channel_id=1, source_target_pairs={{0,4},{4,0},{8,12},{12,8},{16,20},{20,16},{24,28},{28,24},{1,5},{5... | collective-permute-start | bytes 98312 | tf_op jit(solution)/shard_map/ppermute | solution.py:25
  44.4 2.7 %collective-permute-done.13.got_ref = f32[32,256]{1,0:T(8,128)S(1)} collective-permute-done((f32[32,256]{1,0:T(8,128)S(1)}, f32[32,256]{1,0:T(8,128)S(1)}, u32[]{:S(2)}, u32[]{:S(2)}) %collective-permute-start.13) | collective-permute-done | bytes 32800 | tf_op jit(solution)/shard_map/ppermute | solution.py:25
  47.2 0.1 collective-permute-start.14
  47.3 1.1 %collective-permute-done.14.b_ref = f32[1,256]{1,0:T(1,128)S(1)} collective-permute-done((f32[1,256]{1,0:T(1,128)S(1)}, f32[1,256]{1,0:T(1,128)S(1)}, u32[]{:S(2)}, u32[]{:S(2)}) %collective-permute-start.14) | collective-permute-done | bytes 1056 | tf_op jit(solution)/shard_map/ppermute | solution.py:25
  48.4 1.0 %collective-permute-start.15 = (f32[1,256]{1,0:T(1,128)S(1)}, f32[1,256]{1,0:T(1,128)S(1)}, u32[]{:S(2)}, u32[]{:S(2)}) collective-permute-start(f32[1,256]{1,0:T(1,128)S(1)} %shard_map.140.a_ref), channel_id=1, source_target_pairs={{0,2},{1,3},{2,0},{3,1},{4,6},{5,7},{6,4},{7,5},{8,10},{9,11},{10,... | collective-permute-start | bytes 3080 | tf_op jit(solution)/shard_map/ppermute | solution.py:25
  49.4 2.6 %collective-permute-done.15.b_ref = f32[1,256]{1,0:T(1,128)S(1)} collective-permute-done((f32[1,256]{1,0:T(1,128)S(1)}, f32[1,256]{1,0:T(1,128)S(1)}, u32[]{:S(2)}, u32[]{:S(2)}) %collective-permute-start.15) | collective-permute-done | bytes 1056 | tf_op jit(solution)/shard_map/ppermute | solution.py:25
  52.0 0.5 collective-permute-start.16
  52.5 3.8 %collective-permute-start.17 = (f32[8,256]{1,0:T(8,128)S(1)}, f32[8,256]{1,0:T(8,128)S(1)}, u32[]{:S(2)}, u32[]{:S(2)}) collective-permute-start(f32[8,256]{1,0:T(8,128)S(1)} %get-tuple-element.100), channel_id=1, source_target_pairs={{0,16},{4,20},{8,24},{12,28},{16,0},{20,4},{24,8},{28,12},{1,17},{... | collective-permute-start | bytes 24584 | tf_op jit(solution)/shard_map/ppermute | solution.py:25
  56.3 0.0 collective-permute-done.16.refs_1_
  56.3 3.1 %collective-permute-start.18 = (f32[8,256]{1,0:T(8,128)S(1)}, f32[8,256]{1,0:T(8,128)S(1)}, u32[]{:S(2)}, u32[]{:S(2)}) collective-permute-start(f32[8,256]{1,0:T(8,128)S(1)} %get-tuple-element.101), channel_id=1, source_target_pairs={{0,24},{4,28},{8,16},{12,20},{16,8},{20,12},{24,0},{28,4},{1,25},{... | collective-permute-start | bytes 24584 | tf_op jit(solution)/shard_map/ppermute | solution.py:25
  59.4 0.0 copy-done.1
  59.4 1.5 %shard_map.134 = (bf16[256,512]{1,0:T(8,128)(2,1)}, bf16[256,512]{1,0:T(8,128)(2,1)}) custom-call(bf16[256,512]{1,0:T(8,128)(2,1)S(1)} %bitcast.15, f32[1,128]{1,0:T(1,128)S(1)} %bitcast.23, f32[144,1024]{1,0:T(8,128)S(1)} %get-tuple-element.82.acc, bf16[128,1024]{1,0:T(8,128)(2,1)S(1)} %get-tuple-element.83.mixed_ref), custom_call_target="tpu_custom_call" | custom-call | flops 134217728 | bytes 1048576 | tf_op jit(solution)/shard_map/pallas_call | solution.py:38
  60.9 0.0 collective-permute-done.17.refs_2_
  60.9 0.8 %collective-permute-done.18.refs_3_ = f32[8,256]{1,0:T(8,128)S(1)} collective-permute-done((f32[8,256]{1,0:T(8,128)S(1)}, f32[8,256]{1,0:T(8,128)S(1)}, u32[]{:S(2)}, u32[]{:S(2)}) %collective-permute-start.18) | collective-permute-done | bytes 8224 | tf_op jit(solution)/shard_map/ppermute | solution.py:25
  61.8 0.0 copy-done.2
  61.8 0.6 shard_map.142
  62.4 0.0 collective-permute-done.12.refs_4_
  62.4 0.0 collective-permute-done.11.refs_3_
  62.4 0.0 collective-permute-done.10.refs_2_
  62.4 0.0 copy-done
  62.4 0.9 %shard_map.138 = (bf16[256,128]{1,0:T(8,128)(2,1)}, bf16[256,128]{1,0:T(8,128)(2,1)}) custom-call(bf16[256,128]{1,0:T(8,128)(2,1)S(1)} %bitcast.13, f32[1,128]{1,0:T(1,128)S(1)} %bitcast.20, bf16[256,256]{1,0:T(8,128)(2,1)S(1)} %get-tuple-element.86.refs_0_, bf16[512,256]{1,0:T(8,128)(2,1)S(1)} %collective-permute-done.8.b_ref.refs_1_, ...), custom_call_target="tpu_custom_call" | custom-call | flops 134217728 | bytes 1048576 | tf_op jit(solution)/shard_map/pallas_call | solution.py:38
  (6 shorter events, 0.1 us)
Async XLA Ops:
  1.7 7.2 %collective-permute-start.1 = (bf16[272,256]{1,0:T(8,128)(2,1)S(1)}, bf16[272,256]{1,0:T(8,128)(2,1)S(1)}, u32[]{:S(2)}, u32[]{:S(2)}) collective-permute-start(bf16[272,256]{1,0:T(8,128)(2,1)S(1)} %get-tuple-element.56.refs_4_.refs_15_), channel_id=1, source_target_pairs={{0,8},{4,12},{8,0},{12,4},{16,24},{20,28},{24,16},{28,20},{1,9},{5... | collective-permute-start | bytes 417800 | tf_op jit(solution)/shard_map/ppermute | solution.py:25
  4.9 10.1 %collective-permute-start.2 = (bf16[272,256]{1,0:T(8,128)(2,1)S(1)}, bf16[272,256]{1,0:T(8,128)(2,1)S(1)}, u32[]{:S(2)}, u32[]{:S(2)}) collective-permute-start(bf16[272,256]{1,0:T(8,128)(2,1)S(1)} %get-tuple-element.56.refs_4_.refs_15_), channel_id=1, source_target_pairs={{0,24},{4,28},{8,16},{12,20},{16,8},{20,12},{24,0},{28,4},{1,25},{... | collective-permute-start | bytes 417800 | tf_op jit(solution)/shard_map/ppermute | solution.py:25
  7.3 15.8 %collective-permute-start.5 = (bf16[272,256]{1,0:T(8,128)(2,1)S(1)}, bf16[272,256]{1,0:T(8,128)(2,1)S(1)}, u32[]{:S(2)}, u32[]{:S(2)}) collective-permute-start(bf16[272,256]{1,0:T(8,128)(2,1)S(1)} %get-tuple-element.56.refs_4_.refs_15_), channel_id=1, source_target_pairs={{0,16},{4,20},{8,24},{12,28},{16,0},{20,4},{24,8},{28,12},{1,17},{... | collective-permute-start | bytes 417800 | tf_op jit(solution)/shard_map/ppermute | solution.py:25
  7.5 17.3 %collective-permute-start = (bf16[272,256]{1,0:T(8,128)(2,1)S(1)}, bf16[272,256]{1,0:T(8,128)(2,1)S(1)}, u32[]{:S(2)}, u32[]{:S(2)}) collective-permute-start(bf16[272,256]{1,0:T(8,128)(2,1)S(1)} %get-tuple-element.56.refs_4_.refs_15_), channel_id=1, source_target_pairs={{0,4},{4,0},{8,12},{12,8},{16,20},{20,16},{24,28},{28,24},{1,5},{5... | collective-permute-start | bytes 417800 | tf_op jit(solution)/shard_map/ppermute | solution.py:25
  9.0 15.8 %collective-permute-start.4 = (bf16[272,256]{1,0:T(8,128)(2,1)S(1)}, bf16[272,256]{1,0:T(8,128)(2,1)S(1)}, u32[]{:S(2)}, u32[]{:S(2)}) collective-permute-start(bf16[272,256]{1,0:T(8,128)(2,1)S(1)} %collective-permute-done.1.refs_1_.refs_16_), channel_id=1, source_target_pairs={{0,4},{4,0},{8,12},{12,8},{16,20},{20,16},{24,28},{28,24},{1,5},{5... | collective-permute-start | bytes 417800 | tf_op jit(solution)/shard_map/ppermute | solution.py:25
  14.9 9.9 %collective-permute-start.6 = (bf16[272,256]{1,0:T(8,128)(2,1)S(1)}, bf16[272,256]{1,0:T(8,128)(2,1)S(1)}, u32[]{:S(2)}, u32[]{:S(2)}) collective-permute-start(bf16[272,256]{1,0:T(8,128)(2,1)S(1)} %collective-permute-done.2.refs_2_.refs_4_.refs_18_), channel_id=1, source_target_pairs={{0,4},{4,0},{8,12},{12,8},{16,20},{20,16},{24,28},{28,24},{1,5},{5... | collective-permute-start | bytes 417800 | tf_op jit(solution)/shard_map/ppermute | solution.py:25
  16.5 8.3 %collective-permute-start.3 = (bf16[16,256]{1,0:T(8,128)(2,1)S(1)}, bf16[16,256]{1,0:T(8,128)(2,1)S(1)}, u32[]{:S(2)}, u32[]{:S(2)}) collective-permute-start(bf16[16,256]{1,0:T(8,128)(2,1)S(1)} %get-tuple-element.63), channel_id=1, source_target_pairs={{0,20},{4,16},{8,28},{12,24},{16,4},{20,0},{24,12},{28,8},{1,21},{... | collective-permute-start | bytes 24584 | tf_op jit(solution)/shard_map/ppermute | solution.py:25
  23.1 5.3 %collective-permute-start.7 = (bf16[272,256]{1,0:T(8,128)(2,1)S(1)}, bf16[272,256]{1,0:T(8,128)(2,1)S(1)}, u32[]{:S(2)}, u32[]{:S(2)}) collective-permute-start(bf16[272,256]{1,0:T(8,128)(2,1)S(1)} %collective-permute-done.5.refs_3_.refs_17_), channel_id=1, source_target_pairs={{0,4},{4,0},{8,12},{12,8},{16,20},{20,16},{24,28},{28,24},{1,5},{5... | collective-permute-start | bytes 417800 | tf_op jit(solution)/shard_map/ppermute | solution.py:25
  28.7 2.5 %copy-start.3 = (f32[128]{0:T(128)S(1)}, f32[128]{0:T(128)}, u32[]{:S(2)}) copy-start(f32[128]{0:T(128)} %param.14) | copy-start | bytes 1540
  28.7 2.5 %copy-start.4 = (f32[128]{0:T(128)S(1)}, f32[128]{0:T(128)}, u32[]{:S(2)}) copy-start(f32[128]{0:T(128)} %param.13) | copy-start | bytes 1540
  28.8 7.9 %collective-permute-start.8 = (bf16[512,256]{1,0:T(8,128)(2,1)S(1)}, bf16[512,256]{1,0:T(8,128)(2,1)S(1)}, u32[]{:S(2)}, u32[]{:S(2)}) collective-permute-start(bf16[512,256]{1,0:T(8,128)(2,1)S(1)} %get-tuple-element.87), channel_id=1, source_target_pairs={{0,4},{4,0},{8,12},{12,8},{16,20},{20,16},{24,28},{28,24},{1,5},{5... | collective-permute-start | bytes 786440 | tf_op jit(solution)/shard_map/ppermute | solution.py:25
  31.1 8.4 %collective-permute-start.9 = (bf16[512,256]{1,0:T(8,128)(2,1)S(1)}, bf16[512,256]{1,0:T(8,128)(2,1)S(1)}, u32[]{:S(2)}, u32[]{:S(2)}) collective-permute-start(bf16[512,256]{1,0:T(8,128)(2,1)S(1)} %get-tuple-element.89), channel_id=1, source_target_pairs={{0,4},{4,0},{8,12},{12,8},{16,20},{20,16},{24,28},{28,24},{1,5},{5... | collective-permute-start | bytes 786440 | tf_op jit(solution)/shard_map/ppermute | solution.py:25
  31.1 28.3 %copy-start.1 = (bf16[1,256,512]{2,1,0:T(8,128)(2,1)S(1)}, bf16[1,256,512]{2,1,0:T(8,128)(2,1)}, u32[]{:S(2)}) copy-start(bf16[1,256,512]{2,1,0:T(8,128)(2,1)} %param.8) | copy-start | bytes 786436
  32.4 29.3 %copy-start.2 = (bf16[1,4,256]{2,1,0:T(4,128)(2,1)S(1)}, bf16[1,4,256]{2,1,0:T(4,128)(2,1)}, u32[]{:S(2)}) copy-start(bf16[1,4,256]{2,1,0:T(4,128)(2,1)} %param.11) | copy-start | bytes 6148
  32.4 30.0 %copy-start = (bf16[1,256,128]{2,1,0:T(8,128)(2,1)S(1)}, bf16[1,256,128]{2,1,0:T(8,128)(2,1)}, u32[]{:S(2)}) copy-start(bf16[1,256,128]{2,1,0:T(8,128)(2,1)} %param.9) | copy-start | bytes 196612
  36.7 25.6 %collective-permute-start.12 = (bf16[256,256]{1,0:T(8,128)(2,1)S(1)}, bf16[256,256]{1,0:T(8,128)(2,1)S(1)}, u32[]{:S(2)}, u32[]{:S(2)}) collective-permute-start(bf16[256,256]{1,0:T(8,128)(2,1)S(1)} %shard_map.137), channel_id=1, source_target_pairs={{0,8},{4,12},{8,0},{12,4},{16,24},{20,28},{24,16},{28,20},{1,9},{5... | collective-permute-start | bytes 393224 | tf_op jit(solution)/shard_map/ppermute | solution.py:25
  39.5 22.8 %collective-permute-start.11 = (bf16[256,256]{1,0:T(8,128)(2,1)S(1)}, bf16[256,256]{1,0:T(8,128)(2,1)S(1)}, u32[]{:S(2)}, u32[]{:S(2)}) collective-permute-start(bf16[256,256]{1,0:T(8,128)(2,1)S(1)} %shard_map.136), channel_id=1, source_target_pairs={{0,16},{4,20},{8,24},{12,28},{16,0},{20,4},{24,8},{28,12},{1,17},{... | collective-permute-start | bytes 393224 | tf_op jit(solution)/shard_map/ppermute | solution.py:25
  43.1 19.3 %collective-permute-start.10 = (bf16[256,256]{1,0:T(8,128)(2,1)S(1)}, bf16[256,256]{1,0:T(8,128)(2,1)S(1)}, u32[]{:S(2)}, u32[]{:S(2)}) collective-permute-start(bf16[256,256]{1,0:T(8,128)(2,1)S(1)} %shard_map.135), channel_id=1, source_target_pairs={{0,24},{4,28},{8,16},{12,20},{16,8},{20,12},{24,0},{28,4},{1,25},{... | collective-permute-start | bytes 393224 | tf_op jit(solution)/shard_map/ppermute | solution.py:25
  43.2 4.0 %collective-permute-start.13 = (f32[32,256]{1,0:T(8,128)S(1)}, f32[32,256]{1,0:T(8,128)S(1)}, u32[]{:S(2)}, u32[]{:S(2)}) collective-permute-start(f32[32,256]{1,0:T(8,128)S(1)} %get-tuple-element.95), channel_id=1, source_target_pairs={{0,4},{4,0},{8,12},{12,8},{16,20},{20,16},{24,28},{28,24},{1,5},{5... | collective-permute-start | bytes 98312 | tf_op jit(solution)/shard_map/ppermute | solution.py:25
  47.2 1.2 %collective-permute-start.14 = (f32[1,256]{1,0:T(1,128)S(1)}, f32[1,256]{1,0:T(1,128)S(1)}, u32[]{:S(2)}, u32[]{:S(2)}) collective-permute-start(f32[1,256]{1,0:T(1,128)S(1)} %get-tuple-element.97.a_ref), channel_id=1, source_target_pairs={{0,1},{1,0},{2,3},{3,2},{4,5},{5,4},{6,7},{7,6},{8,9},{9,8},{10,11... | collective-permute-start | bytes 3080 | tf_op jit(solution)/shard_map/ppermute | solution.py:25
  48.4 3.6 %collective-permute-start.15 = (f32[1,256]{1,0:T(1,128)S(1)}, f32[1,256]{1,0:T(1,128)S(1)}, u32[]{:S(2)}, u32[]{:S(2)}) collective-permute-start(f32[1,256]{1,0:T(1,128)S(1)} %shard_map.140.a_ref), channel_id=1, source_target_pairs={{0,2},{1,3},{2,0},{3,1},{4,6},{5,7},{6,4},{7,5},{8,10},{9,11},{10,... | collective-permute-start | bytes 3080 | tf_op jit(solution)/shard_map/ppermute | solution.py:25
  52.0 4.3 %collective-permute-start.16 = (f32[8,256]{1,0:T(8,128)S(1)}, f32[8,256]{1,0:T(8,128)S(1)}, u32[]{:S(2)}, u32[]{:S(2)}) collective-permute-start(f32[8,256]{1,0:T(8,128)S(1)} %get-tuple-element.99), channel_id=1, source_target_pairs={{0,8},{4,12},{8,0},{12,4},{16,24},{20,28},{24,16},{28,20},{1,9},{5... | collective-permute-start | bytes 24584 | tf_op jit(solution)/shard_map/ppermute | solution.py:25
  52.5 8.4 %collective-permute-start.17 = (f32[8,256]{1,0:T(8,128)S(1)}, f32[8,256]{1,0:T(8,128)S(1)}, u32[]{:S(2)}, u32[]{:S(2)}) collective-permute-start(f32[8,256]{1,0:T(8,128)S(1)} %get-tuple-element.100), channel_id=1, source_target_pairs={{0,16},{4,20},{8,24},{12,28},{16,0},{20,4},{24,8},{28,12},{1,17},{... | collective-permute-start | bytes 24584 | tf_op jit(solution)/shard_map/ppermute | solution.py:25
  56.3 5.4 %collective-permute-start.18 = (f32[8,256]{1,0:T(8,128)S(1)}, f32[8,256]{1,0:T(8,128)S(1)}, u32[]{:S(2)}, u32[]{:S(2)}) collective-permute-start(f32[8,256]{1,0:T(8,128)S(1)} %get-tuple-element.101), channel_id=1, source_target_pairs={{0,24},{4,28},{8,16},{12,20},{16,8},{20,12},{24,0},{28,4},{1,25},{... | collective-permute-start | bytes 24584 | tf_op jit(solution)/shard_map/ppermute | solution.py:25

commit v3 on v2

--- a/solution.py
+++ b/solution.py
@@ -258,6 +258,10 @@
                 kaug, qt, raw, tail, extra_ref[k], kt_ref.at[i], w_ref.at[i], mixed, False
             )
 
+        @pl.when(jnp.logical_not(is_active(me, low, k)))
+        def _():
+            clear(kt_ref.at[i], w_ref.at[i])
+
 
 def second_kernel(n, heads, before, ks, last, low_ref, qt, extra_ref, acc0, o_ref, share_ref, *refs):
     raw_refs = dict(zip([k for k in range(1, n) if k != last], refs[: n - 2]))
@@ -302,21 +306,34 @@
                 kaug, qt, raw, tail, extra_ref[k], kt_ref.at[i], w_ref.at[i], mixed, False
             )
 
-
-def backward_block(rows, raw, weights, factor, inner, kt, qt, gt, ds, plow, acc, kg, piece, gcol):
-    dim = raw.shape[1] // 2
+        @pl.when(jnp.logical_not(is_active(me, low, k)))
+        def _():
+            clear(kt_ref.at[i], w_ref.at[i])
+
+
+def backward_blocks(rows, items, inner, qt, gt, ds, plow, acc, kg):
+    dim = gt.shape[0]
+    for i, (raw, weights, factor, kt, piece, gcol) in enumerate(items):
+        for part in chunks(qt.shape[1]):
+            grad = dot_nn(raw[:rows, dim:], gt[:, part])
+            prob = weights[:, part].astype(F32) * factor[:, part]
+            plow[i, :, part] = prob.astype(BF16)
+            ds[i, :, part] = (prob * (grad - inner[:, part])).astype(BF16)
     for part in chunks(qt.shape[1]):
-        grad = dot_nn(raw[:rows, dim:], gt[:, part])
-        prob = weights[:, part].astype(F32) * factor[:, part]
-        plow[:, part] = prob.astype(BF16)
-        ds[:, part] = (prob * (grad - inner[:, part])).astype(BF16)
-    for part in chunks(qt.shape[1]):
-        acc[:, part] += dot_nn(kt[...], ds[:, part])
-    key_part = dot_nt(qt[: dim + ONES, :], ds[...])
-    piece[:dim, :] = key_part[:dim].astype(BF16)
-    gcol[...] = -key_part[dim : dim + 8]
-    kg[...] += key_part[:dim] * kt[:dim, :].astype(F32)
-    piece[dim:, :] = dot_nt(gt[...], plow[...]).astype(BF16)
+        acc[:, part] += sum(dot_nn(item[3][...], ds[i, :, part]) for i, item in enumerate(items))
+    total = kg[...]
+    for i, (raw, weights, factor, kt, piece, gcol) in enumerate(items):
+        key_part = dot_nt(qt[: dim + ONES, :], ds[i])
+        piece[:dim, :] = key_part[:dim].astype(BF16)
+        gcol[...] = -key_part[dim : dim + 8]
+        total = total + key_part[:dim] * kt[:dim, :].astype(F32)
+        piece[dim:, :] = dot_nt(gt[...], plow[i]).astype(BF16)
+    kg[...] = total
+
+
+def clear(*targets):
+    for ref in targets:
+        ref[...] = jnp.zeros(ref.shape, ref.dtype)
 
 
 def idle_block(piece, gcol):
@@ -326,21 +343,22 @@
 
 def backward_set(ks, me, low, rows, raws, sources, between, log_ref, inner, state, pieces, gcols):
     qt, gt, ds, plow, acc, kg = state
-    for i, k in enumerate(ks):
-        weights, kt = sources[k]
-
-        @pl.when(is_active(me, low, k))
+    for at in range(0, len(ks), 2):
+        group = list(range(at, min(at + 2, len(ks))))
+        needed = functools.reduce(jnp.logical_or, [is_active(me, low, ks[i]) for i in group])
+
+        @pl.when(needed)
         def _():
-            factor = jnp.exp(between[k] - log_ref[...])
-            backward_block(
-                rows, raws[k], weights, factor, inner, kt, qt, gt, ds, plow, acc, kg,
-                pieces[i], gcols[i],
-            )
-
-        if k:
-
-            @pl.when(~is_active(me, low, k))
-            def _():
+            items = []
+            for i in group:
+                weights, kt = sources[ks[i]]
+                factor = jnp.exp(between[ks[i]] - log_ref[...])
+                items.append((raws[ks[i]], weights, factor, kt, pieces[i], gcols[i]))
+            backward_blocks(rows, items, inner, qt, gt, ds, plow, acc, kg)
+
+        @pl.when(jnp.logical_not(needed))
+        def _():
+            for i in group:
                 idle_block(pieces[i], gcols[i])
 
 
@@ -376,6 +394,10 @@
         raw = raws[last]
         tail = strictly_after(raw[rows:, :])
         forward_block(kaug, qt, raw, tail, extra_ref[last], kt_last, w_last, mixed, False)
+
+    @pl.when(jnp.logical_not(is_active(me, low, last)))
+    def _():
+        clear(kt_last, w_last)
 
     for part in chunks(qt.shape[1]):
         total = acc[dim : dim + 1, part]
@@ -418,7 +440,7 @@
     acc, keep_ref, give_ref = refs[half : half + 3]
     piece_refs = refs[half + 3 : 2 * half + 3]
     kg, ds, plow, gall = refs[2 * half + 3 :]
-    rows = ds.shape[0]
+    rows = ds.shape[1]
     dim = qgain_ref.shape[1]
     heads = qt.shape[1] // rows
     me, low = first_block(low_ref)
@@ -546,7 +568,7 @@
     state = struct(tall, wide, dtype=F32)
     key_sum = struct(dim, rows, dtype=F32)
     piece = struct(rows, width)
-    wide_scratch = pltpu.VMEM((rows, wide), BF16)
+    wide_scratch = pltpu.VMEM((2, rows, wide), BF16)
 
     inputs = [lengths, key, values[0], logit, kgain]
     own, share, own_tail, low = kernel_call(

time: 63.5 us -> 63.2 us (level)
  waiting for transfers between devices: 22.4 us -> 19.9 us
  starting transfers between devices: 32 us -> 33.3 us
  Pallas kernels: 8.14 us -> 9 us
    ppermute x19, waiting for transfers between devices: 22.4 us -> 19.9 us  [swap(): return lax.ppermute(value, axis, [(i, i ^ bit) for i in range(count)])]
    ppermute x19, starting transfers between devices: 32 us -> 33.3 us  [swap(): return lax.ppermute(value, axis, [(i, i ^ bit) for i in range(count)])]
    pallas_call x16, Pallas kernels: 8.14 us -> 9 us  [kernel_call(): pl.pallas_call(kernel, out_shape=outs, in_specs=in_specs, out_specs=jax.t...]
  transfers between devices with their start and end apart: 19 -> 19, of which waited for: 8 -> 8; matrix products, arithmetic and copies ran while one was open for 0% -> 0% of each run, Pallas kernels for 9% -> 11%
where the time goes in v3:
time: 63.2 us; the launch traced here: 63 us
  starting transfers between devices  33.3 us (53%)
  waiting for transfers between devices  19.9 us (31%)
  Pallas kernels  9 us (14%)
  between operations  0.81 us (1%)
    ppermute x19, starting transfers between devices, swap(): return lax.ppermute(value, axis, [(i, i ^ bit) for i in range(count)])  33.3 us
    ppermute x19, waiting for transfers between devices, swap(): return lax.ppermute(value, axis, [(i, i ^ bit) for i in range(count)])  19.9 us
    pallas_call x16, Pallas kernels, kernel_call(): pl.pallas_call(kernel, out_shape=outs, in_specs=in_specs, out_specs=jax.t...  9 us
  transfers between devices with their start and end apart: 19, of which 8 were waited for; matrix products, arithmetic and copies ran while one was open for 0% of the time, Pallas kernels for 11%

profile of v3, /device:TPU:0, one launch (start us, length us, event | category | flops | bytes accessed | tf_op | source)
XLA Modules:
  0.0 63.0 jit_solution(16368261007096021776)
XLA Ops:
  0.6 1.1 %shard_map.127 = (bf16[272,256]{1,0:T(8,128)(2,1)S(1)}, bf16[16,256]{1,0:T(8,128)(2,1)S(1)}, bf16[16,256]{1,0:T(8,128)(2,1)S(1)}, s32[8,128]{1,0:T(8,128)S(1)}) custom-call(s32[1,4]{1,0:T(1,128)} %refs_0_.3, bf16[256,128]{1,0:T(8,128)(2,1)} %bitcast.12, bf16[256,128]{1,0:T(8,128)(2,1)} %bitcast.24, bf16[4,256]{1,0:T(4,128)(2,1)} %bitcast.16, f32[1,128]{1,0:T(1,128)} %bitcast.18), custom_call_target="tpu_custom_call" | custom-call | flops 1048576 | bytes 1048576 | tf_op jit(solution)/shard_map/pallas_call | solution.py:38
  1.7 3.1 %collective-permute-start.1 = (bf16[272,256]{1,0:T(8,128)(2,1)S(1)}, bf16[272,256]{1,0:T(8,128)(2,1)S(1)}, u32[]{:S(2)}, u32[]{:S(2)}) collective-permute-start(bf16[272,256]{1,0:T(8,128)(2,1)S(1)} %get-tuple-element.56.refs_4_.refs_15_), channel_id=1, source_target_pairs={{0,8},{4,12},{8,0},{12,4},{16,24},{20,28},{24,16},{28,20},{1,9},{5... | collective-permute-start | bytes 417800 | tf_op jit(solution)/shard_map/ppermute | solution.py:25
  4.9 2.5 %collective-permute-start.2 = (bf16[272,256]{1,0:T(8,128)(2,1)S(1)}, bf16[272,256]{1,0:T(8,128)(2,1)S(1)}, u32[]{:S(2)}, u32[]{:S(2)}) collective-permute-start(bf16[272,256]{1,0:T(8,128)(2,1)S(1)} %get-tuple-element.56.refs_4_.refs_15_), channel_id=1, source_target_pairs={{0,24},{4,28},{8,16},{12,20},{16,8},{20,12},{24,0},{28,4},{1,25},{... | collective-permute-start | bytes 417800 | tf_op jit(solution)/shard_map/ppermute | solution.py:25
  7.3 0.1 collective-permute-start.5
  7.5 1.5 %collective-permute-start = (bf16[272,256]{1,0:T(8,128)(2,1)S(1)}, bf16[272,256]{1,0:T(8,128)(2,1)S(1)}, u32[]{:S(2)}, u32[]{:S(2)}) collective-permute-start(bf16[272,256]{1,0:T(8,128)(2,1)S(1)} %get-tuple-element.56.refs_4_.refs_15_), channel_id=1, source_target_pairs={{0,4},{4,0},{8,12},{12,8},{16,20},{20,16},{24,28},{28,24},{1,5},{5... | collective-permute-start | bytes 417800 | tf_op jit(solution)/shard_map/ppermute | solution.py:25
  9.0 0.0 collective-permute-done.1.refs_1_.refs_16_
  9.0 1.2 %collective-permute-start.4 = (bf16[272,256]{1,0:T(8,128)(2,1)S(1)}, bf16[272,256]{1,0:T(8,128)(2,1)S(1)}, u32[]{:S(2)}, u32[]{:S(2)}) collective-permute-start(bf16[272,256]{1,0:T(8,128)(2,1)S(1)} %collective-permute-done.1.refs_1_.refs_16_), channel_id=1, source_target_pairs={{0,4},{4,0},{8,12},{12,8},{16,20},{20,16},{24,28},{28,24},{1,5},{5... | collective-permute-start | bytes 417800 | tf_op jit(solution)/shard_map/ppermute | solution.py:25
  10.2 4.7 %collective-permute-done.2.refs_2_.refs_4_.refs_18_ = bf16[272,256]{1,0:T(8,128)(2,1)S(1)} collective-permute-done((bf16[272,256]{1,0:T(8,128)(2,1)S(1)}, bf16[272,256]{1,0:T(8,128)(2,1)S(1)}, u32[]{:S(2)}, u32[]{:S(2)}) %collective-permute-start.2) | collective-permute-done | bytes 139296 | tf_op jit(solution)/shard_map/ppermute | solution.py:25
  14.9 1.5 %collective-permute-start.6 = (bf16[272,256]{1,0:T(8,128)(2,1)S(1)}, bf16[272,256]{1,0:T(8,128)(2,1)S(1)}, u32[]{:S(2)}, u32[]{:S(2)}) collective-permute-start(bf16[272,256]{1,0:T(8,128)(2,1)S(1)} %collective-permute-done.2.refs_2_.refs_4_.refs_18_), channel_id=1, source_target_pairs={{0,4},{4,0},{8,12},{12,8},{16,20},{20,16},{24,28},{28,24},{1,5},{5... | collective-permute-start | bytes 417800 | tf_op jit(solution)/shard_map/ppermute | solution.py:25
  16.5 4.7 %collective-permute-start.3 = (bf16[16,256]{1,0:T(8,128)(2,1)S(1)}, bf16[16,256]{1,0:T(8,128)(2,1)S(1)}, u32[]{:S(2)}, u32[]{:S(2)}) collective-permute-start(bf16[16,256]{1,0:T(8,128)(2,1)S(1)} %get-tuple-element.63), channel_id=1, source_target_pairs={{0,20},{4,16},{8,28},{12,24},{16,4},{20,0},{24,12},{28,8},{1,21},{... | collective-permute-start | bytes 24584 | tf_op jit(solution)/shard_map/ppermute | solution.py:25
  21.1 2.0 %shard_map.128 = (bf16[256,1024]{1,0:T(8,128)(2,1)S(1)}, bf16[128,1024]{1,0:T(8,128)(2,1)S(1)}, f32[144,1024]{1,0:T(8,128)S(1)}, bf16[256,1024]{1,0:T(8,128)(2,1...) custom-call(s32[1,4]{1,0:T(1,128)} %refs_0_.3, bf16[256,512]{1,0:T(8,128)(2,1)} %bitcast.14, ...), custom_call_target="tpu_custom_call" | custom-call | flops 268435456 | bytes 1048576 | tf_op jit(solution)/shard_map/pallas_call | solution.py:38
  23.1 0.0 collective-permute-done.5.refs_3_.refs_17_
  23.1 1.6 %collective-permute-start.7 = (bf16[272,256]{1,0:T(8,128)(2,1)S(1)}, bf16[272,256]{1,0:T(8,128)(2,1)S(1)}, u32[]{:S(2)}, u32[]{:S(2)}) collective-permute-start(bf16[272,256]{1,0:T(8,128)(2,1)S(1)} %collective-permute-done.5.refs_3_.refs_17_), channel_id=1, source_target_pairs={{0,4},{4,0},{8,12},{12,8},{16,20},{20,16},{24,28},{28,24},{1,5},{5... | collective-permute-start | bytes 417800 | tf_op jit(solution)/shard_map/ppermute | solution.py:25
  24.7 0.0 collective-permute-done.refs_0_.refs_15_
  24.7 0.2 shard_map.129
  24.9 0.0 collective-permute-done.3.share_ref
  24.9 0.0 collective-permute-done.4.refs_2_.refs_14_
  24.9 0.0 collective-permute-done.6.refs_5_.refs_11_
  24.9 0.3 shard_map.130
  25.2 3.0 %collective-permute-done.7.refs_10_.refs_12_ = bf16[272,256]{1,0:T(8,128)(2,1)S(1)} collective-permute-done((bf16[272,256]{1,0:T(8,128)(2,1)S(1)}, bf16[272,256]{1,0:T(8,128)(2,1)S(1)}, u32[]{:S(2)}, u32[]{:S(2)}) %collective-permute-start.7) | collective-permute-done | bytes 139296 | tf_op jit(solution)/shard_map/ppermute | solution.py:25
  28.3 0.3 shard_map.131
  28.5 0.0 copy-start.3
  28.5 0.0 copy-start.4
  28.6 0.1 shard_map.132
  28.6 3.0 %collective-permute-start.8 = (bf16[512,256]{1,0:T(8,128)(2,1)S(1)}, bf16[512,256]{1,0:T(8,128)(2,1)S(1)}, u32[]{:S(2)}, u32[]{:S(2)}) collective-permute-start(bf16[512,256]{1,0:T(8,128)(2,1)S(1)} %get-tuple-element.87), channel_id=1, source_target_pairs={{0,4},{4,0},{8,12},{12,8},{16,20},{20,16},{24,28},{28,24},{1,5},{5... | collective-permute-start | bytes 786440 | tf_op jit(solution)/shard_map/ppermute | solution.py:25
  31.6 0.1 collective-permute-start.9
  31.7 0.0 copy-done.3
  31.7 0.0 copy-done.4
  31.7 0.0 copy-start.1
  31.7 1.9 %shard_map.133 = (f32[144,1024]{1,0:T(8,128)S(1)}, f32[32,256]{1,0:T(8,128)S(1)}, f32[32,256]{1,0:T(8,128)S(1)}, bf16[256,256]{1,0:T(8,128)(2,1)S(1)}, bf16[256,...) custom-call(s32[8,128]{1,0:T(8,128)S(1)} %get-tuple-element.55.low_ref.refs_0_, ...), custom_call_target="tpu_custom_call" | custom-call | flops 2147483648 | bytes 1048576 | tf_op jit(solution)/shard_map/pallas_call | solution.py:38
  33.6 0.0 copy-start.2
  33.6 0.0 copy-start
  33.6 3.5 %collective-permute-done.8.b_ref.refs_1_ = bf16[512,256]{1,0:T(8,128)(2,1)S(1)} collective-permute-done((bf16[512,256]{1,0:T(8,128)(2,1)S(1)}, bf16[512,256]{1,0:T(8,128)(2,1)S(1)}, u32[]{:S(2)}, u32[]{:S(2)}) %collective-permute-start.8) | collective-permute-done | bytes 262176 | tf_op jit(solution)/shard_map/ppermute | solution.py:25
  37.1 0.1 collective-permute-start.12
  37.2 2.7 %collective-permute-done.9.b_ref = bf16[512,256]{1,0:T(8,128)(2,1)S(1)} collective-permute-done((bf16[512,256]{1,0:T(8,128)(2,1)S(1)}, bf16[512,256]{1,0:T(8,128)(2,1)S(1)}, u32[]{:S(2)}, u32[]{:S(2)}) %collective-permute-start.9) | collective-permute-done | bytes 262176 | tf_op jit(solution)/shard_map/ppermute | solution.py:25
  39.9 2.8 %collective-permute-start.11 = (bf16[256,256]{1,0:T(8,128)(2,1)S(1)}, bf16[256,256]{1,0:T(8,128)(2,1)S(1)}, u32[]{:S(2)}, u32[]{:S(2)}) collective-permute-start(bf16[256,256]{1,0:T(8,128)(2,1)S(1)} %shard_map.136), channel_id=1, source_target_pairs={{0,16},{4,20},{8,24},{12,28},{16,0},{20,4},{24,8},{28,12},{1,17},{... | collective-permute-start | bytes 393224 | tf_op jit(solution)/shard_map/ppermute | solution.py:25
  42.8 0.1 collective-permute-start.10
  42.9 1.8 %collective-permute-start.13 = (f32[32,256]{1,0:T(8,128)S(1)}, f32[32,256]{1,0:T(8,128)S(1)}, u32[]{:S(2)}, u32[]{:S(2)}) collective-permute-start(f32[32,256]{1,0:T(8,128)S(1)} %get-tuple-element.95), channel_id=1, source_target_pairs={{0,4},{4,0},{8,12},{12,8},{16,20},{20,16},{24,28},{28,24},{1,5},{5... | collective-permute-start | bytes 98312 | tf_op jit(solution)/shard_map/ppermute | solution.py:25
  44.6 2.2 %collective-permute-done.13.got_ref = f32[32,256]{1,0:T(8,128)S(1)} collective-permute-done((f32[32,256]{1,0:T(8,128)S(1)}, f32[32,256]{1,0:T(8,128)S(1)}, u32[]{:S(2)}, u32[]{:S(2)}) %collective-permute-start.13) | collective-permute-done | bytes 32800 | tf_op jit(solution)/shard_map/ppermute | solution.py:25
  46.9 0.1 collective-permute-start.14
  46.9 1.1 %collective-permute-done.14.b_ref = f32[1,256]{1,0:T(1,128)S(1)} collective-permute-done((f32[1,256]{1,0:T(1,128)S(1)}, f32[1,256]{1,0:T(1,128)S(1)}, u32[]{:S(2)}, u32[]{:S(2)}) %collective-permute-start.14) | collective-permute-done | bytes 1056 | tf_op jit(solution)/shard_map/ppermute | solution.py:25
  48.1 1.8 %collective-permute-start.15 = (f32[1,256]{1,0:T(1,128)S(1)}, f32[1,256]{1,0:T(1,128)S(1)}, u32[]{:S(2)}, u32[]{:S(2)}) collective-permute-start(f32[1,256]{1,0:T(1,128)S(1)} %shard_map.140.a_ref), channel_id=1, source_target_pairs={{0,2},{1,3},{2,0},{3,1},{4,6},{5,7},{6,4},{7,5},{8,10},{9,11},{10,... | collective-permute-start | bytes 3080 | tf_op jit(solution)/shard_map/ppermute | solution.py:25
  49.9 1.8 %collective-permute-done.15.b_ref = f32[1,256]{1,0:T(1,128)S(1)} collective-permute-done((f32[1,256]{1,0:T(1,128)S(1)}, f32[1,256]{1,0:T(1,128)S(1)}, u32[]{:S(2)}, u32[]{:S(2)}) %collective-permute-start.15) | collective-permute-done | bytes 1056 | tf_op jit(solution)/shard_map/ppermute | solution.py:25
  51.7 0.7 %collective-permute-start.16 = (f32[8,256]{1,0:T(8,128)S(1)}, f32[8,256]{1,0:T(8,128)S(1)}, u32[]{:S(2)}, u32[]{:S(2)}) collective-permute-start(f32[8,256]{1,0:T(8,128)S(1)} %get-tuple-element.99), channel_id=1, source_target_pairs={{0,8},{4,12},{8,0},{12,4},{16,24},{20,28},{24,16},{28,20},{1,9},{5... | collective-permute-start | bytes 24584 | tf_op jit(solution)/shard_map/ppermute | solution.py:25
  52.3 3.6 %collective-permute-start.17 = (f32[8,256]{1,0:T(8,128)S(1)}, f32[8,256]{1,0:T(8,128)S(1)}, u32[]{:S(2)}, u32[]{:S(2)}) collective-permute-start(f32[8,256]{1,0:T(8,128)S(1)} %get-tuple-element.100), channel_id=1, source_target_pairs={{0,16},{4,20},{8,24},{12,28},{16,0},{20,4},{24,8},{28,12},{1,17},{... | collective-permute-start | bytes 24584 | tf_op jit(solution)/shard_map/ppermute | solution.py:25
  56.0 0.0 collective-permute-done.16.refs_1_
  56.0 3.1 %collective-permute-start.18 = (f32[8,256]{1,0:T(8,128)S(1)}, f32[8,256]{1,0:T(8,128)S(1)}, u32[]{:S(2)}, u32[]{:S(2)}) collective-permute-start(f32[8,256]{1,0:T(8,128)S(1)} %get-tuple-element.101), channel_id=1, source_target_pairs={{0,24},{4,28},{8,16},{12,20},{16,8},{20,12},{24,0},{28,4},{1,25},{... | collective-permute-start | bytes 24584 | tf_op jit(solution)/shard_map/ppermute | solution.py:25
  59.1 0.0 copy-done.1
  59.1 1.5 %shard_map.134 = (bf16[256,512]{1,0:T(8,128)(2,1)}, bf16[256,512]{1,0:T(8,128)(2,1)}) custom-call(bf16[256,512]{1,0:T(8,128)(2,1)S(1)} %bitcast.15, f32[1,128]{1,0:T(1,128)S(1)} %bitcast.23, f32[144,1024]{1,0:T(8,128)S(1)} %get-tuple-element.82.acc, bf16[128,1024]{1,0:T(8,128)(2,1)S(1)} %get-tuple-element.83.mixed_ref), custom_call_target="tpu_custom_call" | custom-call | flops 134217728 | bytes 1048576 | tf_op jit(solution)/shard_map/pallas_call | solution.py:38
  60.6 0.0 collective-permute-done.17.refs_2_
  60.6 0.8 %collective-permute-done.18.refs_3_ = f32[8,256]{1,0:T(8,128)S(1)} collective-permute-done((f32[8,256]{1,0:T(8,128)S(1)}, f32[8,256]{1,0:T(8,128)S(1)}, u32[]{:S(2)}, u32[]{:S(2)}) %collective-permute-start.18) | collective-permute-done | bytes 8224 | tf_op jit(solution)/shard_map/ppermute | solution.py:25
  61.4 0.0 copy-done.2
  61.4 0.6 shard_map.142
  62.0 0.0 collective-permute-done.12.refs_4_
  62.1 0.0 collective-permute-done.11.refs_3_
  62.1 0.0 collective-permute-done.10.refs_2_
  62.1 0.0 copy-done
  62.1 0.9 %shard_map.138 = (bf16[256,128]{1,0:T(8,128)(2,1)}, bf16[256,128]{1,0:T(8,128)(2,1)}) custom-call(bf16[256,128]{1,0:T(8,128)(2,1)S(1)} %bitcast.13, f32[1,128]{1,0:T(1,128)S(1)} %bitcast.20, bf16[256,256]{1,0:T(8,128)(2,1)S(1)} %get-tuple-element.86.refs_0_, bf16[512,256]{1,0:T(8,128)(2,1)S(1)} %collective-permute-done.8.b_ref.refs_1_, ...), custom_call_target="tpu_custom_call" | custom-call | flops 134217728 | bytes 1048576 | tf_op jit(solution)/shard_map/pallas_call | solution.py:38
  (6 shorter events, 0.1 us)
Async XLA Ops:
  1.7 7.2 %collective-permute-start.1 = (bf16[272,256]{1,0:T(8,128)(2,1)S(1)}, bf16[272,256]{1,0:T(8,128)(2,1)S(1)}, u32[]{:S(2)}, u32[]{:S(2)}) collective-permute-start(bf16[272,256]{1,0:T(8,128)(2,1)S(1)} %get-tuple-element.56.refs_4_.refs_15_), channel_id=1, source_target_pairs={{0,8},{4,12},{8,0},{12,4},{16,24},{20,28},{24,16},{28,20},{1,9},{5... | collective-permute-start | bytes 417800 | tf_op jit(solution)/shard_map/ppermute | solution.py:25
  4.9 10.1 %collective-permute-start.2 = (bf16[272,256]{1,0:T(8,128)(2,1)S(1)}, bf16[272,256]{1,0:T(8,128)(2,1)S(1)}, u32[]{:S(2)}, u32[]{:S(2)}) collective-permute-start(bf16[272,256]{1,0:T(8,128)(2,1)S(1)} %get-tuple-element.56.refs_4_.refs_15_), channel_id=1, source_target_pairs={{0,24},{4,28},{8,16},{12,20},{16,8},{20,12},{24,0},{28,4},{1,25},{... | collective-permute-start | bytes 417800 | tf_op jit(solution)/shard_map/ppermute | solution.py:25
  7.3 15.8 %collective-permute-start.5 = (bf16[272,256]{1,0:T(8,128)(2,1)S(1)}, bf16[272,256]{1,0:T(8,128)(2,1)S(1)}, u32[]{:S(2)}, u32[]{:S(2)}) collective-permute-start(bf16[272,256]{1,0:T(8,128)(2,1)S(1)} %get-tuple-element.56.refs_4_.refs_15_), channel_id=1, source_target_pairs={{0,16},{4,20},{8,24},{12,28},{16,0},{20,4},{24,8},{28,12},{1,17},{... | collective-permute-start | bytes 417800 | tf_op jit(solution)/shard_map/ppermute | solution.py:25
  7.5 17.3 %collective-permute-start = (bf16[272,256]{1,0:T(8,128)(2,1)S(1)}, bf16[272,256]{1,0:T(8,128)(2,1)S(1)}, u32[]{:S(2)}, u32[]{:S(2)}) collective-permute-start(bf16[272,256]{1,0:T(8,128)(2,1)S(1)} %get-tuple-element.56.refs_4_.refs_15_), channel_id=1, source_target_pairs={{0,4},{4,0},{8,12},{12,8},{16,20},{20,16},{24,28},{28,24},{1,5},{5... | collective-permute-start | bytes 417800 | tf_op jit(solution)/shard_map/ppermute | solution.py:25
  9.0 15.9 %collective-permute-start.4 = (bf16[272,256]{1,0:T(8,128)(2,1)S(1)}, bf16[272,256]{1,0:T(8,128)(2,1)S(1)}, u32[]{:S(2)}, u32[]{:S(2)}) collective-permute-start(bf16[272,256]{1,0:T(8,128)(2,1)S(1)} %collective-permute-done.1.refs_1_.refs_16_), channel_id=1, source_target_pairs={{0,4},{4,0},{8,12},{12,8},{16,20},{20,16},{24,28},{28,24},{1,5},{5... | collective-permute-start | bytes 417800 | tf_op jit(solution)/shard_map/ppermute | solution.py:25
  14.9 10.0 %collective-permute-start.6 = (bf16[272,256]{1,0:T(8,128)(2,1)S(1)}, bf16[272,256]{1,0:T(8,128)(2,1)S(1)}, u32[]{:S(2)}, u32[]{:S(2)}) collective-permute-start(bf16[272,256]{1,0:T(8,128)(2,1)S(1)} %collective-permute-done.2.refs_2_.refs_4_.refs_18_), channel_id=1, source_target_pairs={{0,4},{4,0},{8,12},{12,8},{16,20},{20,16},{24,28},{28,24},{1,5},{5... | collective-permute-start | bytes 417800 | tf_op jit(solution)/shard_map/ppermute | solution.py:25
  16.5 8.5 %collective-permute-start.3 = (bf16[16,256]{1,0:T(8,128)(2,1)S(1)}, bf16[16,256]{1,0:T(8,128)(2,1)S(1)}, u32[]{:S(2)}, u32[]{:S(2)}) collective-permute-start(bf16[16,256]{1,0:T(8,128)(2,1)S(1)} %get-tuple-element.63), channel_id=1, source_target_pairs={{0,20},{4,16},{8,28},{12,24},{16,4},{20,0},{24,12},{28,8},{1,21},{... | collective-permute-start | bytes 24584 | tf_op jit(solution)/shard_map/ppermute | solution.py:25
  23.1 5.1 %collective-permute-start.7 = (bf16[272,256]{1,0:T(8,128)(2,1)S(1)}, bf16[272,256]{1,0:T(8,128)(2,1)S(1)}, u32[]{:S(2)}, u32[]{:S(2)}) collective-permute-start(bf16[272,256]{1,0:T(8,128)(2,1)S(1)} %collective-permute-done.5.refs_3_.refs_17_), channel_id=1, source_target_pairs={{0,4},{4,0},{8,12},{12,8},{16,20},{20,16},{24,28},{28,24},{1,5},{5... | collective-permute-start | bytes 417800 | tf_op jit(solution)/shard_map/ppermute | solution.py:25
  28.5 3.2 %copy-start.3 = (f32[128]{0:T(128)S(1)}, f32[128]{0:T(128)}, u32[]{:S(2)}) copy-start(f32[128]{0:T(128)} %param.14) | copy-start | bytes 1540
  28.5 3.2 %copy-start.4 = (f32[128]{0:T(128)S(1)}, f32[128]{0:T(128)}, u32[]{:S(2)}) copy-start(f32[128]{0:T(128)} %param.13) | copy-start | bytes 1540
  28.6 8.4 %collective-permute-start.8 = (bf16[512,256]{1,0:T(8,128)(2,1)S(1)}, bf16[512,256]{1,0:T(8,128)(2,1)S(1)}, u32[]{:S(2)}, u32[]{:S(2)}) collective-permute-start(bf16[512,256]{1,0:T(8,128)(2,1)S(1)} %get-tuple-element.87), channel_id=1, source_target_pairs={{0,4},{4,0},{8,12},{12,8},{16,20},{20,16},{24,28},{28,24},{1,5},{5... | collective-permute-start | bytes 786440 | tf_op jit(solution)/shard_map/ppermute | solution.py:25
  31.6 8.3 %collective-permute-start.9 = (bf16[512,256]{1,0:T(8,128)(2,1)S(1)}, bf16[512,256]{1,0:T(8,128)(2,1)S(1)}, u32[]{:S(2)}, u32[]{:S(2)}) collective-permute-start(bf16[512,256]{1,0:T(8,128)(2,1)S(1)} %get-tuple-element.89), channel_id=1, source_target_pairs={{0,4},{4,0},{8,12},{12,8},{16,20},{20,16},{24,28},{28,24},{1,5},{5... | collective-permute-start | bytes 786440 | tf_op jit(solution)/shard_map/ppermute | solution.py:25
  31.7 27.4 %copy-start.1 = (bf16[1,256,512]{2,1,0:T(8,128)(2,1)S(1)}, bf16[1,256,512]{2,1,0:T(8,128)(2,1)}, u32[]{:S(2)}) copy-start(bf16[1,256,512]{2,1,0:T(8,128)(2,1)} %param.8) | copy-start | bytes 786436
  33.6 27.8 %copy-start.2 = (bf16[1,4,256]{2,1,0:T(4,128)(2,1)S(1)}, bf16[1,4,256]{2,1,0:T(4,128)(2,1)}, u32[]{:S(2)}) copy-start(bf16[1,4,256]{2,1,0:T(4,128)(2,1)} %param.11) | copy-start | bytes 6148
  33.6 28.5 %copy-start = (bf16[1,256,128]{2,1,0:T(8,128)(2,1)S(1)}, bf16[1,256,128]{2,1,0:T(8,128)(2,1)}, u32[]{:S(2)}) copy-start(bf16[1,256,128]{2,1,0:T(8,128)(2,1)} %param.9) | copy-start | bytes 196612
  37.1 24.9 %collective-permute-start.12 = (bf16[256,256]{1,0:T(8,128)(2,1)S(1)}, bf16[256,256]{1,0:T(8,128)(2,1)S(1)}, u32[]{:S(2)}, u32[]{:S(2)}) collective-permute-start(bf16[256,256]{1,0:T(8,128)(2,1)S(1)} %shard_map.137), channel_id=1, source_target_pairs={{0,8},{4,12},{8,0},{12,4},{16,24},{20,28},{24,16},{28,20},{1,9},{5... | collective-permute-start | bytes 393224 | tf_op jit(solution)/shard_map/ppermute | solution.py:25
  39.9 22.1 %collective-permute-start.11 = (bf16[256,256]{1,0:T(8,128)(2,1)S(1)}, bf16[256,256]{1,0:T(8,128)(2,1)S(1)}, u32[]{:S(2)}, u32[]{:S(2)}) collective-permute-start(bf16[256,256]{1,0:T(8,128)(2,1)S(1)} %shard_map.136), channel_id=1, source_target_pairs={{0,16},{4,20},{8,24},{12,28},{16,0},{20,4},{24,8},{28,12},{1,17},{... | collective-permute-start | bytes 393224 | tf_op jit(solution)/shard_map/ppermute | solution.py:25
  42.8 19.3 %collective-permute-start.10 = (bf16[256,256]{1,0:T(8,128)(2,1)S(1)}, bf16[256,256]{1,0:T(8,128)(2,1)S(1)}, u32[]{:S(2)}, u32[]{:S(2)}) collective-permute-start(bf16[256,256]{1,0:T(8,128)(2,1)S(1)} %shard_map.135), channel_id=1, source_target_pairs={{0,24},{4,28},{8,16},{12,20},{16,8},{20,12},{24,0},{28,4},{1,25},{... | collective-permute-start | bytes 393224 | tf_op jit(solution)/shard_map/ppermute | solution.py:25
  42.9 4.0 %collective-permute-start.13 = (f32[32,256]{1,0:T(8,128)S(1)}, f32[32,256]{1,0:T(8,128)S(1)}, u32[]{:S(2)}, u32[]{:S(2)}) collective-permute-start(f32[32,256]{1,0:T(8,128)S(1)} %get-tuple-element.95), channel_id=1, source_target_pairs={{0,4},{4,0},{8,12},{12,8},{16,20},{20,16},{24,28},{28,24},{1,5},{5... | collective-permute-start | bytes 98312 | tf_op jit(solution)/shard_map/ppermute | solution.py:25
  46.9 1.2 %collective-permute-start.14 = (f32[1,256]{1,0:T(1,128)S(1)}, f32[1,256]{1,0:T(1,128)S(1)}, u32[]{:S(2)}, u32[]{:S(2)}) collective-permute-start(f32[1,256]{1,0:T(1,128)S(1)} %get-tuple-element.97.a_ref), channel_id=1, source_target_pairs={{0,1},{1,0},{2,3},{3,2},{4,5},{5,4},{6,7},{7,6},{8,9},{9,8},{10,11... | collective-permute-start | bytes 3080 | tf_op jit(solution)/shard_map/ppermute | solution.py:25
  48.1 3.6 %collective-permute-start.15 = (f32[1,256]{1,0:T(1,128)S(1)}, f32[1,256]{1,0:T(1,128)S(1)}, u32[]{:S(2)}, u32[]{:S(2)}) collective-permute-start(f32[1,256]{1,0:T(1,128)S(1)} %shard_map.140.a_ref), channel_id=1, source_target_pairs={{0,2},{1,3},{2,0},{3,1},{4,6},{5,7},{6,4},{7,5},{8,10},{9,11},{10,... | collective-permute-start | bytes 3080 | tf_op jit(solution)/shard_map/ppermute | solution.py:25
  51.7 4.3 %collective-permute-start.16 = (f32[8,256]{1,0:T(8,128)S(1)}, f32[8,256]{1,0:T(8,128)S(1)}, u32[]{:S(2)}, u32[]{:S(2)}) collective-permute-start(f32[8,256]{1,0:T(8,128)S(1)} %get-tuple-element.99), channel_id=1, source_target_pairs={{0,8},{4,12},{8,0},{12,4},{16,24},{20,28},{24,16},{28,20},{1,9},{5... | collective-permute-start | bytes 24584 | tf_op jit(solution)/shard_map/ppermute | solution.py:25
  52.3 8.3 %collective-permute-start.17 = (f32[8,256]{1,0:T(8,128)S(1)}, f32[8,256]{1,0:T(8,128)S(1)}, u32[]{:S(2)}, u32[]{:S(2)}) collective-permute-start(f32[8,256]{1,0:T(8,128)S(1)} %get-tuple-element.100), channel_id=1, source_target_pairs={{0,16},{4,20},{8,24},{12,28},{16,0},{20,4},{24,8},{28,12},{1,17},{... | collective-permute-start | bytes 24584 | tf_op jit(solution)/shard_map/ppermute | solution.py:25
  56.0 5.4 %collective-permute-start.18 = (f32[8,256]{1,0:T(8,128)S(1)}, f32[8,256]{1,0:T(8,128)S(1)}, u32[]{:S(2)}, u32[]{:S(2)}) collective-permute-start(f32[8,256]{1,0:T(8,128)S(1)} %get-tuple-element.101), channel_id=1, source_target_pairs={{0,24},{4,28},{8,16},{12,20},{16,8},{20,12},{24,0},{28,4},{1,25},{... | collective-permute-start | bytes 24584 | tf_op jit(solution)/shard_map/ppermute | solution.py:25
